TPU v7x, 32 devices: a whole 2x2x4 slice. The times are simulated.
32 devices in a mesh: pipe: 2 (over x), expert: 16 (over z, y, core).
Axes of the slice: x: 2, y: 2, z: 4, core: 2. Of those that a mesh axis runs over, the one named last changes fastest.
Arguments:
- fwd_input: bfloat16 [2, 1024, 3584], P('pipe', 'expert'), may hold values from -6 to 6
- fwd_routes: int32 [2, 1024, 2], P('pipe', 'expert'), may hold values from 0 to 3, all different within a row; in each aligned block of 64 rows (0 to 63, 64 to 127, ..., all dimensions but the last counted through in order) at most 40 rows name the same one
- fwd_gates: bfloat16 [2, 1024, 2], P('pipe', 'expert'), may hold values from 0.19921875 to 1
- bwd_input: bfloat16 [2, 1024, 3584], P('pipe', 'expert'), may hold values from -6 to 6
- bwd_routes: int32 [2, 1024, 2], P('pipe', 'expert'), may hold values from 0 to 3, all different within a row; in each aligned block of 64 rows (0 to 63, 64 to 127, ..., all dimensions but the last counted through in order) at most 40 rows name the same one
- bwd_gates: bfloat16 [2, 1024, 2], P('pipe', 'expert'), may hold values from 0.19921875 to 1
- out_grad: bfloat16 [2, 1024, 3584], P('pipe', 'expert'), may hold values from -12 to 12
- norm_gain: float32 [2, 3584], P('pipe'), may hold values from 0.25 to 1.75
- gate_weight: bfloat16 [2, 3584, 4096], P('pipe', None, 'expert'), may hold values from -0.09375 to 0.09375
- up_weight: bfloat16 [2, 3584, 4096], P('pipe', None, 'expert'), may hold values from -0.09375 to 0.09375
- down_weight: bfloat16 [2, 4096, 3584], P('pipe', 'expert'), may hold values from -0.1875 to 0.1875
Outputs:
- act_next: bfloat16 [2, 1024, 3584], P('pipe', 'expert')
- grad_prev: bfloat16 [2, 1024, 3584], P('pipe', 'expert')
- gate_grad: float32 [2, 1024, 2], P('pipe', 'expert')
- gain_grad: float32 [2, 3584], P('pipe')
- grad_gate_weight: bfloat16 [2, 3584, 4096], P('pipe', None, 'expert')
- grad_up_weight: bfloat16 [2, 3584, 4096], P('pipe', None, 'expert')
- grad_down_weight: bfloat16 [2, 4096, 3584], P('pipe', 'expert')
Inputs may be any that keep to these rules, and one draw needn't show every extreme that they name: `fwd_routes`: each row names 2 different experts. In the 64 rows of one device (aligned blocks of the flattened rows) no expert is named by more than 40 rows, a bound that some block reaches. `bwd_routes`: each row names 2 different experts. In the 64 rows of one device (aligned blocks of the flattened rows) no expert is named by more than 40 rows, a bound that some block reaches.
All inputs are finite; a program needn't handle non-finite values.
Results may differ from a plain program's by a relative error of at most 0.008.
Values may be sent and summed in bfloat16 or wider, within the bound.
No kernel may reach another device: no remote copies, remote signals or barrier semaphores. Data moves between devices by JAX's collectives and lax.ppermute only.
A program may use at most 128 MiB of HBM per device.

v0:
```python
import jax
import jax.numpy as jnp
from jax import lax
from jax.sharding import PartitionSpec as P

UNIT_SPLIT_COUNT = 4


epsilon = 1e-06


def partner_2(value, axis, apart):
    mask = 2**apart
    pairs = [(source, source ^ mask) for source in range(lax.axis_size(axis))]
    return lax.ppermute(value, axis, pairs)


def from_behind(value, axis, steps):
    count = lax.axis_size(axis)
    first, last = (max(0, -steps), min(count, count - steps))
    return lax.ppermute(value, axis, [(source, source + steps) for source in range(first, last)])


def normalize(values, gain):
    wide = values.astype(jnp.float32)
    inverse = lax.rsqrt(jnp.mean(wide * wide, axis=-1, keepdims=True) + epsilon)
    normed = wide * inverse
    return ((normed * gain[None, :]).astype(jnp.bfloat16), normed, inverse)


def slot_table(route_ids, experts, capacity):
    local_rows, picks = route_ids.shape
    flat = route_ids.reshape(-1)
    onehot = (flat[:, None] == jnp.arange(experts, dtype=jnp.int32)[None, :]).astype(jnp.int32)
    before = jnp.sum((jnp.cumsum(onehot, axis=0) - onehot) * onehot, axis=1)
    destination = flat * capacity + before
    source = jnp.full((experts * capacity,), local_rows * picks, jnp.int32)
    source = source.at[destination].set(jnp.arange(local_rows * picks, dtype=jnp.int32))
    return (destination, source)


def contract_rows(left, right):
    return lax.dot_general(
        left, right, (((0,), (0,)), ((), ())), preferred_element_type=jnp.float32
    )


def contract_cols(left, right):
    return lax.dot_general(
        left, right, (((1,), (1,)), ((), ())), preferred_element_type=jnp.float32
    )


def on_device(
    fwd_input,
    fwd_routes,
    fwd_gates,
    bwd_input,
    bwd_routes,
    bwd_gates,
    out_grad,
    norm_gain,
    gate_weight,
    up_weight,
    down_weight,
):
    devices = lax.axis_size("expert")
    experts = devices // UNIT_SPLIT_COUNT
    local_rows = fwd_input.shape[1]
    model_width = fwd_input.shape[2]
    picks = fwd_routes.shape[2]
    capacity = min(local_rows, local_rows * picks * 5 // (4 * experts))
    piece_width = model_width // UNIT_SPLIT_COUNT
    position = lax.axis_index("expert")
    gain = norm_gain[0]
    fwd_norm, unused_normed, unused_inverse = normalize(fwd_input[0], gain)
    bwd_norm, bwd_normed, bwd_inverse = normalize(bwd_input[0], gain)
    fwd_target, fwd_source = slot_table(fwd_routes[0], experts, capacity)
    bwd_target, bwd_source = slot_table(bwd_routes[0], experts, capacity)
    zero_row = jnp.zeros((1, model_width), jnp.bfloat16)
    fwd_rows = jnp.concatenate([fwd_norm, zero_row], axis=0)[fwd_source // picks]
    bwd_rows = jnp.concatenate([bwd_norm, zero_row], axis=0)[bwd_source // picks]
    cot_rows = jnp.concatenate([out_grad[0], zero_row], axis=0)[bwd_source // picks]
    slot_gates = jnp.concatenate([bwd_gates[0].reshape(-1), jnp.zeros((1,), jnp.bfloat16)])[
        bwd_source
    ]
    stacked = jnp.stack([fwd_rows, bwd_rows, cot_rows], axis=1).reshape(
        experts, capacity, 3, model_width
    )
    gates_out = jnp.broadcast_to(
        slot_gates.reshape(experts, 1, capacity), (experts, UNIT_SPLIT_COUNT, capacity)
    ).reshape(devices, capacity)
    sliced = stacked.reshape(experts, capacity, 3, UNIT_SPLIT_COUNT, piece_width)
    sliced = jnp.transpose(sliced, (0, 3, 1, 2, 4)).reshape(devices, capacity, 3, piece_width)
    received, received_gates = (
        lax.all_to_all(sliced, "expert", split_axis=0, concat_axis=0, tiled=True),
        lax.all_to_all(gates_out, "expert", split_axis=0, concat_axis=0, tiled=True),
    )
    for bit_level in range(UNIT_SPLIT_COUNT.bit_length() - 1):
        partner = partner_2(received, "expert", bit_level)
        upper_half = position // (1 << bit_level) % 2 == 1
        received = jnp.where(
            upper_half,
            jnp.concatenate([partner, received], axis=-1),
            jnp.concatenate([received, partner], axis=-1),
        )
    slot_rows = devices * capacity
    rows_fwd = received[:, :, 0].reshape(slot_rows, model_width)
    rows_bwd = received[:, :, 1].reshape(slot_rows, model_width)
    rows_cot = received[:, :, 2].reshape(slot_rows, model_width)
    row_gate = received_gates.reshape(slot_rows).astype(jnp.float32)[:, None]
    gate_matrix = gate_weight[0]
    up_matrix = up_weight[0]
    weight_down = down_weight[0]
    pre_gate = jnp.dot(rows_fwd, gate_matrix, preferred_element_type=jnp.float32)
    pre_up = jnp.dot(rows_fwd, up_matrix, preferred_element_type=jnp.float32)
    live_inner_units = (pre_gate * jax.nn.sigmoid(pre_gate) * pre_up).astype(jnp.bfloat16)
    out_fwd = jnp.dot(live_inner_units, weight_down, preferred_element_type=jnp.float32).astype(
        jnp.bfloat16
    )
    pre_gate_b = jnp.dot(rows_bwd, gate_matrix, preferred_element_type=jnp.float32)
    pre_up_b = jnp.dot(rows_bwd, up_matrix, preferred_element_type=jnp.float32)
    sigma = jax.nn.sigmoid(pre_gate_b)
    swish = pre_gate_b * sigma
    active_b = (swish * pre_up_b).astype(jnp.bfloat16)
    upstream = contract_cols(rows_cot, weight_down)
    switch_portion = jnp.sum(active_b.astype(jnp.float32) * upstream, axis=-1).astype(jnp.bfloat16)
    scaled = (row_gate * rows_cot.astype(jnp.float32)).astype(jnp.bfloat16)
    grad_down = contract_rows(active_b, scaled).astype(jnp.bfloat16)
    act_grad = row_gate * upstream
    gate_preact_gradient = (
        act_grad * pre_up_b * sigma * (1.0 + pre_gate_b * (1.0 - sigma))
    ).astype(jnp.bfloat16)
    up_preact_gradient = (act_grad * swish).astype(jnp.bfloat16)
    grad_gate = contract_rows(rows_bwd, gate_preact_gradient).astype(jnp.bfloat16)
    grad_up = contract_rows(rows_bwd, up_preact_gradient).astype(jnp.bfloat16)
    norm_part = (
        contract_cols(gate_preact_gradient, gate_matrix)
        + contract_cols(up_preact_gradient, up_matrix)
    ).astype(jnp.bfloat16)
    outgoing = jnp.stack([out_fwd, norm_part], axis=1).reshape(devices, capacity, 2, model_width)
    returned, returned_gates = (
        lax.all_to_all(outgoing, "expert", split_axis=0, concat_axis=0, tiled=True),
        lax.all_to_all(
            switch_portion.reshape(devices, capacity),
            "expert",
            split_axis=0,
            concat_axis=0,
            tiled=True,
        ),
    )
    summed = jnp.sum(
        returned.reshape(experts, UNIT_SPLIT_COUNT, capacity, 2, model_width).astype(jnp.float32),
        axis=1,
    )
    summed = summed.reshape(experts * capacity, 2, model_width)
    summed_gates = jnp.sum(
        returned_gates.reshape(experts, UNIT_SPLIT_COUNT, capacity).astype(jnp.float32), axis=1
    ).reshape(-1)
    fwd_value = summed[fwd_target, 0].reshape(local_rows, picks, model_width)
    mixed = (
        fwd_input[0].astype(jnp.float32)
        + jnp.sum(fwd_gates[0].astype(jnp.float32)[:, :, None] * fwd_value, axis=1)
    ).astype(jnp.bfloat16)
    norm_grad = jnp.sum(summed[bwd_target, 1].reshape(local_rows, picks, model_width), axis=1)
    gate_grad = summed_gates[bwd_target].reshape(local_rows, picks)
    gain_grad = lax.psum(jnp.sum(norm_grad * bwd_normed, axis=0), "expert")
    scaled_grad = norm_grad * gain[None, :]
    input_grad = (
        out_grad[0].astype(jnp.float32)
        + bwd_inverse
        * (scaled_grad - bwd_normed * jnp.mean(scaled_grad * bwd_normed, axis=-1, keepdims=True))
    ).astype(jnp.bfloat16)
    act_next = from_behind(mixed, "pipe", 1)
    grad_prev = from_behind(input_grad, "pipe", -1)
    return (
        act_next[None],
        grad_prev[None],
        gate_grad[None],
        gain_grad[None],
        grad_gate[None],
        grad_up[None],
        grad_down[None],
    )


def solution(mesh):
    placed = (
        P("pipe", "expert", None),
        P("pipe", "expert", None),
        P("pipe", "expert", None),
        P("pipe", "expert", None),
        P("pipe", "expert", None),
        P("pipe", "expert", None),
        P("pipe", "expert", None),
        P("pipe", None),
        P("pipe", None, "expert"),
        P("pipe", None, "expert"),
        P("pipe", "expert", None),
    )
    return jax.shard_map(
        on_device,
        mesh=mesh,
        in_specs=placed,
        out_specs=(
            P("pipe", "expert", None),
            P("pipe", "expert", None),
            P("pipe", "expert", None),
            P("pipe", None),
            P("pipe", None, "expert"),
            P("pipe", None, "expert"),
            P("pipe", "expert", None),
        ),
        check_vma=False,
    )
```

profile of v0, /device:TPU:0, one launch (start us, length us, event | category | flops | bytes accessed | tf_op | source)
XLA Modules:
  0.0 669.1 jit_solution(14907783184808667723)
XLA Ops:
  9.9 2.2 fusion.32
  17.0 2.3 gather_fusion.2
  19.3 2.2 stack.23
  21.5 2.4 copy.78
  32.1 2.3 gather_fusion
  39.5 84.3 %all_to_all.25 = bf16[16,40,3,896]{3,1,2,0:T(8,128)(2,1)} all-to-all(bf16[16,40,3,896]{3,1,2,0:T(8,128)(2,1)S(1)} %bitcast.99), channel_id=1, replica_groups=mesh['pipe'=2,'expert'=16] {'expert'}, dimensions={0} | all-to-all | bytes 6881280 | tf_op jit(solution)/shard_map/all_to_all | solution.py:96
  124.6 6.0 collective-permute-done
  130.6 9.3 %maximum_select_fusion.1 = bf16[16,40,3,1792]{3,1,2,0:T(8,128)(2,1)} fusion(bf16[16,40,3,896]{3,1,2,0:T(8,128)(2,1)} %all_to_all.25, bf16[16,40,3,896]{3,1,2,0:T(8,128)(2,1)} %collective-permute-done, pred[]{:T(512)S(6)} %eq.40), kind=kLoop, calls=%fused_computation.14 | loop fusion | flops 30965760 | bytes 13762561 | tf_op jit(solution)/shard_map/jit(_where)/select_n | solution.py:102
  143.5 3.9 all-to-all-start.1
  147.4 143.3 %all-to-all-done.1 = bf16[16,1,40]{2,1,0:T(2,128)(2,1)S(1)} async-done(((bf16[16,1,40]{2,1,0:T(2,128)(2,1)}), bf16[16,1,40]{2,1,0:T(2,128)(2,1)S(1)}, u32[]{:S(2)}, u32[]{:S(2)}) %all-to-all-start.1) | async-done | bytes 1312 | tf_op jit(solution)/shard_map/all_to_all | solution.py:97
  290.8 14.0 %maximum_select_fusion = bf16[16,40,3,3584]{3,1,2,0:T(8,128)(2,1)S(1)} fusion(bf16[16,40,3,1792]{3,1,2,0:T(8,128)(2,1)} %maximum_select_fusion.1, bf16[16,40,3,1792]{3,1,2,0:T(8,128)(2,1)} %collective-permute-done.1, pred[]{:T(512)S(6)} %eq.39), kind=kLoop, calls=%fused_computation.10 | loop fusion | flops 61931520 | bytes 27525120 | tf_op jit(solution)/shard_map/jit(_where)/select_n | solution.py:102
  304.9 4.0 fusion.47
  315.3 10.0 %convolution_convert_fusion = bf16[640,3584]{1,0:T(8,128)(2,1)} fusion(bf16[1,256,3584]{2,1,0:T(8,128)(2,1)} %param.21, f32[640,256]{1,0:T(8,128)S(1)} %fusion.10, bf16[640,3584]{1,0:T(8,128)(2,1)} %bitcast.107, bf16[1,3584,256]{2,1,0:T(8,128)(2,1)S(1)} %copy-done), kind=kOutput, calls=%fused_computation.15 | convolution fusion | flops 2352087040 | bytes 13500416 | tf_op jit(solution)/shard_map/dot_general | solution.py:118
  325.2 6.0 multiply_reduce_fusion.1
  332.7 3.5 add_convert_fusion
  336.2 8.1 %pad_maximum_fusion = bf16[16,40,2,3584]{3,1,2,0:T(8,128)(2,1)} fusion(bf16[16,40,1,3584]{3,1,2,0:T(8,128)(2,1)} %bitcast.98, bf16[16,40,1,3584]{3,1,2,0:T(8,128)(2,1)} %bitcast.106), kind=kLoop, calls=%fused_computation.11 | loop fusion | flops 4587520 | bytes 18350080 | tf_op jit(solution)/shard_map/stack | solution.py:141
  344.3 5.1 all-to-all-start.2
  350.1 5.2 fusion.1
  355.3 158.2 %all-to-all-done.2 = bf16[16,40,2,3584]{3,1,2,0:T(8,128)(2,1)} async-done(((bf16[16,40,2,3584]{3,1,2,0:T(8,128)(2,1)}), bf16[16,40,2,3584]{3,1,2,0:T(8,128)(2,1)}, u32[]{:S(2)}, u32[]{:S(2)}) %all-to-all-start.2) | async-done | bytes 9175072 | tf_op jit(solution)/shard_map/all_to_all | solution.py:143
  513.5 5.6 convert_reduce_fusion
  519.1 5.6 copy.89
  524.7 3.4 gather_fusion.5
  528.1 2.3 reshape.169
  530.5 3.9 reduce_sum.111
  537.7 4.5 gather_fusion.4
  542.2 2.5 reshape.168
  544.7 2.5 multiply_reduce_fusion
  547.4 4.6 collective-permute-start.2
  552.0 5.2 fusion
  557.9 39.6 %all-to-all-start.3 = ((bf16[16,1,40]{2,1,0:T(2,128)(2,1)}), bf16[16,1,40]{2,1,0:T(2,128)(2,1)S(1)}, u32[]{:S(2)}, u32[]{:S(2)}) async-start(bf16[16,1,40]{2,1,0:T(2,128)(2,1)} %convert_element_type.158), calls=%async_computation.3 | async-start | bytes 16384 | tf_op jit(solution)/shard_map/all_to_all | solution.py:144
  597.5 5.5 fusion.2
  606.0 61.1 %psum.7 = f32[1,3584]{1,0:T(1,128)} all-reduce(f32[1,3584]{1,0:T(1,128)S(1)} %broadcast_in_dim.57), channel_id=1, replica_groups=mesh['pipe'=2,'expert'=16] {'expert'}, use_global_device_ids=true, to_apply=%region_15.16 | all-reduce | flops 3584 | bytes 28672 | tf_op jit(solution)/shard_map/psum | solution.py:167
  (115 shorter events, 49.0 us)
Async XLA Ops:
  0.6 308.3 %copy-start = (bf16[1,3584,256]{2,1,0:T(8,128)(2,1)S(1)}, bf16[1,3584,256]{2,1,0:T(8,128)(2,1)}, u32[]{:S(2)}) copy-start(bf16[1,3584,256]{2,1,0:T(8,128)(2,1)} %param.19) | copy-start | bytes 5505028
  5.1 3.5 copy-start.13
  9.2 3.0 copy-start.10
  123.8 6.8 %collective-permute-start = (bf16[16,40,3,896]{3,1,2,0:T(8,128)(2,1)}, bf16[16,40,3,896]{3,1,2,0:T(8,128)(2,1)}, u32[]{:S(2)}, u32[]{:S(2)}) collective-permute-start(bf16[16,40,3,896]{3,1,2,0:T(8,128)(2,1)} %all_to_all.25), channel_id=1, source_target_pairs={{0,1},{1,0},{2,3},{3,2},{4,5},{5,4},{6,7},{7,6},{8,9},{9,8},{10,11... | collective-permute-start | bytes 10321928 | tf_op jit(solution)/shard_map/ppermute | solution.py:15
  124.6 16.2 %copy-start.15 = (bf16[1,64,2]{1,2,0:T(2,128)(2,1)S(1)}, bf16[1,64,2]{1,2,0:T(2,128)(2,1)}, u32[]{:S(2)}) copy-start(bf16[1,64,2]{1,2,0:T(2,128)(2,1)} %param.16) | copy-start | bytes 772
  139.9 150.9 %collective-permute-start.1 = (bf16[16,40,3,1792]{3,1,2,0:T(8,128)(2,1)}, bf16[16,40,3,1792]{3,1,2,0:T(8,128)(2,1)}, u32[]{:S(2)}, u32[]{:S(2)}) collective-permute-start(bf16[16,40,3,1792]{3,1,2,0:T(8,128)(2,1)} %maximum_select_fusion.1), channel_id=1, source_target_pairs={{0,2},{1,3},{2,0},{3,1},{4,6},{5,7},{6,4},{7,5},{8,10},{9,11},{10,... | collective-permute-start | bytes 20643848 | tf_op jit(solution)/shard_map/ppermute | solution.py:15
  143.5 147.2 %all-to-all-start.1 = ((bf16[16,1,40]{2,1,0:T(2,128)(2,1)}), bf16[16,1,40]{2,1,0:T(2,128)(2,1)S(1)}, u32[]{:S(2)}, u32[]{:S(2)}) async-start(bf16[16,1,40]{2,1,0:T(2,128)(2,1)} %copy.80), calls=%async_computation.1 | async-start | bytes 16384 | tf_op jit(solution)/shard_map/all_to_all | solution.py:97
  308.9 5.0 copy-start.3
  308.9 2.8 copy-start.6
  308.9 5.0 slice-start
  311.7 2.2 slice-start.1
  331.2 1.5 copy-start.7
  344.2 5.1 copy-start.16
  344.2 5.9 copy-start.14
  344.3 169.3 %all-to-all-start.2 = ((bf16[16,40,2,3584]{3,1,2,0:T(8,128)(2,1)}), bf16[16,40,2,3584]{3,1,2,0:T(8,128)(2,1)}, u32[]{:S(2)}, u32[]{:S(2)}) async-start(bf16[16,40,2,3584]{3,1,2,0:T(8,128)(2,1)} %pad_maximum_fusion), calls=%async_computation.2 | async-start | bytes 18350080 | tf_op jit(solution)/shard_map/all_to_all | solution.py:143
  528.1 6.3 copy-start.2
  528.1 6.3 copy-start.11
  528.1 7.2 %copy-start.5 = (bf16[1,64,3584]{2,1,0:T(8,128)(2,1)S(1)}, bf16[1,64,3584]{2,1,0:T(8,128)(2,1)}, u32[]{:S(2)}) copy-start(bf16[1,64,3584]{2,1,0:T(8,128)(2,1)} %param.17) | copy-start | bytes 1376260
  536.4 130.7 %collective-permute-start.3 = (bf16[64,3584]{1,0:T(8,128)(2,1)}, bf16[64,3584]{1,0:T(8,128)(2,1)S(1)}, u32[]{:S(2)}, u32[]{:S(2)}) collective-permute-start(bf16[64,3584]{1,0:T(8,128)(2,1)} %fusion.27), channel_id=1, source_target_pairs={{16,0},{17,1},{18,2},{19,3},{20,4},{21,5},{22,6},{23,7},{24,8},{25... | collective-permute-start | bytes 1376264 | tf_op jit(solution)/shard_map/ppermute | solution.py:21
  537.7 7.0 %copy-start.8 = (f32[64,2]{1,0:T(8,128)S(1)}, f32[64,2]{1,0:T(8,128)}, u32[]{:S(2)}) copy-start(f32[64,2]{1,0:T(8,128)} %copy.71) | copy-start | bytes 1540
  542.2 5.0 copy-start.4
  547.4 9.8 %copy-start.12 = (bf16[640]{0:T(1024)(128)(2,1)S(1)}, bf16[640]{0:T(1024)(128)(2,1)}, u32[]{:S(2)}) copy-start(bf16[640]{0:T(1024)(128)(2,1)} %get-tuple-element.37) | copy-start | bytes 3844
  547.4 119.7 %collective-permute-start.2 = (bf16[64,3584]{1,0:T(8,128)(2,1)S(1)}, bf16[64,3584]{1,0:T(8,128)(2,1)S(1)}, u32[]{:S(2)}, u32[]{:S(2)}) collective-permute-start(bf16[64,3584]{1,0:T(8,128)(2,1)S(1)} %fusion.33), channel_id=1, source_target_pairs={{0,16},{1,17},{2,18},{3,19},{4,20},{5,21},{6,22},{7,23},{8,24},{9,... | collective-permute-start | bytes 1376264 | tf_op jit(solution)/shard_map/ppermute | solution.py:21
  557.1 48.8 %copy-start.9 = (f32[3584]{0:T(1024)S(1)}, f32[3584]{0:T(1024)}, u32[]{:S(2)}) copy-start(f32[3584]{0:T(1024)} %get-tuple-element.35) | copy-start | bytes 43012
  557.9 46.0 %all-to-all-start.3 = ((bf16[16,1,40]{2,1,0:T(2,128)(2,1)}), bf16[16,1,40]{2,1,0:T(2,128)(2,1)S(1)}, u32[]{:S(2)}, u32[]{:S(2)}) async-start(bf16[16,1,40]{2,1,0:T(2,128)(2,1)} %convert_element_type.158), calls=%async_computation.3 | async-start | bytes 16384 | tf_op jit(solution)/shard_map/all_to_all | solution.py:144
  597.5 71.1 %copy-start.1 = (bf16[1,3584,256]{2,1,0:T(8,128)(2,1)S(1)}, bf16[1,3584,256]{2,1,0:T(8,128)(2,1)}, u32[]{:S(2)}) copy-start(bf16[1,3584,256]{2,1,0:T(8,128)(2,1)} %param.19) | copy-start | bytes 5505028
where the time goes:
time: 676 us; the launch traced here: 669 us
  waiting for transfers between devices  308 us (46%)
  blocking collectives  145 us (21%)
  other arithmetic  60 us (9%)
  starting transfers between devices  56.2 us (8%)
  local copies, waits for them, and re-layouts  55.2 us (8%)
  matrix products  42.3 us (6%)
    all_to_all x1, waiting for transfers between devices, on_device(): lax.all_to_all(outgoing, 'expert', split_axis=0, concat_axis=0, tiled=True)  158 us
    all_to_all x1, waiting for transfers between devices, on_device(): lax.all_to_all(gates_out, 'expert', split_axis=0, concat_axis=0, tiled=True)  143 us
    all_to_all x1, blocking collectives, on_device(): lax.all_to_all(sliced, 'expert', split_axis=0, concat_axis=0, tiled=True)  84.3 us
    psum x1, blocking collectives, on_device(): gain_grad = lax.psum(jnp.sum(norm_grad * bwd_normed, axis=0), 'expert')  61.1 us
    all_to_all x1, starting transfers between devices, on_device(): lax.all_to_all(switch_portion.reshape(devices, capacity), 'expert', split...  39.6 us
    select_n x2, other arithmetic, on_device(): jnp.where(upper_half, jnp.concatenate([partner, received], axis=-1), jnp....  23.3 us
    dot_general x3, matrix products, contract_rows(): lax.dot_general(left, right, (((0,), (0,)), ((), ())), preferred_element_...  15.8 us
  transfers between devices with their start and end apart: 7, of which 4 were waited for; matrix products, arithmetic and copies ran while one was open for 5% of the time, Pallas kernels for 0%

commit v1 on v0

v1 whole, which is shorter than its diff:
```python
import functools

import jax
import jax.numpy as jnp
from jax import lax
from jax.experimental import pallas as pl
from jax.experimental.pallas import tpu as pltpu
from jax.sharding import PartitionSpec as P

UNIT_SPLIT_COUNT = 4
EPSILON = 1e-06
LANES = 128
BF16 = jnp.bfloat16
F32 = jnp.float32


def chunk_of(width):
    for size in (512, 256, 128):
        if width % size == 0:
            return size
    return width


def swap(value, mask):
    count = lax.axis_size("expert")
    return lax.ppermute(value, "expert", [(source, source ^ mask) for source in range(count)])


def along_pipe(value, steps):
    count = lax.axis_size("pipe")
    first, last = (max(0, -steps), min(count, count - steps))
    return lax.ppermute(value, "pipe", [(source, source + steps) for source in range(first, last)])


def dot_rows(left, right):
    return lax.dot_general(left, right, (((0,), (0,)), ((), ())), preferred_element_type=F32)


def dot_cols(left, right):
    return lax.dot_general(left, right, (((1,), (1,)), ((), ())), preferred_element_type=F32)


def dot(left, right):
    return lax.dot_general(left, right, (((1,), (0,)), ((), ())), preferred_element_type=F32)


def members(plane, routes, experts):
    tokens = routes.shape[1]
    height = -(-experts // 8) * 8
    expert = lax.broadcasted_iota(jnp.int32, (height, tokens), 0) ^ plane
    named = [routes[k : k + 1, :] == expert for k in range(routes.shape[0])]
    chosen = functools.reduce(jnp.logical_or, named)
    earlier = lax.broadcasted_iota(jnp.int32, (tokens, tokens), 0) < lax.broadcasted_iota(
        jnp.int32, (tokens, tokens), 1
    )
    rank = dot(chosen.astype(F32).astype(BF16), earlier.astype(F32).astype(BF16)).astype(jnp.int32)
    return chosen, rank, named


def slots_of(chosen, rank, d, slots):
    tokens = rank.shape[1]
    place = lax.broadcasted_iota(jnp.int32, (slots, tokens), 0)
    row = jnp.where(chosen[d : d + 1, :], rank[d : d + 1, :], -1)
    return place == row


def norm_factor(values_ref, chunk):
    tokens, width = values_ref.shape

    def add(i, total):
        part = values_ref[:, pl.ds(pl.multiple_of(i * chunk, chunk), chunk)].astype(F32)
        return total + jnp.sum(part * part, axis=1, keepdims=True)

    total = lax.fori_loop(0, width // chunk, add, jnp.zeros((tokens, 1), F32))
    return lax.rsqrt(total * (1.0 / width) + EPSILON)


def select_norm_kernel(experts, slots, plane_ref, routes_ref, values_ref, gain_ref, *out_refs):
    width = values_ref.shape[1]
    chunk = chunk_of(width)
    chosen, rank, _ = members(plane_ref[0], routes_ref[...], experts)
    picks = jnp.concatenate(
        [slots_of(chosen, rank, d, slots).astype(F32) for d in range(experts)], axis=0
    ).astype(BF16)
    inverse = norm_factor(values_ref, chunk)

    def step(i, carry):
        cols = pl.ds(pl.multiple_of(i * chunk, chunk), chunk)
        normed = values_ref[:, cols].astype(F32) * inverse
        rows = dot(picks, (normed * gain_ref[:, cols]).astype(BF16)).astype(BF16)
        for d in range(experts):
            out_refs[d][0, :, cols] = rows[d * slots : (d + 1) * slots]
        return carry

    lax.fori_loop(0, width // chunk, step, 0)


def select_both_kernel(
    experts, slots, plane_ref, routes_ref, gates_ref, values_ref, gain_ref, cot_ref, *out_refs
):
    width = values_ref.shape[1]
    chunk = chunk_of(width)
    chosen, rank, named = members(plane_ref[0], routes_ref[...], experts)
    gates = gates_ref[...].astype(F32)
    gate_of = sum(jnp.where(hit, gates[k : k + 1, :], 0.0) for k, hit in enumerate(named))
    hits = [slots_of(chosen, rank, d, slots) for d in range(experts)]
    picks = jnp.concatenate([hit.astype(F32) for hit in hits], axis=0).astype(BF16)
    gate_col = jnp.concatenate(
        [
            jnp.sum(jnp.where(hit, gate_of[d : d + 1, :], 0.0), axis=1, keepdims=True)
            for d, hit in enumerate(hits)
        ],
        axis=0,
    )
    inverse = norm_factor(values_ref, chunk)

    def step(i, carry):
        cols = pl.ds(pl.multiple_of(i * chunk, chunk), chunk)
        normed = values_ref[:, cols].astype(F32) * inverse
        rows = dot(picks, (normed * gain_ref[:, cols]).astype(BF16)).astype(BF16)
        scaled = (dot(picks, cot_ref[:, cols]) * gate_col).astype(BF16)
        for d in range(experts):
            out_refs[d][0, :, cols] = rows[d * slots : (d + 1) * slots]
            out_refs[d][1, :, cols] = scaled[d * slots : (d + 1) * slots]
        return carry

    lax.fori_loop(0, width // chunk, step, 0)


def forward_kernel(rows_ref, gate_ref, up_ref, down_ref, out_ref):
    rows = rows_ref[0]
    pre_gate = dot(rows, gate_ref[...])
    pre_up = dot(rows, up_ref[...])
    act = (pre_gate * jax.nn.sigmoid(pre_gate) * pre_up).astype(BF16)
    width = out_ref.shape[1]
    chunk = chunk_of(width)

    def step(i, carry):
        cols = pl.ds(pl.multiple_of(i * chunk, chunk), chunk)
        out_ref[:, cols] = dot(act, down_ref[:, cols]).astype(BF16)
        return carry

    lax.fori_loop(0, width // chunk, step, 0)


def backward_kernel(
    rows_ref, gate_ref, up_ref, down_ref, out_ref, act_ref, gate_grad_ref, up_grad_ref, gain_ref
):
    width = gain_ref.shape[1]
    chunk = chunk_of(width)
    pre_gate = dot(rows_ref[0], gate_ref[...])
    pre_up = dot(rows_ref[0], up_ref[...])
    upstream = dot_cols(rows_ref[1], down_ref[...])
    sigma = jax.nn.sigmoid(pre_gate)
    swish = pre_gate * sigma
    act = (swish * pre_up).astype(BF16)
    act_ref[...] = act
    gate_grad = (upstream * pre_up * sigma * (1.0 + pre_gate * (1.0 - sigma))).astype(BF16)
    up_grad = (upstream * swish).astype(BF16)
    gate_grad_ref[...] = gate_grad
    up_grad_ref[...] = up_grad
    term = jnp.sum(act.astype(F32) * upstream, axis=1, keepdims=True)
    high = term.astype(BF16).astype(F32)
    lane = lax.broadcasted_iota(jnp.int32, (term.shape[0], LANES), 1)
    out_ref[:, width:] = jnp.where(lane < LANES // 2, high, term - high).astype(BF16)

    def step(i, carry):
        cols = pl.ds(pl.multiple_of(i * chunk, chunk), chunk)
        grads = dot_cols(gate_grad, gate_ref[cols, :]) + dot_cols(up_grad, up_ref[cols, :])
        out_ref[:, cols] = grads.astype(BF16)
        gain_ref[:, cols] = jnp.sum(
            grads * rows_ref[0, :, cols].astype(F32), axis=0, keepdims=True
        )
        return carry

    lax.fori_loop(0, width // chunk, step, 0)


def weight_kernel(
    own_ref, other_ref, act_own, act_other, gate_own, gate_other, up_own, up_other,
    grad_gate_ref, grad_up_ref, grad_down_ref,
):
    own, other = own_ref[0], other_ref[0]
    grad_gate_ref[...] = (dot_rows(own, gate_own[...]) + dot_rows(other, gate_other[...])).astype(
        BF16
    )
    grad_up_ref[...] = (dot_rows(own, up_own[...]) + dot_rows(other, up_other[...])).astype(BF16)
    grad_down_ref[...] = (
        dot_rows(act_own[...], own_ref[1]) + dot_rows(act_other[...], other_ref[1])
    ).astype(BF16)


def mixed_kernel(experts, slots, plane_ref, routes_ref, gates_ref, values_ref, *refs):
    block_refs, out_ref = refs[:experts], refs[experts]
    width = values_ref.shape[1]
    chunk = chunk_of(width)
    chosen, rank, named = members(plane_ref[0], routes_ref[...], experts)
    gates = gates_ref[...].astype(F32)
    gate_of = sum(jnp.where(hit, gates[k : k + 1, :], 0.0) for k, hit in enumerate(named))
    weights = [
        jnp.where(slots_of(chosen, rank, d, slots), gate_of[d : d + 1, :], 0.0).astype(BF16)
        for d in range(experts)
    ]

    def step(i, carry):
        cols = pl.ds(pl.multiple_of(i * chunk, chunk), chunk)
        total = sum(dot_rows(weights[d], block_refs[d][:, cols]) for d in range(experts))
        out_ref[:, cols] = (values_ref[:, cols].astype(F32) + total).astype(BF16)
        return carry

    lax.fori_loop(0, width // chunk, step, 0)


def input_grad_kernel(
    experts, slots, plane_ref, routes_ref, gates_ref, values_ref, cot_ref, gain_ref, *refs
):
    block_refs = refs[:experts]
    out_ref, gate_out_ref, scaled_ref = refs[experts:]
    tokens, width = values_ref.shape
    chunk = chunk_of(width)
    chosen, rank, named = members(plane_ref[0], routes_ref[...], experts)
    hits = [slots_of(chosen, rank, d, slots) for d in range(experts)]
    picks = [hit.astype(F32).astype(BF16) for hit in hits]
    inverse = norm_factor(values_ref, chunk)

    terms = []
    for named_k in named:
        total = jnp.zeros((LANES, tokens), F32)
        for d in range(experts):
            mine = jnp.where(named_k[d : d + 1, :], hits[d].astype(F32), 0.0).astype(BF16)
            total = total + dot_rows(block_refs[d][:, width:], mine)
        terms.append(total[0:1] + total[LANES // 2 : LANES // 2 + 1])
    gate_out_ref[...] = jnp.concatenate(terms, axis=0) / gates_ref[...].astype(F32)

    def first(i, carry):
        cols = pl.ds(pl.multiple_of(i * chunk, chunk), chunk)
        grads = sum(dot_rows(picks[d], block_refs[d][:, cols]) for d in range(experts))
        grads = grads * gain_ref[:, cols]
        scaled_ref[:, cols] = grads
        normed = values_ref[:, cols].astype(F32) * inverse
        return carry + jnp.sum(grads * normed, axis=1, keepdims=True)

    mean = lax.fori_loop(0, width // chunk, first, jnp.zeros((tokens, 1), F32)) * (1.0 / width)

    def second(i, carry):
        cols = pl.ds(pl.multiple_of(i * chunk, chunk), chunk)
        normed = values_ref[:, cols].astype(F32) * inverse
        out_ref[:, cols] = (
            cot_ref[:, cols].astype(F32) + inverse * (scaled_ref[:, cols] - normed * mean)
        ).astype(BF16)
        return carry

    lax.fori_loop(0, width // chunk, second, 0)


SMEM_SPEC = pl.BlockSpec(memory_space=pltpu.SMEM)
VMEM_SPEC = pl.BlockSpec(memory_space=pltpu.VMEM)


def call(body, out_shapes, args, name, scratch=(), scalars=0):
    return pl.pallas_call(
        body,
        out_shape=[jax.ShapeDtypeStruct(shape, dtype) for shape, dtype in out_shapes],
        in_specs=[SMEM_SPEC] * scalars + [VMEM_SPEC] * (len(args) - scalars),
        out_specs=[VMEM_SPEC] * len(out_shapes),
        scratch_shapes=list(scratch),
        compiler_params=pltpu.CompilerParams(vmem_limit_bytes=48 << 20),
        name=name,
    )(*args)


def weight_grads(own, other, acts, gates, ups):
    pair, rows, width = own.shape
    units = acts[0].shape[1]
    chunk = chunk_of(width)
    whole = pl.BlockSpec((rows, units), lambda i: (0, 0))
    return pl.pallas_call(
        weight_kernel,
        grid=(width // chunk,),
        out_shape=[
            jax.ShapeDtypeStruct((width, units), BF16),
            jax.ShapeDtypeStruct((width, units), BF16),
            jax.ShapeDtypeStruct((units, width), BF16),
        ],
        in_specs=[pl.BlockSpec((pair, rows, chunk), lambda i: (0, 0, i))] * 2 + [whole] * 6,
        out_specs=[
            pl.BlockSpec((chunk, units), lambda i: (i, 0)),
            pl.BlockSpec((chunk, units), lambda i: (i, 0)),
            pl.BlockSpec((units, chunk), lambda i: (0, i)),
        ],
        compiler_params=pltpu.CompilerParams(vmem_limit_bytes=48 << 20),
        name="weight_grads",
    )(own, other, *acts, *gates, *ups)


def gather_rows(blocks):
    landed = [swap(block, d * UNIT_SPLIT_COUNT) if d else block for d, block in enumerate(blocks)]
    crossed = [swap(block, 2) for block in landed]
    own = jnp.concatenate(landed + crossed, axis=1)
    return own, swap(own, 1)


def return_rows(own, other, experts, slots):
    partner = swap(other, 1)

    def part(index):
        rows = slice(index * slots, (index + 1) * slots)
        return own[rows].astype(F32) + partner[rows].astype(F32)

    crossed = [swap(part(experts + d).astype(BF16), 2) for d in range(experts)]
    sums = [(part(d) + crossed[d].astype(F32)).astype(BF16) for d in range(experts)]
    return [swap(block, d * UNIT_SPLIT_COUNT) if d else block for d, block in enumerate(sums)]


def on_device(
    fwd_input,
    fwd_routes,
    fwd_gates,
    bwd_input,
    bwd_routes,
    bwd_gates,
    out_grad,
    norm_gain,
    gate_weight,
    up_weight,
    down_weight,
):
    devices = lax.axis_size("expert")
    experts = devices // UNIT_SPLIT_COUNT
    tokens, width = fwd_input.shape[1:]
    picks = fwd_routes.shape[2]
    capacity = min(tokens, tokens * picks * 5 // (4 * experts))
    slots = -(-capacity // 8) * 8
    plane = (lax.axis_index("expert") // UNIT_SPLIT_COUNT).astype(jnp.int32).reshape(1)
    gate_matrix, up_matrix, down_matrix = gate_weight[0], up_weight[0], down_weight[0]
    units = gate_matrix.shape[1]
    fwd_ids, bwd_ids = fwd_routes[0].T, bwd_routes[0].T
    fwd_g, bwd_g = fwd_gates[0].T, bwd_gates[0].T

    bwd_blocks = call(
        functools.partial(select_both_kernel, experts, slots),
        [((2, slots, width), BF16)] * experts,
        (plane, bwd_ids, bwd_g, bwd_input[0], norm_gain, out_grad[0]),
        "select_bwd",
        scalars=1,
    )
    fwd_blocks = call(
        functools.partial(select_norm_kernel, experts, slots),
        [((1, slots, width), BF16)] * experts,
        (plane, fwd_ids, fwd_input[0], norm_gain),
        "select_fwd",
        scalars=1,
    )
    bwd_own, bwd_other = gather_rows(bwd_blocks)
    fwd_own, fwd_other = gather_rows(fwd_blocks)
    rows = bwd_own.shape[1]

    def backward(rows_in, name):
        return call(
            backward_kernel,
            [((rows, width + LANES), BF16)] + [((rows, units), BF16)] * 3 + [((1, width), F32)],
            (rows_in, gate_matrix, up_matrix, down_matrix),
            name,
        )

    def forward(rows_in, name):
        return call(
            forward_kernel,
            [((rows, width), BF16)],
            (rows_in, gate_matrix, up_matrix, down_matrix),
            name,
        )[0]

    norm_own, act_own, dgate_own, dup_own, gain_own = backward(bwd_own, "backward_own")
    norm_other, act_other, dgate_other, dup_other, gain_other = backward(bwd_other, "backward_other")
    norm_back = return_rows(norm_own, norm_other, experts, slots)
    out_own = forward(fwd_own, "forward_own")
    out_other = forward(fwd_other, "forward_other")
    out_back = return_rows(out_own, out_other, experts, slots)
    grad_gate, grad_up, grad_down = weight_grads(
        bwd_own, bwd_other, (act_own, act_other), (dgate_own, dgate_other), (dup_own, dup_other)
    )
    gain_sum = gain_own + gain_other
    bit = 1
    while bit < devices:
        gain_sum = gain_sum + swap(gain_sum, bit)
        bit *= 2
    gain_grad = gain_sum / norm_gain

    input_grad, gate_grad = call(
        functools.partial(input_grad_kernel, experts, slots),
        [((tokens, width), BF16), ((picks, tokens), F32)],
        (plane, bwd_ids, bwd_g, bwd_input[0], out_grad[0], norm_gain, *norm_back),
        "input_grad",
        scratch=[pltpu.VMEM((tokens, width), F32)],
        scalars=1,
    )
    mixed = call(
        functools.partial(mixed_kernel, experts, slots),
        [((tokens, width), BF16)],
        (plane, fwd_ids, fwd_g, fwd_input[0], *out_back),
        "mixed",
        scalars=1,
    )[0]
    act_next = along_pipe(mixed, 1)
    grad_prev = along_pipe(input_grad, -1)
    return (
        act_next[None],
        grad_prev[None],
        gate_grad.T[None],
        gain_grad,
        grad_gate[None],
        grad_up[None],
        grad_down[None],
    )


def solution(mesh):
    rows = P("pipe", "expert", None)
    columns = P("pipe", None, "expert")
    return jax.shard_map(
        on_device,
        mesh=mesh,
        in_specs=(rows,) * 7 + (P("pipe", None), columns, columns, rows),
        out_specs=(rows, rows, rows, P("pipe", None), columns, columns, rows),
        check_vma=False,
    )
```

time: 676 us -> 279 us (0.41)
  waiting for transfers between devices: 308 us -> 149 us
  blocking collectives: 145 us -> 0 us
  other arithmetic: 60 us -> 6.86 us
  Pallas kernels: 0 us -> 49.6 us
  local copies, waits for them, and re-layouts: 55.2 us -> 12.1 us
  matrix products: 42.3 us -> 0 us
    all_to_all x3 -> x0, waiting for transfers between devices: 302 us -> none  [the longest x1 158 us: on_device(): lax.all_to_all(outgoing, 'expert', split_axis=0, concat_axis=0, tiled=True)]
    ppermute x4 -> x38, waiting for transfers between devices: 6.06 us -> 149 us  [the longest x36 137 us: swap(): lax.ppermute(value, 'expert', [(source, source ^ mask) for source in rang...]
    all_to_all x1 -> x0, blocking collectives: 84.3 us -> none  [on_device(): lax.all_to_all(sliced, 'expert', split_axis=0, concat_axis=0, tiled=True)]
    psum x1 -> x0, blocking collectives: 61.1 us -> none  [on_device(): gain_grad = lax.psum(jnp.sum(norm_grad * bwd_normed, axis=0), 'expert')]
    ppermute x4 -> x38, starting transfers between devices: 7.54 us -> 59.5 us  [the longest x36 54.8 us: swap(): lax.ppermute(value, 'expert', [(source, source ^ mask) for source in rang...]
    pallas_call x0 -> x9, Pallas kernels: none -> 49.6 us  [the longest x8 40 us: call(): pl.pallas_call(body, out_shape=[jax.ShapeDtypeStruct(shape, dtype) for sh...]
    all_to_all x3 -> x0, starting transfers between devices: 48.7 us -> none  [the longest x1 39.6 us: on_device(): lax.all_to_all(switch_portion.reshape(devices, capacity), 'expert', split...]
    dot_general x10 -> x0, matrix products: 42.3 us -> none  [the longest x3 15.8 us: contract_rows(): lax.dot_general(left, right, (((0,), (0,)), ((), ())), preferred_element_...]
  transfers between devices with their start and end apart: 7 -> 38, of which waited for: 4 -> 18; matrix products, arithmetic and copies ran while one was open for 5% -> 3% of each run, Pallas kernels for 0% -> 17%
where the time goes in v1:
time: 279 us; the launch traced here: 278 us
  waiting for transfers between devices  149 us (53%)
  starting transfers between devices  59.5 us (21%)
  Pallas kernels  49.6 us (18%)
  local copies, waits for them, and re-layouts  12.1 us (4%)
  other arithmetic  6.86 us (2%)
    ppermute x36, waiting for transfers between devices, swap(): lax.ppermute(value, 'expert', [(source, source ^ mask) for source in rang...  137 us
    ppermute x36, starting transfers between devices, swap(): lax.ppermute(value, 'expert', [(source, source ^ mask) for source in rang...  54.8 us
    pallas_call x8, Pallas kernels, call(): pl.pallas_call(body, out_shape=[jax.ShapeDtypeStruct(shape, dtype) for sh...  40 us
    ppermute x2, waiting for transfers between devices, along_pipe(): lax.ppermute(value, 'pipe', [(source, source + steps) for source in range...  12 us
    unnamed x68, local copies, waits for them, and re-layouts  12 us
    pallas_call x1, Pallas kernels, weight_grads(): pl.pallas_call(weight_kernel, grid=(width // chunk,), out_shape=[jax.Shap...  9.57 us
  transfers between devices with their start and end apart: 38, of which 18 were waited for; matrix products, arithmetic and copies ran while one was open for 3% of the time, Pallas kernels for 17%

profile of v1, /device:TPU:0, one launch (start us, length us, event | category | flops | bytes accessed | tf_op | source)
XLA Modules:
  0.0 278.2 jit_solution(6483098469870446862)
XLA Ops:
  3.1 2.1 select_fwd.1
  5.2 3.1 %collective-permute-start = (bf16[1,40,3584]{2,1,0:T(8,128)(2,1)S(1)}, bf16[1,40,3584]{2,1,0:T(8,128)(2,1)}, u32[]{:S(2)}, u32[]{:S(2)}) collective-permute-start(bf16[1,40,3584]{2,1,0:T(8,128)(2,1)S(1)} %get-tuple-element.31), channel_id=1, source_target_pairs={{0,4},{1,5},{2,6},{3,7},{4,0},{5,1},{6,2},{7,3},{8,12},{9,13},{10,... | collective-permute-start | bytes 860168 | tf_op jit(solution)/shard_map/ppermute | solution.py:26
  8.3 2.6 collective-permute-start.1
  16.7 2.5 select_bwd.1
  21.6 9.7 %collective-permute-done.1 = bf16[1,40,3584]{2,1,0:T(8,128)(2,1)S(1)} collective-permute-done((bf16[1,40,3584]{2,1,0:T(8,128)(2,1)S(1)}, bf16[1,40,3584]{2,1,0:T(8,128)(2,1)S(1)}, u32[]{:S(2)}, u32[]{:S(2)}) %collective-permute-start.1) | collective-permute-done | bytes 286752 | tf_op jit(solution)/shard_map/ppermute | solution.py:26
  31.3 2.5 collective-permute-start.19
  33.8 13.8 %collective-permute-done.17 = bf16[2,40,3584]{2,1,0:T(8,128)(2,1)S(1)} collective-permute-done((bf16[2,40,3584]{2,1,0:T(8,128)(2,1)S(1)}, bf16[2,40,3584]{2,1,0:T(8,128)(2,1)S(1)}, u32[]{:S(2)}, u32[]{:S(2)}) %collective-permute-start.17) | collective-permute-done | bytes 573472 | tf_op jit(solution)/shard_map/ppermute | solution.py:26
  49.1 25.2 %collective-permute-done.18 = bf16[2,40,3584]{2,1,0:T(8,128)(2,1)S(1)} collective-permute-done((bf16[2,40,3584]{2,1,0:T(8,128)(2,1)S(1)}, bf16[2,40,3584]{2,1,0:T(8,128)(2,1)S(1)}, u32[]{:S(2)}, u32[]{:S(2)}) %collective-permute-start.18) | collective-permute-done | bytes 573472 | tf_op jit(solution)/shard_map/ppermute | solution.py:26
  78.1 18.2 %collective-permute-done.21 = bf16[2,40,3584]{2,1,0:T(8,128)(2,1)S(1)} collective-permute-done((bf16[2,40,3584]{2,1,0:T(8,128)(2,1)S(1)}, bf16[2,40,3584]{2,1,0:T(8,128)(2,1)S(1)}, u32[]{:S(2)}, u32[]{:S(2)}) %collective-permute-start.21) | collective-permute-done | bytes 573472 | tf_op jit(solution)/shard_map/ppermute | solution.py:26
  98.0 10.7 %collective-permute-done.22 = bf16[2,40,3584]{2,1,0:T(8,128)(2,1)S(1)} collective-permute-done((bf16[2,40,3584]{2,1,0:T(8,128)(2,1)S(1)}, bf16[2,40,3584]{2,1,0:T(8,128)(2,1)S(1)}, u32[]{:S(2)}, u32[]{:S(2)}) %collective-permute-start.22) | collective-permute-done | bytes 573472 | tf_op jit(solution)/shard_map/ppermute | solution.py:26
  110.2 10.0 %collective-permute-done.23 = bf16[2,40,3584]{2,1,0:T(8,128)(2,1)S(1)} collective-permute-done((bf16[2,40,3584]{2,1,0:T(8,128)(2,1)S(1)}, bf16[2,40,3584]{2,1,0:T(8,128)(2,1)S(1)}, u32[]{:S(2)}, u32[]{:S(2)}) %collective-permute-start.23) | collective-permute-done | bytes 573472 | tf_op jit(solution)/shard_map/ppermute | solution.py:26
  123.4 7.9 %collective-permute-done.7.rows_ref = bf16[1,320,3584]{2,1,0:T(8,128)(2,1)S(1)} collective-permute-done((bf16[1,320,3584]{2,1,0:T(8,128)(2,1)S(1)}, bf16[1,320,3584]{2,1,0:T(8,128)(2,1)S(1)}, u32[]{:S(2)}, u32[]{:S(2)}) %collective-permute-start.7) | collective-permute-done | bytes 2293792 | tf_op jit(solution)/shard_map/ppermute | solution.py:26
  132.8 6.1 %forward_other.1 = bf16[320,3584]{1,0:T(8,128)(2,1)} custom-call(bf16[1,320,3584]{2,1,0:T(8,128)(2,1)} %copy-done.23, bf16[3584,256]{1,0:T(8,128)(2,1)S(1)} %bitcast.27, bf16[3584,256]{1,0:T(8,128)(2,1)S(1)} %bitcast.31, bf16[256,3584]{1,0:T(8,128)(2,1)S(1)} %bitcast.35), custom_call_target="tpu_custom_call" | custom-call | tf_op jit(solution)/shard_map/forward_other/pallas_call | solution.py:261
  139.0 8.5 %backward_other.1 = (bf16[320,3712]{1,0:T(8,128)(2,1)}, bf16[320,256]{1,0:T(8,128)(2,1)S(1)}, bf16[320,256]{1,0:T(8,128)(2,1)S(1)}, bf16[320,256]{1,0:T(8,128)(2,1)S(1)}, f32[1,3584]{1,0:T(1,128)S(1)}) custom-call(bf16[2,320,3584]{2,1,0:T(8,128)(2,1)} %collective-permute-done.24.rows_ref.other_ref, bf16[3584,256]{1,0:T(8,128)(2,1)S(1)} %bitcast.28, ...), custom_call_target="tpu_custom_call" | custom-call | tf_op jit(solution)/shard_map/backward_other/pallas_call | solution.py:261
  147.9 6.1 %forward_own.1 = bf16[320,3584]{1,0:T(8,128)(2,1)} custom-call(bf16[1,320,3584]{2,1,0:T(8,128)(2,1)} %copy-done.21, bf16[3584,256]{1,0:T(8,128)(2,1)S(1)} %bitcast.29, bf16[3584,256]{1,0:T(8,128)(2,1)S(1)} %bitcast.33, bf16[256,3584]{1,0:T(8,128)(2,1)S(1)} %bitcast.37), custom_call_target="tpu_custom_call" | custom-call | tf_op jit(solution)/shard_map/forward_own/pallas_call | solution.py:261
  154.0 8.6 %backward_own.1 = (bf16[320,3712]{1,0:T(8,128)(2,1)}, bf16[320,256]{1,0:T(8,128)(2,1)S(1)}, bf16[320,256]{1,0:T(8,128)(2,1)S(1)}, bf16[320,256]{1,0:T(8,128)(2,1)S(1)}, f32[1,3584]{1,0:T(1,128)S(1)}) custom-call(bf16[2,320,3584]{2,1,0:T(8,128)(2,1)} %copy-done.3, bf16[3584,256]{1,0:T(8,128)(2,1)S(1)} %bitcast.30, bf16[3584,256]{1,0:T(8,128)(2,1)S(1)} %bitcast.34, ...), custom_call_target="tpu_custom_call" | custom-call | tf_op jit(solution)/shard_map/backward_own/pallas_call | solution.py:261
  167.1 6.3 %collective-permute-done.14 = bf16[40,3584]{1,0:T(8,128)(2,1)S(1)} collective-permute-done((bf16[40,3584]{1,0:T(8,128)(2,1)S(1)}, bf16[40,3584]{1,0:T(8,128)(2,1)S(1)}, u32[]{:S(2)}, u32[]{:S(2)}) %collective-permute-start.14) | collective-permute-done | bytes 286752 | tf_op jit(solution)/shard_map/ppermute | solution.py:26
  178.8 2.5 collective-permute-start.15
  182.3 3.6 %collective-permute-done.12 = bf16[40,3584]{1,0:T(8,128)(2,1)S(1)} collective-permute-done((bf16[40,3584]{1,0:T(8,128)(2,1)S(1)}, bf16[40,3584]{1,0:T(8,128)(2,1)S(1)}, u32[]{:S(2)}, u32[]{:S(2)}) %collective-permute-start.12) | collective-permute-done | bytes 286752 | tf_op jit(solution)/shard_map/ppermute | solution.py:26
  187.4 4.6 %collective-permute-done.10 = bf16[40,3584]{1,0:T(8,128)(2,1)S(1)} collective-permute-done((bf16[40,3584]{1,0:T(8,128)(2,1)S(1)}, bf16[40,3584]{1,0:T(8,128)(2,1)S(1)}, u32[]{:S(2)}, u32[]{:S(2)}) %collective-permute-start.10) | collective-permute-done | bytes 286752 | tf_op jit(solution)/shard_map/ppermute | solution.py:26
  193.6 4.6 %collective-permute-done.9 = bf16[40,3584]{1,0:T(8,128)(2,1)S(1)} collective-permute-done((bf16[40,3584]{1,0:T(8,128)(2,1)S(1)}, bf16[40,3584]{1,0:T(8,128)(2,1)S(1)}, u32[]{:S(2)}, u32[]{:S(2)}) %collective-permute-start.9) | collective-permute-done | bytes 286752 | tf_op jit(solution)/shard_map/ppermute | solution.py:26
  201.2 6.1 %collective-permute-start.11 = (bf16[40,3584]{1,0:T(8,128)(2,1)S(1)}, bf16[40,3584]{1,0:T(8,128)(2,1)S(1)}, u32[]{:S(2)}, u32[]{:S(2)}) collective-permute-start(bf16[40,3584]{1,0:T(8,128)(2,1)S(1)} %get-tuple-element.65), channel_id=1, source_target_pairs={{0,4},{1,5},{2,6},{3,7},{4,0},{5,1},{6,2},{7,3},{8,12},{9,13},{10,... | collective-permute-start | bytes 860168 | tf_op jit(solution)/shard_map/ppermute | solution.py:26
  207.3 3.6 %collective-permute-start.36 = (f32[1,3584]{1,0:T(1,128)S(1)}, f32[1,3584]{1,0:T(1,128)S(1)}, u32[]{:S(2)}, u32[]{:S(2)}) collective-permute-start(f32[1,3584]{1,0:T(1,128)S(1)} %add.114), channel_id=1, source_target_pairs={{0,4},{1,5},{2,6},{3,7},{4,0},{5,1},{6,2},{7,3},{8,12},{9,13},{10,... | collective-permute-start | bytes 43016 | tf_op jit(solution)/shard_map/ppermute | solution.py:26
  211.2 2.5 collective-permute-start.32
  213.7 3.1 %collective-permute-done.26 = bf16[40,3712]{1,0:T(8,128)(2,1)S(1)} collective-permute-done((bf16[40,3712]{1,0:T(8,128)(2,1)S(1)}, bf16[40,3712]{1,0:T(8,128)(2,1)S(1)}, u32[]{:S(2)}, u32[]{:S(2)}) %collective-permute-start.26) | collective-permute-done | bytes 296992 | tf_op jit(solution)/shard_map/ppermute | solution.py:26
  217.2 6.0 %collective-permute-start.28 = (bf16[40,3712]{1,0:T(8,128)(2,1)S(1)}, bf16[40,3712]{1,0:T(8,128)(2,1)S(1)}, u32[]{:S(2)}, u32[]{:S(2)}) collective-permute-start(bf16[40,3712]{1,0:T(8,128)(2,1)S(1)} %get-tuple-element.58), channel_id=1, source_target_pairs={{0,4},{1,5},{2,6},{3,7},{4,0},{5,1},{6,2},{7,3},{8,12},{9,13},{10,... | collective-permute-start | bytes 890888 | tf_op jit(solution)/shard_map/ppermute | solution.py:26
  227.4 9.6 %weight_grads.1 = (bf16[3584,256]{1,0:T(8,128)(2,1)}, bf16[3584,256]{1,0:T(8,128)(2,1)}, bf16[256,3584]{1,0:T(8,128)(2,1)}) custom-call(bf16[2,320,3584]{2,1,0:T(8,128)(2,1)S(1)} %bitcast.40, bf16[2,320,3584]{2,1,0:T(8,128)(2,1)} %collective-permute-done.24.rows_ref.other_ref, bf16[320,256]{1,0:T(8,128)(2,1)S(1)} %get-tuple-element.44.act_own, ...), custom_call_target="tpu_custom_call" | custom-call | tf_op jit(solution)/shard_map/weight_grads/pallas_call | solution.py:277
  237.0 16.1 %collective-permute-done.13.refs_2_ = bf16[40,3584]{1,0:T(8,128)(2,1)S(1)} collective-permute-done((bf16[40,3584]{1,0:T(8,128)(2,1)S(1)}, bf16[40,3584]{1,0:T(8,128)(2,1)S(1)}, u32[]{:S(2)}, u32[]{:S(2)}) %collective-permute-start.13) | collective-permute-done | bytes 286752 | tf_op jit(solution)/shard_map/ppermute | solution.py:26
  255.1 3.4 %collective-permute-start.16 = (bf16[64,3584]{1,0:T(8,128)(2,1)S(1)}, bf16[64,3584]{1,0:T(8,128)(2,1)S(1)}, u32[]{:S(2)}, u32[]{:S(2)}) collective-permute-start(bf16[64,3584]{1,0:T(8,128)(2,1)S(1)} %mixed.1), channel_id=1, source_target_pairs={{0,16},{1,17},{2,18},{3,19},{4,20},{5,21},{6,22},{7,23},{8,24},{9,... | collective-permute-start | bytes 1376264 | tf_op jit(solution)/shard_map/ppermute | solution.py:32
  258.5 4.2 %input_grad.1 = (bf16[64,3584]{1,0:T(8,128)(2,1)S(1)}, f32[2,64]{1,0:T(2,128)}) custom-call(s32[1]{0:T(128)} %bitcast.plane_ref, s32[2,64]{1,0:T(2,128)S(1)} %bitcast.50, bf16[2,64]{1,0:T(2,128)(2,1)S(1)} %bitcast.52, bf16[64,3584]{1,0:T(8,128)(2,1)S(1)} %bitcast.44, bf16[64,3584]{1,0:T(8,128)(2,1)S(1)} %bitcast.46, f32[1,3584]{1,0:T(1,128)S(1)} %copy-done.12, ...), custom_call_target="tpu_custom_call" | custom-call | tf_op jit(solution)/shard_map/input_grad/pallas_call | solution.py:261
  264.6 3.7 %collective-permute-done.16 = bf16[64,3584]{1,0:T(8,128)(2,1)S(1)} collective-permute-done((bf16[64,3584]{1,0:T(8,128)(2,1)S(1)}, bf16[64,3584]{1,0:T(8,128)(2,1)S(1)}, u32[]{:S(2)}, u32[]{:S(2)}) %collective-permute-start.16) | collective-permute-done | bytes 458784 | tf_op jit(solution)/shard_map/ppermute | solution.py:32
  268.3 8.4 %collective-permute-done.33 = bf16[64,3584]{1,0:T(8,128)(2,1)S(1)} collective-permute-done((bf16[64,3584]{1,0:T(8,128)(2,1)S(1)}, bf16[64,3584]{1,0:T(8,128)(2,1)S(1)}, u32[]{:S(2)}, u32[]{:S(2)}) %collective-permute-start.33) | collective-permute-done | bytes 458784 | tf_op jit(solution)/shard_map/ppermute | solution.py:32
  (135 shorter events, 51.1 us)
Async XLA Ops:
  5.2 15.4 %collective-permute-start = (bf16[1,40,3584]{2,1,0:T(8,128)(2,1)S(1)}, bf16[1,40,3584]{2,1,0:T(8,128)(2,1)}, u32[]{:S(2)}, u32[]{:S(2)}) collective-permute-start(bf16[1,40,3584]{2,1,0:T(8,128)(2,1)S(1)} %get-tuple-element.31), channel_id=1, source_target_pairs={{0,4},{1,5},{2,6},{3,7},{4,0},{5,1},{6,2},{7,3},{8,12},{9,13},{10,... | collective-permute-start | bytes 860168 | tf_op jit(solution)/shard_map/ppermute | solution.py:26
  8.3 23.0 %collective-permute-start.1 = (bf16[1,40,3584]{2,1,0:T(8,128)(2,1)S(1)}, bf16[1,40,3584]{2,1,0:T(8,128)(2,1)S(1)}, u32[]{:S(2)}, u32[]{:S(2)}) collective-permute-start(bf16[1,40,3584]{2,1,0:T(8,128)(2,1)S(1)} %get-tuple-element.32), channel_id=1, source_target_pairs={{0,8},{1,9},{2,10},{3,11},{4,12},{5,13},{6,14},{7,15},{8,0},{9,1},... | collective-permute-start | bytes 860168 | tf_op jit(solution)/shard_map/ppermute | solution.py:26
  10.8 20.4 %collective-permute-start.2 = (bf16[1,40,3584]{2,1,0:T(8,128)(2,1)S(1)}, bf16[1,40,3584]{2,1,0:T(8,128)(2,1)S(1)}, u32[]{:S(2)}, u32[]{:S(2)}) collective-permute-start(bf16[1,40,3584]{2,1,0:T(8,128)(2,1)S(1)} %get-tuple-element.33), channel_id=1, source_target_pairs={{0,12},{1,13},{2,14},{3,15},{4,8},{5,9},{6,10},{7,11},{8,4},{9,5},... | collective-permute-start | bytes 860168 | tf_op jit(solution)/shard_map/ppermute | solution.py:26
  10.9 109.5 %collective-permute-start.3 = (bf16[1,40,3584]{2,1,0:T(8,128)(2,1)S(1)}, bf16[1,40,3584]{2,1,0:T(8,128)(2,1)}, u32[]{:S(2)}, u32[]{:S(2)}) collective-permute-start(bf16[1,40,3584]{2,1,0:T(8,128)(2,1)S(1)} %get-tuple-element.30), channel_id=1, source_target_pairs={{0,2},{1,3},{2,0},{3,1},{4,6},{5,7},{6,4},{7,5},{8,10},{9,11},{10,... | collective-permute-start | bytes 860168 | tf_op jit(solution)/shard_map/ppermute | solution.py:26
  19.2 57.3 %collective-permute-start.20 = (bf16[2,40,3584]{2,1,0:T(8,128)(2,1)S(1)}, bf16[2,40,3584]{2,1,0:T(8,128)(2,1)S(1)}, u32[]{:S(2)}, u32[]{:S(2)}) collective-permute-start(bf16[2,40,3584]{2,1,0:T(8,128)(2,1)S(1)} %get-tuple-element.34), channel_id=1, source_target_pairs={{0,2},{1,3},{2,0},{3,1},{4,6},{5,7},{6,4},{7,5},{8,10},{9,11},{10,... | collective-permute-start | bytes 1720328 | tf_op jit(solution)/shard_map/ppermute | solution.py:26
  20.6 27.1 %collective-permute-start.17 = (bf16[2,40,3584]{2,1,0:T(8,128)(2,1)S(1)}, bf16[2,40,3584]{2,1,0:T(8,128)(2,1)S(1)}, u32[]{:S(2)}, u32[]{:S(2)}) collective-permute-start(bf16[2,40,3584]{2,1,0:T(8,128)(2,1)S(1)} %get-tuple-element.35), channel_id=1, source_target_pairs={{0,4},{1,5},{2,6},{3,7},{4,0},{5,1},{6,2},{7,3},{8,12},{9,13},{10,... | collective-permute-start | bytes 1720328 | tf_op jit(solution)/shard_map/ppermute | solution.py:26
  31.2 43.1 %collective-permute-start.18 = (bf16[2,40,3584]{2,1,0:T(8,128)(2,1)S(1)}, bf16[2,40,3584]{2,1,0:T(8,128)(2,1)S(1)}, u32[]{:S(2)}, u32[]{:S(2)}) collective-permute-start(bf16[2,40,3584]{2,1,0:T(8,128)(2,1)S(1)} %get-tuple-element.36), channel_id=1, source_target_pairs={{0,8},{1,9},{2,10},{3,11},{4,12},{5,13},{6,14},{7,15},{8,0},{9,1},... | collective-permute-start | bytes 1720328 | tf_op jit(solution)/shard_map/ppermute | solution.py:26
  31.3 44.6 %collective-permute-start.19 = (bf16[2,40,3584]{2,1,0:T(8,128)(2,1)S(1)}, bf16[2,40,3584]{2,1,0:T(8,128)(2,1)S(1)}, u32[]{:S(2)}, u32[]{:S(2)}) collective-permute-start(bf16[2,40,3584]{2,1,0:T(8,128)(2,1)S(1)} %get-tuple-element.37), channel_id=1, source_target_pairs={{0,12},{1,13},{2,14},{3,15},{4,8},{5,9},{6,10},{7,11},{8,4},{9,5},... | collective-permute-start | bytes 1720328 | tf_op jit(solution)/shard_map/ppermute | solution.py:26
  47.7 73.9 %collective-permute-start.4 = (bf16[1,40,3584]{2,1,0:T(8,128)(2,1)}, bf16[1,40,3584]{2,1,0:T(8,128)(2,1)S(1)}, u32[]{:S(2)}, u32[]{:S(2)}) collective-permute-start(bf16[1,40,3584]{2,1,0:T(8,128)(2,1)} %collective-permute-done), channel_id=1, source_target_pairs={{0,2},{1,3},{2,0},{3,1},{4,6},{5,7},{6,4},{7,5},{8,10},{9,11},{10,... | collective-permute-start | bytes 860168 | tf_op jit(solution)/shard_map/ppermute | solution.py:26
  74.3 47.3 %collective-permute-start.5 = (bf16[1,40,3584]{2,1,0:T(8,128)(2,1)S(1)}, bf16[1,40,3584]{2,1,0:T(8,128)(2,1)S(1)}, u32[]{:S(2)}, u32[]{:S(2)}) collective-permute-start(bf16[1,40,3584]{2,1,0:T(8,128)(2,1)S(1)} %collective-permute-done.1), channel_id=1, source_target_pairs={{0,2},{1,3},{2,0},{3,1},{4,6},{5,7},{6,4},{7,5},{8,10},{9,11},{10,... | collective-permute-start | bytes 860168 | tf_op jit(solution)/shard_map/ppermute | solution.py:26
  75.9 20.5 %collective-permute-start.21 = (bf16[2,40,3584]{2,1,0:T(8,128)(2,1)S(1)}, bf16[2,40,3584]{2,1,0:T(8,128)(2,1)S(1)}, u32[]{:S(2)}, u32[]{:S(2)}) collective-permute-start(bf16[2,40,3584]{2,1,0:T(8,128)(2,1)S(1)} %collective-permute-done.17), channel_id=1, source_target_pairs={{0,2},{1,3},{2,0},{3,1},{4,6},{5,7},{6,4},{7,5},{8,10},{9,11},{10,... | collective-permute-start | bytes 1720328 | tf_op jit(solution)/shard_map/ppermute | solution.py:26
  76.5 32.2 %collective-permute-start.22 = (bf16[2,40,3584]{2,1,0:T(8,128)(2,1)S(1)}, bf16[2,40,3584]{2,1,0:T(8,128)(2,1)S(1)}, u32[]{:S(2)}, u32[]{:S(2)}) collective-permute-start(bf16[2,40,3584]{2,1,0:T(8,128)(2,1)S(1)} %collective-permute-done.18), channel_id=1, source_target_pairs={{0,2},{1,3},{2,0},{3,1},{4,6},{5,7},{6,4},{7,5},{8,10},{9,11},{10,... | collective-permute-start | bytes 1720328 | tf_op jit(solution)/shard_map/ppermute | solution.py:26
  96.4 23.9 %collective-permute-start.23 = (bf16[2,40,3584]{2,1,0:T(8,128)(2,1)S(1)}, bf16[2,40,3584]{2,1,0:T(8,128)(2,1)S(1)}, u32[]{:S(2)}, u32[]{:S(2)}) collective-permute-start(bf16[2,40,3584]{2,1,0:T(8,128)(2,1)S(1)} %collective-permute-done.19), channel_id=1, source_target_pairs={{0,2},{1,3},{2,0},{3,1},{4,6},{5,7},{6,4},{7,5},{8,10},{9,11},{10,... | collective-permute-start | bytes 1720328 | tf_op jit(solution)/shard_map/ppermute | solution.py:26
  108.6 14.7 %collective-permute-start.6 = (bf16[1,40,3584]{2,1,0:T(8,128)(2,1)S(1)}, bf16[1,40,3584]{2,1,0:T(8,128)(2,1)S(1)}, u32[]{:S(2)}, u32[]{:S(2)}) collective-permute-start(bf16[1,40,3584]{2,1,0:T(8,128)(2,1)S(1)} %collective-permute-done.2), channel_id=1, source_target_pairs={{0,2},{1,3},{2,0},{3,1},{4,6},{5,7},{6,4},{7,5},{8,10},{9,11},{10,... | collective-permute-start | bytes 860168 | tf_op jit(solution)/shard_map/ppermute | solution.py:26
  120.3 18.7 %collective-permute-start.24 = (bf16[2,320,3584]{2,1,0:T(8,128)(2,1)S(1)}, bf16[2,320,3584]{2,1,0:T(8,128)(2,1)}, u32[]{:S(2)}, u32[]{:S(2)}) collective-permute-start(bf16[2,320,3584]{2,1,0:T(8,128)(2,1)S(1)} %constant_dynamic-update-slice_fusion.8.rows_ref.own_ref), channel_id=1, source_target_pairs={{0,1},{1,0},{2,3},{3,2},{4,5},{5,4},{6,7},{7,6},{8,9},{9,8},{10,11... | collective-permute-start | bytes 13762568 | tf_op jit(solution)/shard_map/ppermute | solution.py:26
  138.9 23.7 %collective-permute-start.8 = (bf16[320,3584]{1,0:T(8,128)(2,1)}, bf16[320,3584]{1,0:T(8,128)(2,1)}, u32[]{:S(2)}, u32[]{:S(2)}) collective-permute-start(bf16[320,3584]{1,0:T(8,128)(2,1)} %forward_other.1), channel_id=1, source_target_pairs={{0,1},{1,0},{2,3},{3,2},{4,5},{5,4},{6,7},{7,6},{8,9},{9,8},{10,11... | collective-permute-start | bytes 6881288 | tf_op jit(solution)/shard_map/ppermute | solution.py:26
  147.5 17.8 %collective-permute-start.25 = (bf16[320,3712]{1,0:T(8,128)(2,1)}, bf16[320,3712]{1,0:T(8,128)(2,1)S(1)}, u32[]{:S(2)}, u32[]{:S(2)}) collective-permute-start(bf16[320,3712]{1,0:T(8,128)(2,1)} %get-tuple-element.39), channel_id=1, source_target_pairs={{0,1},{1,0},{2,3},{3,2},{4,5},{5,4},{6,7},{7,6},{8,9},{9,8},{10,11... | collective-permute-start | bytes 7127048 | tf_op jit(solution)/shard_map/ppermute | solution.py:26
  166.5 14.8 %collective-permute-start.31 = (bf16[40,3712]{1,0:T(8,128)(2,1)S(1)}, bf16[40,3712]{1,0:T(8,128)(2,1)S(1)}, u32[]{:S(2)}, u32[]{:S(2)}) collective-permute-start(bf16[40,3712]{1,0:T(8,128)(2,1)S(1)} %add_convert_fusion.1), channel_id=1, source_target_pairs={{0,2},{1,3},{2,0},{3,1},{4,6},{5,7},{6,4},{7,5},{8,10},{9,11},{10,... | collective-permute-start | bytes 890888 | tf_op jit(solution)/shard_map/ppermute | solution.py:26
  176.8 15.3 %collective-permute-start.10 = (bf16[40,3584]{1,0:T(8,128)(2,1)S(1)}, bf16[40,3584]{1,0:T(8,128)(2,1)S(1)}, u32[]{:S(2)}, u32[]{:S(2)}) collective-permute-start(bf16[40,3584]{1,0:T(8,128)(2,1)S(1)} %get-tuple-element.62), channel_id=1, source_target_pairs={{0,2},{1,3},{2,0},{3,1},{4,6},{5,7},{6,4},{7,5},{8,10},{9,11},{10,... | collective-permute-start | bytes 860168 | tf_op jit(solution)/shard_map/ppermute | solution.py:26
  177.3 20.9 %collective-permute-start.9 = (bf16[40,3584]{1,0:T(8,128)(2,1)S(1)}, bf16[40,3584]{1,0:T(8,128)(2,1)S(1)}, u32[]{:S(2)}, u32[]{:S(2)}) collective-permute-start(bf16[40,3584]{1,0:T(8,128)(2,1)S(1)} %get-tuple-element.63), channel_id=1, source_target_pairs={{0,2},{1,3},{2,0},{3,1},{4,6},{5,7},{6,4},{7,5},{8,10},{9,11},{10,... | collective-permute-start | bytes 860168 | tf_op jit(solution)/shard_map/ppermute | solution.py:26
  178.8 44.4 %collective-permute-start.15 = (bf16[40,3584]{1,0:T(8,128)(2,1)S(1)}, bf16[40,3584]{1,0:T(8,128)(2,1)S(1)}, u32[]{:S(2)}, u32[]{:S(2)}) collective-permute-start(bf16[40,3584]{1,0:T(8,128)(2,1)S(1)} %get-tuple-element.60), channel_id=1, source_target_pairs={{0,12},{1,13},{2,14},{3,15},{4,8},{5,9},{6,10},{7,11},{8,4},{9,5},... | collective-permute-start | bytes 860168 | tf_op jit(solution)/shard_map/ppermute | solution.py:26
  181.3 19.9 %collective-permute-start.35 = (f32[1,3584]{1,0:T(1,128)S(1)}, f32[1,3584]{1,0:T(1,128)S(1)}, u32[]{:S(2)}, u32[]{:S(2)}) collective-permute-start(f32[1,3584]{1,0:T(1,128)S(1)} %add.113), channel_id=1, source_target_pairs={{0,2},{1,3},{2,0},{3,1},{4,6},{5,7},{6,4},{7,5},{8,10},{9,11},{10,... | collective-permute-start | bytes 43016 | tf_op jit(solution)/shard_map/ppermute | solution.py:26
  185.9 21.4 %collective-permute-start.29 = (bf16[40,3712]{1,0:T(8,128)(2,1)S(1)}, bf16[40,3712]{1,0:T(8,128)(2,1)S(1)}, u32[]{:S(2)}, u32[]{:S(2)}) collective-permute-start(bf16[40,3712]{1,0:T(8,128)(2,1)S(1)} %get-tuple-element.54), channel_id=1, source_target_pairs={{0,2},{1,3},{2,0},{3,1},{4,6},{5,7},{6,4},{7,5},{8,10},{9,11},{10,... | collective-permute-start | bytes 890888 | tf_op jit(solution)/shard_map/ppermute | solution.py:26
  192.1 19.2 %collective-permute-start.27 = (bf16[40,3712]{1,0:T(8,128)(2,1)S(1)}, bf16[40,3712]{1,0:T(8,128)(2,1)S(1)}, u32[]{:S(2)}, u32[]{:S(2)}) collective-permute-start(bf16[40,3712]{1,0:T(8,128)(2,1)S(1)} %get-tuple-element.55), channel_id=1, source_target_pairs={{0,2},{1,3},{2,0},{3,1},{4,6},{5,7},{6,4},{7,5},{8,10},{9,11},{10,... | collective-permute-start | bytes 890888 | tf_op jit(solution)/shard_map/ppermute | solution.py:26
  198.2 18.6 %collective-permute-start.26 = (bf16[40,3712]{1,0:T(8,128)(2,1)S(1)}, bf16[40,3712]{1,0:T(8,128)(2,1)S(1)}, u32[]{:S(2)}, u32[]{:S(2)}) collective-permute-start(bf16[40,3712]{1,0:T(8,128)(2,1)S(1)} %get-tuple-element.56), channel_id=1, source_target_pairs={{0,2},{1,3},{2,0},{3,1},{4,6},{5,7},{6,4},{7,5},{8,10},{9,11},{10,... | collective-permute-start | bytes 890888 | tf_op jit(solution)/shard_map/ppermute | solution.py:26
  201.2 25.0 %collective-permute-start.11 = (bf16[40,3584]{1,0:T(8,128)(2,1)S(1)}, bf16[40,3584]{1,0:T(8,128)(2,1)S(1)}, u32[]{:S(2)}, u32[]{:S(2)}) collective-permute-start(bf16[40,3584]{1,0:T(8,128)(2,1)S(1)} %get-tuple-element.65), channel_id=1, source_target_pairs={{0,4},{1,5},{2,6},{3,7},{4,0},{5,1},{6,2},{7,3},{8,12},{9,13},{10,... | collective-permute-start | bytes 860168 | tf_op jit(solution)/shard_map/ppermute | solution.py:26
  207.3 17.0 %collective-permute-start.36 = (f32[1,3584]{1,0:T(1,128)S(1)}, f32[1,3584]{1,0:T(1,128)S(1)}, u32[]{:S(2)}, u32[]{:S(2)}) collective-permute-start(f32[1,3584]{1,0:T(1,128)S(1)} %add.114), channel_id=1, source_target_pairs={{0,4},{1,5},{2,6},{3,7},{4,0},{5,1},{6,2},{7,3},{8,12},{9,13},{10,... | collective-permute-start | bytes 43016 | tf_op jit(solution)/shard_map/ppermute | solution.py:26
  211.2 47.2 %collective-permute-start.32 = (bf16[40,3712]{1,0:T(8,128)(2,1)S(1)}, bf16[40,3712]{1,0:T(8,128)(2,1)S(1)}, u32[]{:S(2)}, u32[]{:S(2)}) collective-permute-start(bf16[40,3712]{1,0:T(8,128)(2,1)S(1)} %get-tuple-element.53), channel_id=1, source_target_pairs={{0,12},{1,13},{2,14},{3,15},{4,8},{5,9},{6,10},{7,11},{8,4},{9,5},... | collective-permute-start | bytes 890888 | tf_op jit(solution)/shard_map/ppermute | solution.py:26
  217.2 41.3 %collective-permute-start.28 = (bf16[40,3712]{1,0:T(8,128)(2,1)S(1)}, bf16[40,3712]{1,0:T(8,128)(2,1)S(1)}, u32[]{:S(2)}, u32[]{:S(2)}) collective-permute-start(bf16[40,3712]{1,0:T(8,128)(2,1)S(1)} %get-tuple-element.58), channel_id=1, source_target_pairs={{0,4},{1,5},{2,6},{3,7},{4,0},{5,1},{6,2},{7,3},{8,12},{9,13},{10,... | collective-permute-start | bytes 890888 | tf_op jit(solution)/shard_map/ppermute | solution.py:26
  223.2 35.2 %collective-permute-start.30 = (bf16[40,3712]{1,0:T(8,128)(2,1)S(1)}, bf16[40,3712]{1,0:T(8,128)(2,1)S(1)}, u32[]{:S(2)}, u32[]{:S(2)}) collective-permute-start(bf16[40,3712]{1,0:T(8,128)(2,1)S(1)} %get-tuple-element.57), channel_id=1, source_target_pairs={{0,8},{1,9},{2,10},{3,11},{4,12},{5,13},{6,14},{7,15},{8,0},{9,1},... | collective-permute-start | bytes 890888 | tf_op jit(solution)/shard_map/ppermute | solution.py:26
  224.3 28.8 %collective-permute-start.13 = (bf16[40,3584]{1,0:T(8,128)(2,1)S(1)}, bf16[40,3584]{1,0:T(8,128)(2,1)S(1)}, u32[]{:S(2)}, u32[]{:S(2)}) collective-permute-start(bf16[40,3584]{1,0:T(8,128)(2,1)S(1)} %get-tuple-element.64), channel_id=1, source_target_pairs={{0,8},{1,9},{2,10},{3,11},{4,12},{5,13},{6,14},{7,15},{8,0},{9,1},... | collective-permute-start | bytes 860168 | tf_op jit(solution)/shard_map/ppermute | solution.py:26
  226.2 37.8 %collective-permute-start.37 = (f32[1,3584]{1,0:T(1,128)S(1)}, f32[1,3584]{1,0:T(1,128)S(1)}, u32[]{:S(2)}, u32[]{:S(2)}) collective-permute-start(f32[1,3584]{1,0:T(1,128)S(1)} %add.115), channel_id=1, source_target_pairs={{0,8},{1,9},{2,10},{3,11},{4,12},{5,13},{6,14},{7,15},{8,0},{9,1},... | collective-permute-start | bytes 43016 | tf_op jit(solution)/shard_map/ppermute | solution.py:26
  (32 other events, 554.4 us)

commit v2 on v1

--- a/solution.py
+++ b/solution.py
@@ -8,6 +8,7 @@
 from jax.sharding import PartitionSpec as P
 
 UNIT_SPLIT_COUNT = 4
+HINT = pl.CostEstimate(flops=10**11, transcendentals=0, bytes_accessed=1 << 20)
 EPSILON = 1e-06
 LANES = 128
 BF16 = jnp.bfloat16
@@ -89,10 +90,10 @@
         normed = values_ref[:, cols].astype(F32) * inverse
         rows = dot(picks, (normed * gain_ref[:, cols]).astype(BF16)).astype(BF16)
         for d in range(experts):
-            out_refs[d][0, :, cols] = rows[d * slots : (d + 1) * slots]
+            out_refs[d][:, cols] = rows[d * slots : (d + 1) * slots]
         return carry
 
-    lax.fori_loop(0, width // chunk, step, 0)
+    lax.fori_loop(0, width // chunk, step, 0, unroll=True)
 
 
 def select_both_kernel(
@@ -120,15 +121,15 @@
         rows = dot(picks, (normed * gain_ref[:, cols]).astype(BF16)).astype(BF16)
         scaled = (dot(picks, cot_ref[:, cols]) * gate_col).astype(BF16)
         for d in range(experts):
-            out_refs[d][0, :, cols] = rows[d * slots : (d + 1) * slots]
-            out_refs[d][1, :, cols] = scaled[d * slots : (d + 1) * slots]
+            out_refs[d][:, cols] = rows[d * slots : (d + 1) * slots]
+            out_refs[experts + d][:, cols] = scaled[d * slots : (d + 1) * slots]
         return carry
 
-    lax.fori_loop(0, width // chunk, step, 0)
+    lax.fori_loop(0, width // chunk, step, 0, unroll=True)
 
 
 def forward_kernel(rows_ref, gate_ref, up_ref, down_ref, out_ref):
-    rows = rows_ref[0]
+    rows = rows_ref[...]
     pre_gate = dot(rows, gate_ref[...])
     pre_up = dot(rows, up_ref[...])
     act = (pre_gate * jax.nn.sigmoid(pre_gate) * pre_up).astype(BF16)
@@ -140,26 +141,32 @@
         out_ref[:, cols] = dot(act, down_ref[:, cols]).astype(BF16)
         return carry
 
-    lax.fori_loop(0, width // chunk, step, 0)
+    lax.fori_loop(0, width // chunk, step, 0, unroll=True)
+
+
+def hidden_kernel(rows_ref, gate_ref, up_ref, act_ref, gate_factor_ref, up_factor_ref):
+    rows = rows_ref[...]
+    pre_gate = dot(rows, gate_ref[...])
+    pre_up = dot(rows, up_ref[...])
+    sigma = jax.nn.sigmoid(pre_gate)
+    swish = pre_gate * sigma
+    act_ref[...] = (swish * pre_up).astype(BF16)
+    gate_factor_ref[...] = pre_up * sigma * (1.0 + pre_gate * (1.0 - sigma))
+    up_factor_ref[...] = swish
 
 
 def backward_kernel(
-    rows_ref, gate_ref, up_ref, down_ref, out_ref, act_ref, gate_grad_ref, up_grad_ref, gain_ref
+    rows_ref, cot_ref, act_ref, gate_factor_ref, up_factor_ref, gate_ref, up_ref, down_ref,
+    out_ref, gate_grad_ref, up_grad_ref, gain_ref,
 ):
     width = gain_ref.shape[1]
     chunk = chunk_of(width)
-    pre_gate = dot(rows_ref[0], gate_ref[...])
-    pre_up = dot(rows_ref[0], up_ref[...])
-    upstream = dot_cols(rows_ref[1], down_ref[...])
-    sigma = jax.nn.sigmoid(pre_gate)
-    swish = pre_gate * sigma
-    act = (swish * pre_up).astype(BF16)
-    act_ref[...] = act
-    gate_grad = (upstream * pre_up * sigma * (1.0 + pre_gate * (1.0 - sigma))).astype(BF16)
-    up_grad = (upstream * swish).astype(BF16)
+    upstream = dot_cols(cot_ref[...], down_ref[...])
+    gate_grad = (upstream * gate_factor_ref[...]).astype(BF16)
+    up_grad = (upstream * up_factor_ref[...]).astype(BF16)
     gate_grad_ref[...] = gate_grad
     up_grad_ref[...] = up_grad
-    term = jnp.sum(act.astype(F32) * upstream, axis=1, keepdims=True)
+    term = jnp.sum(act_ref[...].astype(F32) * upstream, axis=1, keepdims=True)
     high = term.astype(BF16).astype(F32)
     lane = lax.broadcasted_iota(jnp.int32, (term.shape[0], LANES), 1)
     out_ref[:, width:] = jnp.where(lane < LANES // 2, high, term - high).astype(BF16)
@@ -168,25 +175,23 @@
         cols = pl.ds(pl.multiple_of(i * chunk, chunk), chunk)
         grads = dot_cols(gate_grad, gate_ref[cols, :]) + dot_cols(up_grad, up_ref[cols, :])
         out_ref[:, cols] = grads.astype(BF16)
-        gain_ref[:, cols] = jnp.sum(
-            grads * rows_ref[0, :, cols].astype(F32), axis=0, keepdims=True
-        )
+        gain_ref[:, cols] = jnp.sum(grads * rows_ref[:, cols].astype(F32), axis=0, keepdims=True)
         return carry
 
-    lax.fori_loop(0, width // chunk, step, 0)
+    lax.fori_loop(0, width // chunk, step, 0, unroll=True)
 
 
 def weight_kernel(
-    own_ref, other_ref, act_own, act_other, gate_own, gate_other, up_own, up_other,
-    grad_gate_ref, grad_up_ref, grad_down_ref,
+    own_ref, other_ref, cot_own, cot_other, act_own, act_other, gate_own, gate_other,
+    up_own, up_other, grad_gate_ref, grad_up_ref, grad_down_ref,
 ):
-    own, other = own_ref[0], other_ref[0]
+    own, other = own_ref[...], other_ref[...]
     grad_gate_ref[...] = (dot_rows(own, gate_own[...]) + dot_rows(other, gate_other[...])).astype(
         BF16
     )
     grad_up_ref[...] = (dot_rows(own, up_own[...]) + dot_rows(other, up_other[...])).astype(BF16)
     grad_down_ref[...] = (
-        dot_rows(act_own[...], own_ref[1]) + dot_rows(act_other[...], other_ref[1])
+        dot_rows(act_own[...], cot_own[...]) + dot_rows(act_other[...], cot_other[...])
     ).astype(BF16)
 
 
@@ -208,7 +213,7 @@
         out_ref[:, cols] = (values_ref[:, cols].astype(F32) + total).astype(BF16)
         return carry
 
-    lax.fori_loop(0, width // chunk, step, 0)
+    lax.fori_loop(0, width // chunk, step, 0, unroll=True)
 
 
 def input_grad_kernel(
@@ -264,16 +269,17 @@
         in_specs=[SMEM_SPEC] * scalars + [VMEM_SPEC] * (len(args) - scalars),
         out_specs=[VMEM_SPEC] * len(out_shapes),
         scratch_shapes=list(scratch),
+        cost_estimate=HINT,
         compiler_params=pltpu.CompilerParams(vmem_limit_bytes=48 << 20),
         name=name,
     )(*args)
 
 
-def weight_grads(own, other, acts, gates, ups):
-    pair, rows, width = own.shape
+def weight_grads(rows, cots, acts, gates, ups):
+    count, width = rows[0].shape
     units = acts[0].shape[1]
     chunk = chunk_of(width)
-    whole = pl.BlockSpec((rows, units), lambda i: (0, 0))
+    whole = pl.BlockSpec((count, units), lambda i: (0, 0))
     return pl.pallas_call(
         weight_kernel,
         grid=(width // chunk,),
@@ -282,34 +288,64 @@
             jax.ShapeDtypeStruct((width, units), BF16),
             jax.ShapeDtypeStruct((units, width), BF16),
         ],
-        in_specs=[pl.BlockSpec((pair, rows, chunk), lambda i: (0, 0, i))] * 2 + [whole] * 6,
+        in_specs=[pl.BlockSpec((count, chunk), lambda i: (0, i))] * 4 + [whole] * 6,
         out_specs=[
             pl.BlockSpec((chunk, units), lambda i: (i, 0)),
             pl.BlockSpec((chunk, units), lambda i: (i, 0)),
             pl.BlockSpec((units, chunk), lambda i: (0, i)),
         ],
+        cost_estimate=HINT,
         compiler_params=pltpu.CompilerParams(vmem_limit_bytes=48 << 20),
         name="weight_grads",
-    )(own, other, *acts, *gates, *ups)
-
-
-def gather_rows(blocks):
-    landed = [swap(block, d * UNIT_SPLIT_COUNT) if d else block for d, block in enumerate(blocks)]
-    crossed = [swap(block, 2) for block in landed]
-    own = jnp.concatenate(landed + crossed, axis=1)
-    return own, swap(own, 1)
-
-
-def return_rows(own, other, experts, slots):
-    partner = swap(other, 1)
-
-    def part(index):
-        rows = slice(index * slots, (index + 1) * slots)
-        return own[rows].astype(F32) + partner[rows].astype(F32)
-
-    crossed = [swap(part(experts + d).astype(BF16), 2) for d in range(experts)]
-    sums = [(part(d) + crossed[d].astype(F32)).astype(BF16) for d in range(experts)]
-    return [swap(block, d * UNIT_SPLIT_COUNT) if d else block for d, block in enumerate(sums)]
+    )(*rows, *cots, *acts, *gates, *ups)
+
+
+def after(values, *earlier):
+    return lax.optimization_barrier((tuple(values), tuple(earlier)))[0]
+
+
+def join_kernel(pieces, *refs):
+    in_refs, out_refs, sems = refs[: -len(pieces) - 1], refs[-len(pieces) - 1 : -1], refs[-1]
+    copies, k = [], 0
+    for out_ref, parts in zip(out_refs, pieces):
+        row = 0
+        for source, start, count in parts:
+            copies.append(
+                pltpu.make_async_copy(
+                    in_refs[source].at[pl.ds(start, count)],
+                    out_ref.at[pl.ds(row, count)],
+                    sems.at[k],
+                )
+            )
+            row += count
+            k += 1
+    for copy in copies:
+        copy.start()
+    for copy in copies:
+        copy.wait()
+
+
+def join(arrays, pieces, name):
+    width = arrays[0].shape[1]
+    pieces = tuple(tuple(parts) for parts in pieces)
+    return pl.pallas_call(
+        functools.partial(join_kernel, pieces),
+        out_shape=[
+            jax.ShapeDtypeStruct((sum(part[2] for part in parts), width), BF16)
+            for parts in pieces
+        ],
+        in_specs=[pl.BlockSpec(memory_space=pl.ANY)] * len(arrays),
+        out_specs=[VMEM_SPEC] * len(pieces),
+        scratch_shapes=[pltpu.SemaphoreType.DMA((sum(len(parts) for parts in pieces),))],
+        cost_estimate=HINT,
+        compiler_params=pltpu.CompilerParams(vmem_limit_bytes=48 << 20),
+        name=name,
+    )(*arrays)
+
+
+def part_of(own, partner, index, slots):
+    rows = slice(index * slots, (index + 1) * slots)
+    return own[rows].astype(F32) + partner[rows].astype(F32)
 
 
 def on_device(
@@ -337,31 +373,22 @@
     fwd_ids, bwd_ids = fwd_routes[0].T, bwd_routes[0].T
     fwd_g, bwd_g = fwd_gates[0].T, bwd_gates[0].T
 
-    bwd_blocks = call(
+    fwd_blocks = call(
+        functools.partial(select_norm_kernel, experts, slots),
+        [((slots, width), BF16)] * experts,
+        (plane, fwd_ids, fwd_input[0], norm_gain),
+        "select_fwd",
+        scalars=1,
+    )
+    both = call(
         functools.partial(select_both_kernel, experts, slots),
-        [((2, slots, width), BF16)] * experts,
+        [((slots, width), BF16)] * (2 * experts),
         (plane, bwd_ids, bwd_g, bwd_input[0], norm_gain, out_grad[0]),
         "select_bwd",
         scalars=1,
     )
-    fwd_blocks = call(
-        functools.partial(select_norm_kernel, experts, slots),
-        [((1, slots, width), BF16)] * experts,
-        (plane, fwd_ids, fwd_input[0], norm_gain),
-        "select_fwd",
-        scalars=1,
-    )
-    bwd_own, bwd_other = gather_rows(bwd_blocks)
-    fwd_own, fwd_other = gather_rows(fwd_blocks)
-    rows = bwd_own.shape[1]
-
-    def backward(rows_in, name):
-        return call(
-            backward_kernel,
-            [((rows, width + LANES), BF16)] + [((rows, units), BF16)] * 3 + [((1, width), F32)],
-            (rows_in, gate_matrix, up_matrix, down_matrix),
-            name,
-        )
+    bwd_blocks, cot_blocks = both[:experts], both[experts:]
+    rows = 2 * experts * slots
 
     def forward(rows_in, name):
         return call(
@@ -371,20 +398,118 @@
             name,
         )[0]
 
-    norm_own, act_own, dgate_own, dup_own, gain_own = backward(bwd_own, "backward_own")
-    norm_other, act_other, dgate_other, dup_other, gain_other = backward(bwd_other, "backward_other")
-    norm_back = return_rows(norm_own, norm_other, experts, slots)
+    def hidden(rows_in, name):
+        return call(
+            hidden_kernel,
+            [((rows, units), BF16), ((rows, units), F32), ((rows, units), F32)],
+            (rows_in, gate_matrix, up_matrix),
+            name,
+        )
+
+    def backward(rows_in, cot_in, made, name):
+        return call(
+            backward_kernel,
+            [((rows, width + LANES), BF16)] + [((rows, units), BF16)] * 2 + [((1, width), F32)],
+            (rows_in, cot_in, *made, gate_matrix, up_matrix, down_matrix),
+            name,
+        )
+
+    away = range(1, experts)
+    far = (experts - 1) * slots
+    half = experts * slots
+
+    def over_z(blocks):
+        return [swap(block, d * UNIT_SPLIT_COUNT) for d, block in zip(away, blocks)]
+
+    laid_far = [(k, 0, slots) for k in range(experts - 1)]
+
+    def laid_own(k, first):
+        return [(first, 0, slots), (first + 1, 0, far), (first + 2, k * slots, slots), (first + 3, 0, far)]
+
+    (near,) = join(
+        [fwd_blocks[0], bwd_blocks[0], cot_blocks[0]],
+        [[(k, 0, slots) for k in range(3)]],
+        "near_blocks",
+    )
+    near_crossed, fwd_landed = swap(near, 2), over_z(fwd_blocks[1:])
+    *bwd_send, near_crossed = after((*bwd_blocks[1:], near_crossed), *fwd_landed)
+    (fwd_far,) = join([*fwd_landed, near_crossed], [laid_far], "far_fwd")
+    *bwd_send, fwd_far = after((*bwd_send, fwd_far))
+    bwd_landed, fwd_far_crossed = over_z(bwd_send), swap(fwd_far, 2)
+    bwd_far, fwd_own = join(
+        [*bwd_landed, fwd_blocks[0], fwd_far, near_crossed, fwd_far_crossed],
+        [laid_far, laid_own(0, experts - 1)],
+        "far_bwd_own_fwd",
+    )
+    *cot_send, bwd_far, fwd_own = after((*cot_blocks[1:], bwd_far, fwd_own))
+    cot_landed, bwd_far_crossed, fwd_other = over_z(cot_send), swap(bwd_far, 2), swap(fwd_own, 1)
     out_own = forward(fwd_own, "forward_own")
+    *cot_landed, bwd_far_crossed, fwd_other = after(
+        (*cot_landed, bwd_far_crossed, fwd_other), out_own
+    )
+    cot_far, bwd_own = join(
+        [*cot_landed, bwd_blocks[0], bwd_far, near_crossed, bwd_far_crossed],
+        [laid_far, laid_own(1, experts - 1)],
+        "far_cot_own_bwd",
+    )
+    cot_far, bwd_own, fwd_other = after((cot_far, bwd_own, fwd_other))
+    cot_far_crossed, bwd_other = swap(cot_far, 2), swap(bwd_own, 1)
     out_other = forward(fwd_other, "forward_other")
-    out_back = return_rows(out_own, out_other, experts, slots)
+    out_partner = swap(out_other, 1)
+    made_own = hidden(bwd_own, "hidden_own")
+    made_other = hidden(bwd_other, "hidden_other")
+    cot_far_crossed, bwd_other, out_partner = after(
+        (cot_far_crossed, bwd_other, out_partner), made_own[0], made_other[0]
+    )
+    (cot_own,) = join(
+        [cot_blocks[0], cot_far, near_crossed, cot_far_crossed], [laid_own(2, 0)], "own_cot"
+    )
+    cot_own, out_partner = after((cot_own, out_partner))
+    cot_other = swap(cot_own, 1)
+    norm_own, dgate_own, dup_own, gain_own = backward(bwd_own, cot_own, made_own, "backward_own")
+    norm_other, dgate_other, dup_other, gain_other = backward(
+        bwd_other, cot_other, made_other, "backward_other"
+    )
+    norm_partner = swap(norm_other, 1)
+
+    def crossing(own, partner, first, count):
+        rows = slice(half + first * slots, half + (first + count) * slots)
+        return (own[rows].astype(F32) + partner[rows].astype(F32)).astype(BF16)
+
+    def send_home(own, partner, crossed, d):
+        block = (part_of(own, partner, d, slots) + crossed.astype(F32)).astype(BF16)
+        return swap(block, d * UNIT_SPLIT_COUNT) if d else block
+
+    def go_back(own, partner, *held):
+        middle = experts // 2
+        low, high = crossing(own, partner, 0, middle), crossing(own, partner, middle, middle)
+        low, high = after((low, high), *held)
+        high_crossed = swap(high, 2)
+        low_crossed = swap(low, 2)
+        back = {}
+        for d in range(experts)[::-1]:
+            whole = high_crossed if d >= middle else low_crossed
+            start = (d % middle) * slots
+            back[d] = send_home(own, partner, whole[start : start + slots], d)
+        return [back[d] for d in range(experts)], low_crossed
+
+    out_back, out_low = go_back(out_own, out_partner)
+    norm_back, norm_low = go_back(norm_own, norm_partner, out_low)
+    out_back = after(out_back, norm_low)
+    gain_sum = gain_own + gain_other
+    gain_sum = gain_sum + swap(gain_sum, 1)
+    (gain_sum,) = after((gain_sum,), norm_partner)
+    gain_crossed = swap(gain_sum, 2)
+    gain_sum, gain_crossed = after((gain_sum, gain_crossed), norm_low)
+    gain_sum = gain_sum + gain_crossed
+    gain_sum = sum([swap(gain_sum, d * UNIT_SPLIT_COUNT) for d in away], gain_sum)
     grad_gate, grad_up, grad_down = weight_grads(
-        bwd_own, bwd_other, (act_own, act_other), (dgate_own, dgate_other), (dup_own, dup_other)
-    )
-    gain_sum = gain_own + gain_other
-    bit = 1
-    while bit < devices:
-        gain_sum = gain_sum + swap(gain_sum, bit)
-        bit *= 2
+        (bwd_own, bwd_other),
+        (cot_own, cot_other),
+        (made_own[0], made_other[0]),
+        (dgate_own, dgate_other),
+        (dup_own, dup_other),
+    )
     gain_grad = gain_sum / norm_gain
 
     input_grad, gate_grad = call(

time: 279 us -> 231 us (0.83)
  waiting for transfers between devices: 149 us -> 111 us
  starting transfers between devices: 59.5 us -> 50 us
  Pallas kernels: 49.6 us -> 55.9 us
  local copies, waits for them, and re-layouts: 12.1 us -> 6.53 us
    ppermute x36 -> x33, waiting for transfers between devices: 137 us -> 103 us  [swap(): lax.ppermute(value, 'expert', [(source, source ^ mask) for source in rang...]
    ppermute x36 -> x33, starting transfers between devices: 54.8 us -> 45.3 us  [swap(): lax.ppermute(value, 'expert', [(source, source ^ mask) for source in rang...]
    pallas_call x0 -> x5, Pallas kernels: none -> 7.05 us  [join(): pl.pallas_call(functools.partial(join_kernel, pieces), out_shape=[jax.Sha...]
    unnamed x68, local copies, waits for them, and re-layouts: 12 us -> 6.53 us
    ppermute x2, waiting for transfers between devices: 12 us -> 7.65 us  [along_pipe(): lax.ppermute(value, 'pipe', [(source, source + steps) for source in range...]
    convert_element_type x6 -> x4, other arithmetic: 6.17 us -> 3.75 us  [the longest x2 2.21 us: send_home(): block = (part_of(own, partner, d, slots) + crossed.astype(F32)).astype(BF16)]
    pallas_call x8 -> x10, Pallas kernels: 40 us -> 39 us  [call(): pl.pallas_call(body, out_shape=[jax.ShapeDtypeStruct(shape, dtype) for sh...]
  transfers between devices with their start and end apart: 38 -> 35, of which waited for: 18 -> 14; matrix products, arithmetic and copies ran while one was open for 3% -> 3% of each run, Pallas kernels for 17% -> 20%
where the time goes in v2:
time: 231 us; the launch traced here: 230 us
  waiting for transfers between devices  111 us (48%)
  Pallas kernels  55.9 us (24%)
  starting transfers between devices  50 us (22%)
  local copies, waits for them, and re-layouts  6.53 us (3%)
  other arithmetic  5.79 us (3%)
    ppermute x33, waiting for transfers between devices, swap(): lax.ppermute(value, 'expert', [(source, source ^ mask) for source in rang...  103 us
    ppermute x33, starting transfers between devices, swap(): lax.ppermute(value, 'expert', [(source, source ^ mask) for source in rang...  45.3 us
    pallas_call x10, Pallas kernels, call(): pl.pallas_call(body, out_shape=[jax.ShapeDtypeStruct(shape, dtype) for sh...  39 us
    pallas_call x1, Pallas kernels, weight_grads(): pl.pallas_call(weight_kernel, grid=(width // chunk,), out_shape=[jax.Shap...  9.82 us
    ppermute x2, waiting for transfers between devices, along_pipe(): lax.ppermute(value, 'pipe', [(source, source + steps) for source in range...  7.65 us
    pallas_call x5, Pallas kernels, join(): pl.pallas_call(functools.partial(join_kernel, pieces), out_shape=[jax.Sha...  7.05 us
    unnamed x68, local copies, waits for them, and re-layouts  6.53 us
    ppermute x2, starting transfers between devices, along_pipe(): lax.ppermute(value, 'pipe', [(source, source + steps) for source in range...  4.67 us
  transfers between devices with their start and end apart: 35, of which 14 were waited for; matrix products, arithmetic and copies ran while one was open for 3% of the time, Pallas kernels for 20%

profile of v2, /device:TPU:0, one launch (start us, length us, event | category | flops | bytes accessed | tf_op | source)
XLA Modules:
  0.0 230.1 jit_solution(7817459124305557444)
XLA Ops:
  6.8 3.0 %collective-permute-start = (bf16[120,3584]{1,0:T(8,128)(2,1)S(1)}, bf16[120,3584]{1,0:T(8,128)(2,1)S(1)}, u32[]{:S(2)}, u32[]{:S(2)}) collective-permute-start(bf16[120,3584]{1,0:T(8,128)(2,1)S(1)} %near_blocks.1), channel_id=1, source_target_pairs={{0,2},{1,3},{2,0},{3,1},{4,6},{5,7},{6,4},{7,5},{8,10},{9,11},{10,... | collective-permute-start | bytes 2580488 | tf_op jit(solution)/shard_map/ppermute | solution.py:27
  11.3 2.6 %collective-permute-start.2 = (bf16[40,3584]{1,0:T(8,128)(2,1)S(1)}, bf16[40,3584]{1,0:T(8,128)(2,1)S(1)}, u32[]{:S(2)}, u32[]{:S(2)}) collective-permute-start(bf16[40,3584]{1,0:T(8,128)(2,1)S(1)} %get-tuple-element.89), channel_id=1, source_target_pairs={{0,8},{1,9},{2,10},{3,11},{4,12},{5,13},{6,14},{7,15},{8,0},{9,1},... | collective-permute-start | bytes 860168 | tf_op jit(solution)/shard_map/ppermute | solution.py:27
  14.1 9.1 %collective-permute-done.1.refs_0_ = bf16[40,3584]{1,0:T(8,128)(2,1)S(1)} collective-permute-done((bf16[40,3584]{1,0:T(8,128)(2,1)S(1)}, bf16[40,3584]{1,0:T(8,128)(2,1)S(1)}, u32[]{:S(2)}, u32[]{:S(2)}) %collective-permute-start.1) | collective-permute-done | bytes 286752 | tf_op jit(solution)/shard_map/ppermute | solution.py:27
  23.3 11.0 %collective-permute-done.2.refs_1_ = bf16[40,3584]{1,0:T(8,128)(2,1)S(1)} collective-permute-done((bf16[40,3584]{1,0:T(8,128)(2,1)S(1)}, bf16[40,3584]{1,0:T(8,128)(2,1)S(1)}, u32[]{:S(2)}, u32[]{:S(2)}) %collective-permute-start.2) | collective-permute-done | bytes 286752 | tf_op jit(solution)/shard_map/ppermute | solution.py:27
  35.1 5.0 %collective-permute-start.4 = (bf16[40,3584]{1,0:T(8,128)(2,1)S(1)}, bf16[40,3584]{1,0:T(8,128)(2,1)S(1)}, u32[]{:S(2)}, u32[]{:S(2)}) collective-permute-start(bf16[40,3584]{1,0:T(8,128)(2,1)S(1)} %get-tuple-element.95), channel_id=1, source_target_pairs={{0,4},{1,5},{2,6},{3,7},{4,0},{5,1},{6,2},{7,3},{8,12},{9,13},{10,... | collective-permute-start | bytes 860168 | tf_op jit(solution)/shard_map/ppermute | solution.py:27
  42.6 6.9 %collective-permute-done.4.refs_0_ = bf16[40,3584]{1,0:T(8,128)(2,1)S(1)} collective-permute-done((bf16[40,3584]{1,0:T(8,128)(2,1)S(1)}, bf16[40,3584]{1,0:T(8,128)(2,1)S(1)}, u32[]{:S(2)}, u32[]{:S(2)}) %collective-permute-start.4) | collective-permute-done | bytes 286752 | tf_op jit(solution)/shard_map/ppermute | solution.py:27
  49.5 13.5 %collective-permute-done.5.refs_1_ = bf16[40,3584]{1,0:T(8,128)(2,1)S(1)} collective-permute-done((bf16[40,3584]{1,0:T(8,128)(2,1)S(1)}, bf16[40,3584]{1,0:T(8,128)(2,1)S(1)}, u32[]{:S(2)}, u32[]{:S(2)}) %collective-permute-start.5) | collective-permute-done | bytes 286752 | tf_op jit(solution)/shard_map/ppermute | solution.py:27
  63.0 2.0 far_bwd_own_fwd.1
  65.0 3.7 %collective-permute-start.8 = (bf16[40,3584]{1,0:T(8,128)(2,1)S(1)}, bf16[40,3584]{1,0:T(8,128)(2,1)S(1)}, u32[]{:S(2)}, u32[]{:S(2)}) collective-permute-start(bf16[40,3584]{1,0:T(8,128)(2,1)S(1)} %get-tuple-element.102), channel_id=1, source_target_pairs={{0,4},{1,5},{2,6},{3,7},{4,0},{5,1},{6,2},{7,3},{8,12},{9,13},{10,... | collective-permute-start | bytes 860168 | tf_op jit(solution)/shard_map/ppermute | solution.py:27
  72.7 5.1 %forward_own.1 = bf16[320,3584]{1,0:T(8,128)(2,1)} custom-call(bf16[320,3584]{1,0:T(8,128)(2,1)} %get-tuple-element.101.rows_ref, bf16[3584,256]{1,0:T(8,128)(2,1)S(1)} %bitcast.27, bf16[3584,256]{1,0:T(8,128)(2,1)S(1)} %bitcast.33, bf16[256,3584]{1,0:T(8,128)(2,1)S(1)} %bitcast.41), custom_call_target="tpu_custom_call" | custom-call | flops 99999997952 | bytes 1048576 | tf_op jit(solution)/shard_map/forward_own/pallas_call | solution.py:266
  77.8 12.3 %collective-permute-done.9.refs_1_ = bf16[40,3584]{1,0:T(8,128)(2,1)S(1)} collective-permute-done((bf16[40,3584]{1,0:T(8,128)(2,1)S(1)}, bf16[40,3584]{1,0:T(8,128)(2,1)S(1)}, u32[]{:S(2)}, u32[]{:S(2)}) %collective-permute-start.9) | collective-permute-done | bytes 286752 | tf_op jit(solution)/shard_map/ppermute | solution.py:27
  90.2 2.3 %far_cot_own_bwd.1 = (bf16[120,3584]{1,0:T(8,128)(2,1)}, bf16[320,3584]{1,0:T(8,128)(2,1)}) custom-call(bf16[40,3584]{1,0:T(8,128)(2,1)S(1)} %collective-permute-done.8.refs_0_, bf16[40,3584]{1,0:T(8,128)(2,1)S(1)} %collective-permute-done.9.refs_1_, bf16[40,3584]{1,0:T(8,128)(2,1)S(1)} %collective-permute-done.10.refs_2_, bf16[40,3584]{1,0:T(8,128)(2,1)S(1)} %copy-done.26, ...), custom_call_target="tpu_custom_call" | custom-call | flops 99999997952 | bytes 1048576 | tf_op jit(solution)/shard_map/far_cot_own_bwd/pallas_call | solution.py:331
  92.6 3.0 %hidden_own.1 = (bf16[320,256]{1,0:T(8,128)(2,1)S(1)}, f32[320,256]{1,0:T(8,128)S(1)}, f32[320,256]{1,0:T(8,128)S(1)}) custom-call(bf16[320,3584]{1,0:T(8,128)(2,1)} %get-tuple-element.114.rows_ref.own_ref, bf16[3584,256]{1,0:T(8,128)(2,1)S(1)} %bitcast.28, bf16[3584,256]{1,0:T(8,128)(2,1)S(1)} %bitcast.34), custom_call_target="tpu_custom_call" | custom-call | flops 99999997952 | bytes 1048576 | tf_op jit(solution)/shard_map/hidden_own/pallas_call | solution.py:266
  97.2 5.1 %forward_other.1 = bf16[320,3584]{1,0:T(8,128)(2,1)} custom-call(bf16[320,3584]{1,0:T(8,128)(2,1)} %collective-permute-done.12.rows_ref, bf16[3584,256]{1,0:T(8,128)(2,1)S(1)} %bitcast.29, bf16[3584,256]{1,0:T(8,128)(2,1)S(1)} %bitcast.35, bf16[256,3584]{1,0:T(8,128)(2,1)S(1)} %bitcast.42), custom_call_target="tpu_custom_call" | custom-call | flops 99999997952 | bytes 1048576 | tf_op jit(solution)/shard_map/forward_other/pallas_call | solution.py:266
  102.5 3.1 %hidden_other.1 = (bf16[320,256]{1,0:T(8,128)(2,1)S(1)}, f32[320,256]{1,0:T(8,128)S(1)}, f32[320,256]{1,0:T(8,128)S(1)}) custom-call(bf16[320,3584]{1,0:T(8,128)(2,1)} %collective-permute-done.14.rows_ref.other_ref, bf16[3584,256]{1,0:T(8,128)(2,1)S(1)} %bitcast.30, bf16[3584,256]{1,0:T(8,128)(2,1)S(1)} %bitcast.36), custom_call_target="tpu_custom_call" | custom-call | flops 99999997952 | bytes 1048576 | tf_op jit(solution)/shard_map/hidden_other/pallas_call | solution.py:266
  105.6 11.9 %collective-permute-done.13.refs_3_ = bf16[120,3584]{1,0:T(8,128)(2,1)} collective-permute-done((bf16[120,3584]{1,0:T(8,128)(2,1)}, bf16[120,3584]{1,0:T(8,128)(2,1)}, u32[]{:S(2)}, u32[]{:S(2)}) %collective-permute-start.13) | collective-permute-done | bytes 860192 | tf_op jit(solution)/shard_map/ppermute | solution.py:27
  117.6 2.4 %own_cot.1.cot_ref.cot_own = bf16[320,3584]{1,0:T(8,128)(2,1)S(1)} custom-call(bf16[40,3584]{1,0:T(8,128)(2,1)S(1)} %copy-done.24, bf16[120,3584]{1,0:T(8,128)(2,1)} %get-tuple-element.113.refs_1_, bf16[120,3584]{1,0:T(8,128)(2,1)S(1)} %copy-done.9, bf16[120,3584]{1,0:T(8,128)(2,1)} %collective-permute-done.13.refs_3_), custom_call_target="tpu_custom_call" | custom-call | flops 99999997952 | bytes 1048576 | tf_op jit(solution)/shard_map/own_cot/pallas_call | solution.py:331
  125.8 7.3 %backward_other.1 = (bf16[320,3712]{1,0:T(8,128)(2,1)}, bf16[320,256]{1,0:T(8,128)(2,1)S(1)}, bf16[320,256]{1,0:T(8,128)(2,1)S(1)}, f32[1,3584]{1,0:T(1,128)S(1)}) custom-call(bf16[320,3584]{1,0:T(8,128)(2,1)} %collective-permute-done.14.rows_ref.other_ref, bf16[320,3584]{1,0:T(8,128)(2,1)} %copy-done.32, ...), custom_call_target="tpu_custom_call" | custom-call | flops 99999997952 | bytes 1048576 | tf_op jit(solution)/shard_map/backward_other/pallas_call | solution.py:266
  133.3 7.5 %backward_own.1 = (bf16[320,3712]{1,0:T(8,128)(2,1)}, bf16[320,256]{1,0:T(8,128)(2,1)S(1)}, bf16[320,256]{1,0:T(8,128)(2,1)S(1)}, f32[1,3584]{1,0:T(1,128)S(1)}) custom-call(bf16[320,3584]{1,0:T(8,128)(2,1)} %get-tuple-element.114.rows_ref.own_ref, bf16[320,3584]{1,0:T(8,128)(2,1)} %copy-done.4, bf16[320,256]{1,0:T(8,128)(2,1)S(1)} %get-tuple-element.116.act_ref.act_own, ...), custom_call_target="tpu_custom_call" | custom-call | flops 99999997952 | bytes 1048576 | tf_op jit(solution)/shard_map/backward_own/pallas_call | solution.py:266
  141.3 8.0 %collective-permute-done.16 = bf16[80,3584]{1,0:T(8,128)(2,1)} collective-permute-done((bf16[80,3584]{1,0:T(8,128)(2,1)}, bf16[80,3584]{1,0:T(8,128)(2,1)}, u32[]{:S(2)}, u32[]{:S(2)}) %collective-permute-start.16) | collective-permute-done | bytes 573472 | tf_op jit(solution)/shard_map/ppermute | solution.py:27
  151.0 3.7 %collective-permute-start.17 = (bf16[40,3584]{1,0:T(8,128)(2,1)S(1)}, bf16[40,3584]{1,0:T(8,128)(2,1)S(1)}, u32[]{:S(2)}, u32[]{:S(2)}) collective-permute-start(bf16[40,3584]{1,0:T(8,128)(2,1)S(1)} %get-tuple-element.164), channel_id=1, source_target_pairs={{0,4},{1,5},{2,6},{3,7},{4,0},{5,1},{6,2},{7,3},{8,12},{9,13},{10,... | collective-permute-start | bytes 860168 | tf_op jit(solution)/shard_map/ppermute | solution.py:27
  154.7 1.9 collective-permute-start.19
  163.6 9.8 %weight_grads.1 = (bf16[3584,256]{1,0:T(8,128)(2,1)}, bf16[3584,256]{1,0:T(8,128)(2,1)}, bf16[256,3584]{1,0:T(8,128)(2,1)}) custom-call(bf16[320,3584]{1,0:T(8,128)(2,1)S(1)} %copy-done.3, bf16[320,3584]{1,0:T(8,128)(2,1)} %collective-permute-done.14.rows_ref.other_ref, bf16[320,3584]{1,0:T(8,128)(2,1)} %copy-done.4, bf16[320,3584]{1,0:T(8,128)(2,1)} %copy-done.32, ...), custom_call_target="tpu_custom_call" | custom-call | flops 99999997952 | bytes 1048576 | tf_op jit(solution)/shard_map/weight_grads/pallas_call | solution.py:283
  173.4 2.9 %collective-permute-done.23 = bf16[80,3712]{1,0:T(8,128)(2,1)S(1)} collective-permute-done((bf16[80,3712]{1,0:T(8,128)(2,1)S(1)}, bf16[80,3712]{1,0:T(8,128)(2,1)S(1)}, u32[]{:S(2)}, u32[]{:S(2)}) %collective-permute-start.23) | collective-permute-done | bytes 593952 | tf_op jit(solution)/shard_map/ppermute | solution.py:27
  177.0 2.4 %collective-permute-start.34 = (f32[1,3584]{1,0:T(1,128)}, f32[1,3584]{1,0:T(1,128)}, u32[]{:S(2)}, u32[]{:S(2)}) collective-permute-start(f32[1,3584]{1,0:T(1,128)} %add.101), channel_id=1, source_target_pairs={{0,12},{1,13},{2,14},{3,15},{4,8},{5,9},{6,10},{7,11},{8,4},{9,5},... | collective-permute-start | bytes 43016 | tf_op jit(solution)/shard_map/ppermute | solution.py:27
  179.5 7.0 %collective-permute-done.26 = bf16[80,3712]{1,0:T(8,128)(2,1)S(1)} collective-permute-done((bf16[80,3712]{1,0:T(8,128)(2,1)S(1)}, bf16[80,3712]{1,0:T(8,128)(2,1)S(1)}, u32[]{:S(2)}, u32[]{:S(2)}) %collective-permute-start.26) | collective-permute-done | bytes 593952 | tf_op jit(solution)/shard_map/ppermute | solution.py:27
  187.7 2.4 %collective-permute-start.27 = (bf16[40,3712]{1,0:T(8,128)(2,1)S(1)}, bf16[40,3712]{1,0:T(8,128)(2,1)S(1)}, u32[]{:S(2)}, u32[]{:S(2)}) collective-permute-start(bf16[40,3712]{1,0:T(8,128)(2,1)S(1)} %get-tuple-element.152), channel_id=1, source_target_pairs={{0,8},{1,9},{2,10},{3,11},{4,12},{5,13},{6,14},{7,15},{8,0},{9,1},... | collective-permute-start | bytes 890888 | tf_op jit(solution)/shard_map/ppermute | solution.py:27
  192.4 7.3 %collective-permute-done.25.refs_1_ = bf16[40,3712]{1,0:T(8,128)(2,1)S(1)} collective-permute-done((bf16[40,3712]{1,0:T(8,128)(2,1)S(1)}, bf16[40,3712]{1,0:T(8,128)(2,1)S(1)}, u32[]{:S(2)}, u32[]{:S(2)}) %collective-permute-start.25) | collective-permute-done | bytes 296992 | tf_op jit(solution)/shard_map/ppermute | solution.py:27
  199.7 10.9 %collective-permute-done.27.refs_2_ = bf16[40,3712]{1,0:T(8,128)(2,1)S(1)} collective-permute-done((bf16[40,3712]{1,0:T(8,128)(2,1)S(1)}, bf16[40,3712]{1,0:T(8,128)(2,1)S(1)}, u32[]{:S(2)}, u32[]{:S(2)}) %collective-permute-start.27) | collective-permute-done | bytes 296992 | tf_op jit(solution)/shard_map/ppermute | solution.py:27
  210.6 3.4 %collective-permute-start.24 = (bf16[64,3584]{1,0:T(8,128)(2,1)S(1)}, bf16[64,3584]{1,0:T(8,128)(2,1)S(1)}, u32[]{:S(2)}, u32[]{:S(2)}) collective-permute-start(bf16[64,3584]{1,0:T(8,128)(2,1)S(1)} %mixed.1), channel_id=1, source_target_pairs={{0,16},{1,17},{2,18},{3,19},{4,20},{5,21},{6,22},{7,23},{8,24},{9,... | collective-permute-start | bytes 1376264 | tf_op jit(solution)/shard_map/ppermute | solution.py:33
  214.0 4.2 %input_grad.1 = (bf16[64,3584]{1,0:T(8,128)(2,1)S(1)}, f32[2,64]{1,0:T(2,128)}) custom-call(s32[1]{0:T(128)} %bitcast.plane_ref, s32[2,64]{1,0:T(2,128)S(1)} %bitcast.52, bf16[2,64]{1,0:T(2,128)(2,1)S(1)} %bitcast.55, bf16[64,3584]{1,0:T(8,128)(2,1)S(1)} %bitcast.46, bf16[64,3584]{1,0:T(8,128)(2,1)S(1)} %bitcast.48, f32[1,3584]{1,0:T(1,128)S(1)} %copy-done.2, ...), custom_call_target="tpu_custom_call" | custom-call | flops 99999997952 | bytes 1048576 | tf_op jit(solution)/shard_map/input_grad/pallas_call | solution.py:266
  220.9 7.7 %collective-permute-done.29 = bf16[64,3584]{1,0:T(8,128)(2,1)S(1)} collective-permute-done((bf16[64,3584]{1,0:T(8,128)(2,1)S(1)}, bf16[64,3584]{1,0:T(8,128)(2,1)S(1)}, u32[]{:S(2)}, u32[]{:S(2)}) %collective-permute-start.29) | collective-permute-done | bytes 458784 | tf_op jit(solution)/shard_map/ppermute | solution.py:33
  (130 shorter events, 40.3 us)
Async XLA Ops:
  6.8 27.5 %collective-permute-start = (bf16[120,3584]{1,0:T(8,128)(2,1)S(1)}, bf16[120,3584]{1,0:T(8,128)(2,1)S(1)}, u32[]{:S(2)}, u32[]{:S(2)}) collective-permute-start(bf16[120,3584]{1,0:T(8,128)(2,1)S(1)} %near_blocks.1), channel_id=1, source_target_pairs={{0,2},{1,3},{2,0},{3,1},{4,6},{5,7},{6,4},{7,5},{8,10},{9,11},{10,... | collective-permute-start | bytes 2580488 | tf_op jit(solution)/shard_map/ppermute | solution.py:27
  9.8 13.5 %collective-permute-start.1 = (bf16[40,3584]{1,0:T(8,128)(2,1)S(1)}, bf16[40,3584]{1,0:T(8,128)(2,1)S(1)}, u32[]{:S(2)}, u32[]{:S(2)}) collective-permute-start(bf16[40,3584]{1,0:T(8,128)(2,1)S(1)} %get-tuple-element.88), channel_id=1, source_target_pairs={{0,4},{1,5},{2,6},{3,7},{4,0},{5,1},{6,2},{7,3},{8,12},{9,13},{10,... | collective-permute-start | bytes 860168 | tf_op jit(solution)/shard_map/ppermute | solution.py:27
  11.3 23.0 %collective-permute-start.2 = (bf16[40,3584]{1,0:T(8,128)(2,1)S(1)}, bf16[40,3584]{1,0:T(8,128)(2,1)S(1)}, u32[]{:S(2)}, u32[]{:S(2)}) collective-permute-start(bf16[40,3584]{1,0:T(8,128)(2,1)S(1)} %get-tuple-element.89), channel_id=1, source_target_pairs={{0,8},{1,9},{2,10},{3,11},{4,12},{5,13},{6,14},{7,15},{8,0},{9,1},... | collective-permute-start | bytes 860168 | tf_op jit(solution)/shard_map/ppermute | solution.py:27
  13.9 20.4 %collective-permute-start.3 = (bf16[40,3584]{1,0:T(8,128)(2,1)S(1)}, bf16[40,3584]{1,0:T(8,128)(2,1)S(1)}, u32[]{:S(2)}, u32[]{:S(2)}) collective-permute-start(bf16[40,3584]{1,0:T(8,128)(2,1)S(1)} %get-tuple-element.90), channel_id=1, source_target_pairs={{0,12},{1,13},{2,14},{3,15},{4,8},{5,9},{6,10},{7,11},{8,4},{9,5},... | collective-permute-start | bytes 860168 | tf_op jit(solution)/shard_map/ppermute | solution.py:27
  34.5 28.5 %collective-permute-start.7 = (bf16[120,3584]{1,0:T(8,128)(2,1)S(1)}, bf16[120,3584]{1,0:T(8,128)(2,1)S(1)}, u32[]{:S(2)}, u32[]{:S(2)}) collective-permute-start(bf16[120,3584]{1,0:T(8,128)(2,1)S(1)} %far_fwd.1.refs_4_), channel_id=1, source_target_pairs={{0,2},{1,3},{2,0},{3,1},{4,6},{5,7},{6,4},{7,5},{8,10},{9,11},{10,... | collective-permute-start | bytes 2580488 | tf_op jit(solution)/shard_map/ppermute | solution.py:27
  35.1 14.4 %collective-permute-start.4 = (bf16[40,3584]{1,0:T(8,128)(2,1)S(1)}, bf16[40,3584]{1,0:T(8,128)(2,1)S(1)}, u32[]{:S(2)}, u32[]{:S(2)}) collective-permute-start(bf16[40,3584]{1,0:T(8,128)(2,1)S(1)} %get-tuple-element.95), channel_id=1, source_target_pairs={{0,4},{1,5},{2,6},{3,7},{4,0},{5,1},{6,2},{7,3},{8,12},{9,13},{10,... | collective-permute-start | bytes 860168 | tf_op jit(solution)/shard_map/ppermute | solution.py:27
  40.1 22.9 %collective-permute-start.5 = (bf16[40,3584]{1,0:T(8,128)(2,1)S(1)}, bf16[40,3584]{1,0:T(8,128)(2,1)S(1)}, u32[]{:S(2)}, u32[]{:S(2)}) collective-permute-start(bf16[40,3584]{1,0:T(8,128)(2,1)S(1)} %get-tuple-element.96), channel_id=1, source_target_pairs={{0,8},{1,9},{2,10},{3,11},{4,12},{5,13},{6,14},{7,15},{8,0},{9,1},... | collective-permute-start | bytes 860168 | tf_op jit(solution)/shard_map/ppermute | solution.py:27
  41.1 21.9 %collective-permute-start.6 = (bf16[40,3584]{1,0:T(8,128)(2,1)S(1)}, bf16[40,3584]{1,0:T(8,128)(2,1)S(1)}, u32[]{:S(2)}, u32[]{:S(2)}) collective-permute-start(bf16[40,3584]{1,0:T(8,128)(2,1)S(1)} %get-tuple-element.97), channel_id=1, source_target_pairs={{0,12},{1,13},{2,14},{3,15},{4,8},{5,9},{6,10},{7,11},{8,4},{9,5},... | collective-permute-start | bytes 860168 | tf_op jit(solution)/shard_map/ppermute | solution.py:27
  65.0 12.8 %collective-permute-start.8 = (bf16[40,3584]{1,0:T(8,128)(2,1)S(1)}, bf16[40,3584]{1,0:T(8,128)(2,1)S(1)}, u32[]{:S(2)}, u32[]{:S(2)}) collective-permute-start(bf16[40,3584]{1,0:T(8,128)(2,1)S(1)} %get-tuple-element.102), channel_id=1, source_target_pairs={{0,4},{1,5},{2,6},{3,7},{4,0},{5,1},{6,2},{7,3},{8,12},{9,13},{10,... | collective-permute-start | bytes 860168 | tf_op jit(solution)/shard_map/ppermute | solution.py:27
  68.7 21.5 %collective-permute-start.9 = (bf16[40,3584]{1,0:T(8,128)(2,1)S(1)}, bf16[40,3584]{1,0:T(8,128)(2,1)S(1)}, u32[]{:S(2)}, u32[]{:S(2)}) collective-permute-start(bf16[40,3584]{1,0:T(8,128)(2,1)S(1)} %get-tuple-element.103), channel_id=1, source_target_pairs={{0,8},{1,9},{2,10},{3,11},{4,12},{5,13},{6,14},{7,15},{8,0},{9,1},... | collective-permute-start | bytes 860168 | tf_op jit(solution)/shard_map/ppermute | solution.py:27
  69.8 20.4 %collective-permute-start.10 = (bf16[40,3584]{1,0:T(8,128)(2,1)S(1)}, bf16[40,3584]{1,0:T(8,128)(2,1)S(1)}, u32[]{:S(2)}, u32[]{:S(2)}) collective-permute-start(bf16[40,3584]{1,0:T(8,128)(2,1)S(1)} %get-tuple-element.104), channel_id=1, source_target_pairs={{0,12},{1,13},{2,14},{3,15},{4,8},{5,9},{6,10},{7,11},{8,4},{9,5},... | collective-permute-start | bytes 860168 | tf_op jit(solution)/shard_map/ppermute | solution.py:27
  71.2 19.0 %collective-permute-start.11 = (bf16[120,3584]{1,0:T(8,128)(2,1)S(1)}, bf16[120,3584]{1,0:T(8,128)(2,1)S(1)}, u32[]{:S(2)}, u32[]{:S(2)}) collective-permute-start(bf16[120,3584]{1,0:T(8,128)(2,1)S(1)} %get-tuple-element.105.refs_4_), channel_id=1, source_target_pairs={{0,2},{1,3},{2,0},{3,1},{4,6},{5,7},{6,4},{7,5},{8,10},{9,11},{10,... | collective-permute-start | bytes 2580488 | tf_op jit(solution)/shard_map/ppermute | solution.py:27
  72.7 17.5 %collective-permute-start.12 = (bf16[320,3584]{1,0:T(8,128)(2,1)}, bf16[320,3584]{1,0:T(8,128)(2,1)}, u32[]{:S(2)}, u32[]{:S(2)}) collective-permute-start(bf16[320,3584]{1,0:T(8,128)(2,1)} %get-tuple-element.101.rows_ref), channel_id=1, source_target_pairs={{0,1},{1,0},{2,3},{3,2},{4,5},{5,4},{6,7},{7,6},{8,9},{9,8},{10,11... | collective-permute-start | bytes 6881288 | tf_op jit(solution)/shard_map/ppermute | solution.py:27
  95.7 21.9 %collective-permute-start.13 = (bf16[120,3584]{1,0:T(8,128)(2,1)}, bf16[120,3584]{1,0:T(8,128)(2,1)}, u32[]{:S(2)}, u32[]{:S(2)}) collective-permute-start(bf16[120,3584]{1,0:T(8,128)(2,1)} %get-tuple-element.113.refs_1_), channel_id=1, source_target_pairs={{0,2},{1,3},{2,0},{3,1},{4,6},{5,7},{6,4},{7,5},{8,10},{9,11},{10,... | collective-permute-start | bytes 2580488 | tf_op jit(solution)/shard_map/ppermute | solution.py:27
  102.3 15.3 %collective-permute-start.15 = (bf16[320,3584]{1,0:T(8,128)(2,1)}, bf16[320,3584]{1,0:T(8,128)(2,1)S(1)}, u32[]{:S(2)}, u32[]{:S(2)}) collective-permute-start(bf16[320,3584]{1,0:T(8,128)(2,1)} %forward_other.1), channel_id=1, source_target_pairs={{0,1},{1,0},{2,3},{3,2},{4,5},{5,4},{6,7},{7,6},{8,9},{9,8},{10,11... | collective-permute-start | bytes 6881288 | tf_op jit(solution)/shard_map/ppermute | solution.py:27
  121.8 19.5 %collective-permute-start.18 = (bf16[80,3584]{1,0:T(8,128)(2,1)}, bf16[80,3584]{1,0:T(8,128)(2,1)}, u32[]{:S(2)}, u32[]{:S(2)}) collective-permute-start(bf16[80,3584]{1,0:T(8,128)(2,1)} %get-tuple-element.122), channel_id=1, source_target_pairs={{0,2},{1,3},{2,0},{3,1},{4,6},{5,7},{6,4},{7,5},{8,10},{9,11},{10,... | collective-permute-start | bytes 1720328 | tf_op jit(solution)/shard_map/ppermute | solution.py:27
  123.3 26.0 %collective-permute-start.16 = (bf16[80,3584]{1,0:T(8,128)(2,1)}, bf16[80,3584]{1,0:T(8,128)(2,1)}, u32[]{:S(2)}, u32[]{:S(2)}) collective-permute-start(bf16[80,3584]{1,0:T(8,128)(2,1)} %get-tuple-element.121), channel_id=1, source_target_pairs={{0,2},{1,3},{2,0},{3,1},{4,6},{5,7},{6,4},{7,5},{8,10},{9,11},{10,... | collective-permute-start | bytes 1720328 | tf_op jit(solution)/shard_map/ppermute | solution.py:27
  133.2 24.9 %collective-permute-start.22 = (bf16[320,3712]{1,0:T(8,128)(2,1)}, bf16[320,3712]{1,0:T(8,128)(2,1)S(1)}, u32[]{:S(2)}, u32[]{:S(2)}) collective-permute-start(bf16[320,3712]{1,0:T(8,128)(2,1)} %get-tuple-element.130), channel_id=1, source_target_pairs={{0,1},{1,0},{2,3},{3,2},{4,5},{5,4},{6,7},{7,6},{8,9},{9,8},{10,11... | collective-permute-start | bytes 7127048 | tf_op jit(solution)/shard_map/ppermute | solution.py:27
  140.9 17.2 %collective-permute-start.30 = (f32[1,3584]{1,0:T(1,128)S(1)}, f32[1,3584]{1,0:T(1,128)S(1)}, u32[]{:S(2)}, u32[]{:S(2)}) collective-permute-start(f32[1,3584]{1,0:T(1,128)S(1)} %add.99), channel_id=1, source_target_pairs={{0,1},{1,0},{2,3},{3,2},{4,5},{5,4},{6,7},{7,6},{8,9},{9,8},{10,11... | collective-permute-start | bytes 43016 | tf_op jit(solution)/shard_map/ppermute | solution.py:27
  151.0 28.4 %collective-permute-start.17 = (bf16[40,3584]{1,0:T(8,128)(2,1)S(1)}, bf16[40,3584]{1,0:T(8,128)(2,1)S(1)}, u32[]{:S(2)}, u32[]{:S(2)}) collective-permute-start(bf16[40,3584]{1,0:T(8,128)(2,1)S(1)} %get-tuple-element.164), channel_id=1, source_target_pairs={{0,4},{1,5},{2,6},{3,7},{4,0},{5,1},{6,2},{7,3},{8,12},{9,13},{10,... | collective-permute-start | bytes 860168 | tf_op jit(solution)/shard_map/ppermute | solution.py:27
  154.7 24.7 %collective-permute-start.19 = (bf16[40,3584]{1,0:T(8,128)(2,1)S(1)}, bf16[40,3584]{1,0:T(8,128)(2,1)S(1)}, u32[]{:S(2)}, u32[]{:S(2)}) collective-permute-start(bf16[40,3584]{1,0:T(8,128)(2,1)S(1)} %get-tuple-element.156), channel_id=1, source_target_pairs={{0,8},{1,9},{2,10},{3,11},{4,12},{5,13},{6,14},{7,15},{8,0},{9,1},... | collective-permute-start | bytes 860168 | tf_op jit(solution)/shard_map/ppermute | solution.py:27
  156.7 22.8 %collective-permute-start.20 = (bf16[40,3584]{1,0:T(8,128)(2,1)S(1)}, bf16[40,3584]{1,0:T(8,128)(2,1)S(1)}, u32[]{:S(2)}, u32[]{:S(2)}) collective-permute-start(bf16[40,3584]{1,0:T(8,128)(2,1)S(1)} %get-tuple-element.155), channel_id=1, source_target_pairs={{0,12},{1,13},{2,14},{3,15},{4,8},{5,9},{6,10},{7,11},{8,4},{9,5},... | collective-permute-start | bytes 860168 | tf_op jit(solution)/shard_map/ppermute | solution.py:27
  160.0 16.4 %collective-permute-start.23 = (bf16[80,3712]{1,0:T(8,128)(2,1)S(1)}, bf16[80,3712]{1,0:T(8,128)(2,1)S(1)}, u32[]{:S(2)}, u32[]{:S(2)}) collective-permute-start(bf16[80,3712]{1,0:T(8,128)(2,1)S(1)} %get-tuple-element.131), channel_id=1, source_target_pairs={{0,2},{1,3},{2,0},{3,1},{4,6},{5,7},{6,4},{7,5},{8,10},{9,11},{10,... | collective-permute-start | bytes 1781768 | tf_op jit(solution)/shard_map/ppermute | solution.py:27
  162.0 24.6 %collective-permute-start.26 = (bf16[80,3712]{1,0:T(8,128)(2,1)S(1)}, bf16[80,3712]{1,0:T(8,128)(2,1)S(1)}, u32[]{:S(2)}, u32[]{:S(2)}) collective-permute-start(bf16[80,3712]{1,0:T(8,128)(2,1)S(1)} %get-tuple-element.136), channel_id=1, source_target_pairs={{0,2},{1,3},{2,0},{3,1},{4,6},{5,7},{6,4},{7,5},{8,10},{9,11},{10,... | collective-permute-start | bytes 1781768 | tf_op jit(solution)/shard_map/ppermute | solution.py:27
  177.0 42.5 %collective-permute-start.34 = (f32[1,3584]{1,0:T(1,128)}, f32[1,3584]{1,0:T(1,128)}, u32[]{:S(2)}, u32[]{:S(2)}) collective-permute-start(f32[1,3584]{1,0:T(1,128)} %add.101), channel_id=1, source_target_pairs={{0,12},{1,13},{2,14},{3,15},{4,8},{5,9},{6,10},{7,11},{8,4},{9,5},... | collective-permute-start | bytes 43016 | tf_op jit(solution)/shard_map/ppermute | solution.py:27
  179.5 40.1 %collective-permute-start.33 = (f32[1,3584]{1,0:T(1,128)}, f32[1,3584]{1,0:T(1,128)}, u32[]{:S(2)}, u32[]{:S(2)}) collective-permute-start(f32[1,3584]{1,0:T(1,128)} %add.101), channel_id=1, source_target_pairs={{0,8},{1,9},{2,10},{3,11},{4,12},{5,13},{6,14},{7,15},{8,0},{9,1},... | collective-permute-start | bytes 43016 | tf_op jit(solution)/shard_map/ppermute | solution.py:27
  187.0 12.6 %collective-permute-start.25 = (bf16[40,3712]{1,0:T(8,128)(2,1)S(1)}, bf16[40,3712]{1,0:T(8,128)(2,1)S(1)}, u32[]{:S(2)}, u32[]{:S(2)}) collective-permute-start(bf16[40,3712]{1,0:T(8,128)(2,1)S(1)} %get-tuple-element.160), channel_id=1, source_target_pairs={{0,4},{1,5},{2,6},{3,7},{4,0},{5,1},{6,2},{7,3},{8,12},{9,13},{10,... | collective-permute-start | bytes 890888 | tf_op jit(solution)/shard_map/ppermute | solution.py:27
  187.7 22.9 %collective-permute-start.27 = (bf16[40,3712]{1,0:T(8,128)(2,1)S(1)}, bf16[40,3712]{1,0:T(8,128)(2,1)S(1)}, u32[]{:S(2)}, u32[]{:S(2)}) collective-permute-start(bf16[40,3712]{1,0:T(8,128)(2,1)S(1)} %get-tuple-element.152), channel_id=1, source_target_pairs={{0,8},{1,9},{2,10},{3,11},{4,12},{5,13},{6,14},{7,15},{8,0},{9,1},... | collective-permute-start | bytes 890888 | tf_op jit(solution)/shard_map/ppermute | solution.py:27
  190.1 23.9 %collective-permute-start.28 = (bf16[40,3712]{1,0:T(8,128)(2,1)S(1)}, bf16[40,3712]{1,0:T(8,128)(2,1)S(1)}, u32[]{:S(2)}, u32[]{:S(2)}) collective-permute-start(bf16[40,3712]{1,0:T(8,128)(2,1)S(1)} %get-tuple-element.151), channel_id=1, source_target_pairs={{0,12},{1,13},{2,14},{3,15},{4,8},{5,9},{6,10},{7,11},{8,4},{9,5},... | collective-permute-start | bytes 890888 | tf_op jit(solution)/shard_map/ppermute | solution.py:27
  199.7 19.8 %collective-permute-start.32 = (f32[1,3584]{1,0:T(1,128)}, f32[1,3584]{1,0:T(1,128)S(1)}, u32[]{:S(2)}, u32[]{:S(2)}) collective-permute-start(f32[1,3584]{1,0:T(1,128)} %add.101), channel_id=1, source_target_pairs={{0,4},{1,5},{2,6},{3,7},{4,0},{5,1},{6,2},{7,3},{8,12},{9,13},{10,... | collective-permute-start | bytes 43016 | tf_op jit(solution)/shard_map/ppermute | solution.py:27
  210.6 10.3 %collective-permute-start.24 = (bf16[64,3584]{1,0:T(8,128)(2,1)S(1)}, bf16[64,3584]{1,0:T(8,128)(2,1)S(1)}, u32[]{:S(2)}, u32[]{:S(2)}) collective-permute-start(bf16[64,3584]{1,0:T(8,128)(2,1)S(1)} %mixed.1), channel_id=1, source_target_pairs={{0,16},{1,17},{2,18},{3,19},{4,20},{5,21},{6,22},{7,23},{8,24},{9,... | collective-permute-start | bytes 1376264 | tf_op jit(solution)/shard_map/ppermute | solution.py:33
  218.2 10.4 %collective-permute-start.29 = (bf16[64,3584]{1,0:T(8,128)(2,1)S(1)}, bf16[64,3584]{1,0:T(8,128)(2,1)S(1)}, u32[]{:S(2)}, u32[]{:S(2)}) collective-permute-start(bf16[64,3584]{1,0:T(8,128)(2,1)S(1)} %get-tuple-element.137), channel_id=1, source_target_pairs={{16,0},{17,1},{18,2},{19,3},{20,4},{21,5},{22,6},{23,7},{24,8},{25... | collective-permute-start | bytes 1376264 | tf_op jit(solution)/shard_map/ppermute | solution.py:33
  (36 other events, 479.1 us)

commit v3 on v2

--- a/solution.py
+++ b/solution.py
@@ -195,6 +195,13 @@
     ).astype(BF16)
 
 
+def add_kernel(first, slots, own_ref, partner_ref, crossed_ref, *out_refs):
+    for i, out_ref in enumerate(out_refs):
+        rows, landed = pl.ds((first + i) * slots, slots), pl.ds(i * slots, slots)
+        total = own_ref[rows, :].astype(F32) + partner_ref[rows, :].astype(F32)
+        out_ref[...] = (total + crossed_ref[landed, :].astype(F32)).astype(BF16)
+
+
 def mixed_kernel(experts, slots, plane_ref, routes_ref, gates_ref, values_ref, *refs):
     block_refs, out_ref = refs[:experts], refs[experts]
     width = values_ref.shape[1]
@@ -262,15 +269,15 @@
 VMEM_SPEC = pl.BlockSpec(memory_space=pltpu.VMEM)
 
 
-def call(body, out_shapes, args, name, scratch=(), scalars=0):
+def call(body, out_shapes, args, name, scratch=(), scalars=0, hint=HINT):
     return pl.pallas_call(
         body,
         out_shape=[jax.ShapeDtypeStruct(shape, dtype) for shape, dtype in out_shapes],
         in_specs=[SMEM_SPEC] * scalars + [VMEM_SPEC] * (len(args) - scalars),
         out_specs=[VMEM_SPEC] * len(out_shapes),
         scratch_shapes=list(scratch),
-        cost_estimate=HINT,
-        compiler_params=pltpu.CompilerParams(vmem_limit_bytes=48 << 20),
+        cost_estimate=hint,
+        compiler_params=pltpu.CompilerParams(vmem_limit_bytes=12 << 20),
         name=name,
     )(*args)
 
@@ -295,7 +302,7 @@
             pl.BlockSpec((units, chunk), lambda i: (0, i)),
         ],
         cost_estimate=HINT,
-        compiler_params=pltpu.CompilerParams(vmem_limit_bytes=48 << 20),
+        compiler_params=pltpu.CompilerParams(vmem_limit_bytes=20 << 20),
         name="weight_grads",
     )(*rows, *cots, *acts, *gates, *ups)
 
@@ -338,7 +345,7 @@
         out_specs=[VMEM_SPEC] * len(pieces),
         scratch_shapes=[pltpu.SemaphoreType.DMA((sum(len(parts) for parts in pieces),))],
         cost_estimate=HINT,
-        compiler_params=pltpu.CompilerParams(vmem_limit_bytes=48 << 20),
+        compiler_params=pltpu.CompilerParams(vmem_limit_bytes=4 << 20),
         name=name,
     )(*arrays)
 
@@ -466,43 +473,38 @@
     )
     cot_own, out_partner = after((cot_own, out_partner))
     cot_other = swap(cot_own, 1)
-    norm_own, dgate_own, dup_own, gain_own = backward(bwd_own, cot_own, made_own, "backward_own")
-    norm_other, dgate_other, dup_other, gain_other = backward(
-        bwd_other, cot_other, made_other, "backward_other"
-    )
-    norm_partner = swap(norm_other, 1)
+    middle = experts // 2
 
     def crossing(own, partner, first, count):
         rows = slice(half + first * slots, half + (first + count) * slots)
         return (own[rows].astype(F32) + partner[rows].astype(F32)).astype(BF16)
 
-    def send_home(own, partner, crossed, d):
-        block = (part_of(own, partner, d, slots) + crossed.astype(F32)).astype(BF16)
-        return swap(block, d * UNIT_SPLIT_COUNT) if d else block
-
-    def go_back(own, partner, *held):
-        middle = experts // 2
-        low, high = crossing(own, partner, 0, middle), crossing(own, partner, middle, middle)
-        low, high = after((low, high), *held)
-        high_crossed = swap(high, 2)
-        low_crossed = swap(low, 2)
+    def home(own, partner, crossed, first):
+        sums = call(
+            functools.partial(add_kernel, first, slots),
+            [((slots, own.shape[1]), BF16)] * middle,
+            (own, partner, crossed),
+            "add_columns",
+            hint=None,
+        )
         back = {}
-        for d in range(experts)[::-1]:
-            whole = high_crossed if d >= middle else low_crossed
-            start = (d % middle) * slots
-            back[d] = send_home(own, partner, whole[start : start + slots], d)
-        return [back[d] for d in range(experts)], low_crossed
-
-    out_back, out_low = go_back(out_own, out_partner)
-    norm_back, norm_low = go_back(norm_own, norm_partner, out_low)
-    out_back = after(out_back, norm_low)
-    gain_sum = gain_own + gain_other
-    gain_sum = gain_sum + swap(gain_sum, 1)
-    (gain_sum,) = after((gain_sum,), norm_partner)
-    gain_crossed = swap(gain_sum, 2)
-    gain_sum, gain_crossed = after((gain_sum, gain_crossed), norm_low)
-    gain_sum = gain_sum + gain_crossed
-    gain_sum = sum([swap(gain_sum, d * UNIT_SPLIT_COUNT) for d in away], gain_sum)
+        for i in range(middle)[::-1]:
+            d = first + i
+            back[i] = swap(sums[i], d * UNIT_SPLIT_COUNT) if d else sums[i]
+        return [back[i] for i in range(middle)]
+
+    out_high = swap(crossing(out_own, out_partner, middle, middle), 2)
+    out_low = swap(crossing(out_own, out_partner, 0, middle), 2)
+    norm_other, dgate_other, dup_other, gain_other = backward(
+        bwd_other, cot_other, made_other, "backward_other"
+    )
+    norm_partner = swap(norm_other, 1)
+    norm_own, dgate_own, dup_own, gain_own = backward(bwd_own, cot_own, made_own, "backward_own")
+    (out_high,) = after((out_high,), norm_own)
+    out_far = home(out_own, out_partner, out_high, middle)
+    norm_high = swap(crossing(norm_own, norm_partner, middle, middle), 2)
+    norm_low = swap(crossing(norm_own, norm_partner, 0, middle), 2)
+    (dgate_own,) = after((dgate_own,), out_high, norm_partner)
     grad_gate, grad_up, grad_down = weight_grads(
         (bwd_own, bwd_other),
         (cot_own, cot_other),
@@ -510,6 +512,27 @@
         (dgate_own, dgate_other),
         (dup_own, dup_other),
     )
+    held_high, out_low = after((norm_high, out_low), grad_gate)
+    norm_far = home(norm_own, norm_partner, held_high, middle)
+    out_near = home(out_own, out_partner, out_low, 0)
+    out_back = after(out_near + out_far, held_high)
+    mixed = call(
+        functools.partial(mixed_kernel, experts, slots),
+        [((tokens, width), BF16)],
+        (plane, fwd_ids, fwd_g, fwd_input[0], *out_back),
+        "mixed",
+        scalars=1,
+    )[0]
+    low_own, low_partner, held_low = after((norm_own, norm_partner, norm_low), mixed)
+    norm_near = home(low_own, low_partner, held_low, 0)
+    norm_back = norm_near + norm_far
+    gain_sum = gain_own + gain_other
+    gain_sum = gain_sum + swap(gain_sum, 1)
+    (gain_sum,) = after((gain_sum,), norm_partner)
+    gain_crossed = swap(gain_sum, 2)
+    gain_sum, gain_crossed = after((gain_sum, gain_crossed), mixed)
+    gain_sum = gain_sum + gain_crossed
+    gain_sum = sum([swap(gain_sum, d * UNIT_SPLIT_COUNT) for d in away], gain_sum)
     gain_grad = gain_sum / norm_gain
 
     input_grad, gate_grad = call(
@@ -520,13 +543,6 @@
         scratch=[pltpu.VMEM((tokens, width), F32)],
         scalars=1,
     )
-    mixed = call(
-        functools.partial(mixed_kernel, experts, slots),
-        [((tokens, width), BF16)],
-        (plane, fwd_ids, fwd_g, fwd_input[0], *out_back),
-        "mixed",
-        scalars=1,
-    )[0]
     act_next = along_pipe(mixed, 1)
     grad_prev = along_pipe(input_grad, -1)
     return (

time: 231 us -> 213 us (0.922)
  Pallas kernels: 55.9 us -> 34.6 us
  starting transfers between devices: 50 us -> 53.8 us
  other arithmetic: 5.79 us -> 2.28 us
    pallas_call x10 -> x14, Pallas kernels: 39 us -> 23.8 us  [call(): pl.pallas_call(body, out_shape=[jax.ShapeDtypeStruct(shape, dtype) for sh...]
    pallas_call x5, Pallas kernels: 7.05 us -> 2.22 us  [join(): pl.pallas_call(functools.partial(join_kernel, pieces), out_shape=[jax.Sha...]
    ppermute x33, starting transfers between devices: 45.3 us -> 49.1 us  [swap(): lax.ppermute(value, 'expert', [(source, source ^ mask) for source in rang...]
    ppermute x2, waiting for transfers between devices: 7.65 us -> 10.4 us  [along_pipe(): lax.ppermute(value, 'pipe', [(source, source + steps) for source in range...]
    unnamed x68 -> x66, local copies, waits for them, and re-layouts: 6.53 us -> 7.06 us
  transfers between devices with their start and end apart: 35 -> 35, of which waited for: 14 -> 18; matrix products, arithmetic and copies ran while one was open for 3% -> 1% of each run, Pallas kernels for 20% -> 13%
where the time goes in v3:
time: 213 us; the launch traced here: 210 us
  waiting for transfers between devices  111 us (52%)
  starting transfers between devices  53.8 us (25%)
  Pallas kernels  34.6 us (16%)
  local copies, waits for them, and re-layouts  7.06 us (3%)
  other arithmetic  2.28 us (1%)
    ppermute x33, waiting for transfers between devices, swap(): lax.ppermute(value, 'expert', [(source, source ^ mask) for source in rang...  101 us
    ppermute x33, starting transfers between devices, swap(): lax.ppermute(value, 'expert', [(source, source ^ mask) for source in rang...  49.1 us
    pallas_call x14, Pallas kernels, call(): pl.pallas_call(body, out_shape=[jax.ShapeDtypeStruct(shape, dtype) for sh...  23.8 us
    ppermute x2, waiting for transfers between devices, along_pipe(): lax.ppermute(value, 'pipe', [(source, source + steps) for source in range...  10.4 us
    pallas_call x1, Pallas kernels, weight_grads(): pl.pallas_call(weight_kernel, grid=(width // chunk,), out_shape=[jax.Shap...  8.61 us
    unnamed x66, local copies, waits for them, and re-layouts  7.06 us
    ppermute x2, starting transfers between devices, along_pipe(): lax.ppermute(value, 'pipe', [(source, source + steps) for source in range...  4.68 us
  transfers between devices with their start and end apart: 35, of which 18 were waited for; matrix products, arithmetic and copies ran while one was open for 1% of the time, Pallas kernels for 13%

profile of v3, /device:TPU:0, one launch (start us, length us, event | category | flops | bytes accessed | tf_op | source)
XLA Modules:
  0.0 210.2 jit_solution(2885919532987277107)
XLA Ops:
  4.4 1.6 select_bwd.1
  6.8 3.0 %collective-permute-start = (bf16[120,3584]{1,0:T(8,128)(2,1)S(1)}, bf16[120,3584]{1,0:T(8,128)(2,1)S(1)}, u32[]{:S(2)}, u32[]{:S(2)}) collective-permute-start(bf16[120,3584]{1,0:T(8,128)(2,1)S(1)} %near_blocks.1), channel_id=1, source_target_pairs={{0,2},{1,3},{2,0},{3,1},{4,6},{5,7},{6,4},{7,5},{8,10},{9,11},{10,... | collective-permute-start | bytes 2580488 | tf_op jit(solution)/shard_map/ppermute | solution.py:27
  11.3 2.6 %collective-permute-start.2 = (bf16[40,3584]{1,0:T(8,128)(2,1)S(1)}, bf16[40,3584]{1,0:T(8,128)(2,1)S(1)}, u32[]{:S(2)}, u32[]{:S(2)}) collective-permute-start(bf16[40,3584]{1,0:T(8,128)(2,1)S(1)} %get-tuple-element.100), channel_id=1, source_target_pairs={{0,8},{1,9},{2,10},{3,11},{4,12},{5,13},{6,14},{7,15},{8,0},{9,1},... | collective-permute-start | bytes 860168 | tf_op jit(solution)/shard_map/ppermute | solution.py:27
  14.1 9.1 %collective-permute-done.1.refs_0_ = bf16[40,3584]{1,0:T(8,128)(2,1)S(1)} collective-permute-done((bf16[40,3584]{1,0:T(8,128)(2,1)S(1)}, bf16[40,3584]{1,0:T(8,128)(2,1)S(1)}, u32[]{:S(2)}, u32[]{:S(2)}) %collective-permute-start.1) | collective-permute-done | bytes 286752 | tf_op jit(solution)/shard_map/ppermute | solution.py:27
  23.3 11.0 %collective-permute-done.2.refs_1_ = bf16[40,3584]{1,0:T(8,128)(2,1)S(1)} collective-permute-done((bf16[40,3584]{1,0:T(8,128)(2,1)S(1)}, bf16[40,3584]{1,0:T(8,128)(2,1)S(1)}, u32[]{:S(2)}, u32[]{:S(2)}) %collective-permute-start.2) | collective-permute-done | bytes 286752 | tf_op jit(solution)/shard_map/ppermute | solution.py:27
  35.1 5.0 %collective-permute-start.4 = (bf16[40,3584]{1,0:T(8,128)(2,1)S(1)}, bf16[40,3584]{1,0:T(8,128)(2,1)S(1)}, u32[]{:S(2)}, u32[]{:S(2)}) collective-permute-start(bf16[40,3584]{1,0:T(8,128)(2,1)S(1)} %get-tuple-element.106), channel_id=1, source_target_pairs={{0,4},{1,5},{2,6},{3,7},{4,0},{5,1},{6,2},{7,3},{8,12},{9,13},{10,... | collective-permute-start | bytes 860168 | tf_op jit(solution)/shard_map/ppermute | solution.py:27
  42.6 6.9 %collective-permute-done.4.refs_0_ = bf16[40,3584]{1,0:T(8,128)(2,1)S(1)} collective-permute-done((bf16[40,3584]{1,0:T(8,128)(2,1)S(1)}, bf16[40,3584]{1,0:T(8,128)(2,1)S(1)}, u32[]{:S(2)}, u32[]{:S(2)}) %collective-permute-start.4) | collective-permute-done | bytes 286752 | tf_op jit(solution)/shard_map/ppermute | solution.py:27
  49.5 13.5 %collective-permute-done.5.refs_1_ = bf16[40,3584]{1,0:T(8,128)(2,1)S(1)} collective-permute-done((bf16[40,3584]{1,0:T(8,128)(2,1)S(1)}, bf16[40,3584]{1,0:T(8,128)(2,1)S(1)}, u32[]{:S(2)}, u32[]{:S(2)}) %collective-permute-start.5) | collective-permute-done | bytes 286752 | tf_op jit(solution)/shard_map/ppermute | solution.py:27
  63.6 3.7 %collective-permute-start.8 = (bf16[40,3584]{1,0:T(8,128)(2,1)S(1)}, bf16[40,3584]{1,0:T(8,128)(2,1)S(1)}, u32[]{:S(2)}, u32[]{:S(2)}) collective-permute-start(bf16[40,3584]{1,0:T(8,128)(2,1)S(1)} %get-tuple-element.113), channel_id=1, source_target_pairs={{0,4},{1,5},{2,6},{3,7},{4,0},{5,1},{6,2},{7,3},{8,12},{9,13},{10,... | collective-permute-start | bytes 860168 | tf_op jit(solution)/shard_map/ppermute | solution.py:27
  71.3 2.0 forward_own.1.own_ref
  74.8 14.0 %collective-permute-done.9.refs_1_ = bf16[40,3584]{1,0:T(8,128)(2,1)S(1)} collective-permute-done((bf16[40,3584]{1,0:T(8,128)(2,1)S(1)}, bf16[40,3584]{1,0:T(8,128)(2,1)S(1)}, u32[]{:S(2)}, u32[]{:S(2)}) %collective-permute-start.9) | collective-permute-done | bytes 286752 | tf_op jit(solution)/shard_map/ppermute | solution.py:27
  92.7 2.0 forward_other.1
  94.7 1.6 collective-permute-start.13
  97.7 17.6 %collective-permute-done.13.refs_3_ = bf16[120,3584]{1,0:T(8,128)(2,1)S(1)} collective-permute-done((bf16[120,3584]{1,0:T(8,128)(2,1)S(1)}, bf16[120,3584]{1,0:T(8,128)(2,1)S(1)}, u32[]{:S(2)}, u32[]{:S(2)}) %collective-permute-start.13) | collective-permute-done | bytes 860192 | tf_op jit(solution)/shard_map/ppermute | solution.py:27
  120.5 3.1 %backward_other.1 = (bf16[320,3712]{1,0:T(8,128)(2,1)S(1)}, bf16[320,256]{1,0:T(8,128)(2,1)S(1)}, bf16[320,256]{1,0:T(8,128)(2,1)S(1)}, f32[1,3584]{1,0:T(1,128)S(1)}) custom-call(bf16[320,3584]{1,0:T(8,128)(2,1)S(1)} %collective-permute-done.14.rows_ref.other_ref, bf16[320,3584]{1,0:T(8,128)(2,1)S(1)} %collective-permute-done.16.cot_ref.cot_other, ...), custom_call_target="tpu_custom_call" | custom-call | flops 99999997952 | bytes 1048576 | tf_op jit(solution)/shard_map/backward_other/pallas_call | solution.py:273
  123.7 3.1 %backward_own.1 = (bf16[320,3712]{1,0:T(8,128)(2,1)S(1)}, bf16[320,256]{1,0:T(8,128)(2,1)S(1)}, bf16[320,256]{1,0:T(8,128)(2,1)S(1)}, f32[1,3584]{1,0:T(1,128)S(1)}) custom-call(bf16[320,3584]{1,0:T(8,128)(2,1)S(1)} %copy-done.8, bf16[320,3584]{1,0:T(8,128)(2,1)S(1)} %own_cot.1.cot_ref.cot_own, bf16[320,256]{1,0:T(8,128)(2,1)S(1)} %get-tuple-element.127.act_ref.act_own, ...), custom_call_target="tpu_custom_call" | custom-call | flops 99999997952 | bytes 1048576 | tf_op jit(solution)/shard_map/backward_own/pallas_call | solution.py:273
  126.8 7.4 %collective-permute-done.20.crossed_ref = bf16[80,3584]{1,0:T(8,128)(2,1)} collective-permute-done((bf16[80,3584]{1,0:T(8,128)(2,1)}, bf16[80,3584]{1,0:T(8,128)(2,1)}, u32[]{:S(2)}, u32[]{:S(2)}) %collective-permute-start.20) | collective-permute-done | bytes 573472 | tf_op jit(solution)/shard_map/ppermute | solution.py:27
  135.5 5.6 %collective-permute-start.22 = (bf16[40,3584]{1,0:T(8,128)(2,1)S(1)}, bf16[40,3584]{1,0:T(8,128)(2,1)S(1)}, u32[]{:S(2)}, u32[]{:S(2)}) collective-permute-start(bf16[40,3584]{1,0:T(8,128)(2,1)S(1)} %get-tuple-element.150), channel_id=1, source_target_pairs={{0,8},{1,9},{2,10},{3,11},{4,12},{5,13},{6,14},{7,15},{8,0},{9,1},... | collective-permute-start | bytes 860168 | tf_op jit(solution)/shard_map/ppermute | solution.py:27
  141.8 1.6 collective-permute-start.18
  143.4 8.6 %weight_grads.1 = (bf16[3584,256]{1,0:T(8,128)(2,1)}, bf16[3584,256]{1,0:T(8,128)(2,1)}, bf16[256,3584]{1,0:T(8,128)(2,1)}) custom-call(bf16[320,3584]{1,0:T(8,128)(2,1)S(1)} %copy-done.8, bf16[320,3584]{1,0:T(8,128)(2,1)S(1)} %collective-permute-done.14.rows_ref.other_ref, bf16[320,3584]{1,0:T(8,128)(2,1)S(1)} %own_cot.1.cot_ref.cot_own, ...), custom_call_target="tpu_custom_call" | custom-call | flops 99999997952 | bytes 1048576 | tf_op jit(solution)/shard_map/weight_grads/pallas_call | solution.py:290
  152.0 6.0 %collective-permute-done.18.crossed_ref = bf16[80,3712]{1,0:T(8,128)(2,1)S(1)} collective-permute-done((bf16[80,3712]{1,0:T(8,128)(2,1)S(1)}, bf16[80,3712]{1,0:T(8,128)(2,1)S(1)}, u32[]{:S(2)}, u32[]{:S(2)}) %collective-permute-start.18) | collective-permute-done | bytes 593952 | tf_op jit(solution)/shard_map/ppermute | solution.py:27
  159.2 3.7 %collective-permute-start.21 = (bf16[40,3584]{1,0:T(8,128)(2,1)S(1)}, bf16[40,3584]{1,0:T(8,128)(2,1)S(1)}, u32[]{:S(2)}, u32[]{:S(2)}) collective-permute-start(bf16[40,3584]{1,0:T(8,128)(2,1)S(1)} %get-tuple-element.149), channel_id=1, source_target_pairs={{0,4},{1,5},{2,6},{3,7},{4,0},{5,1},{6,2},{7,3},{8,12},{9,13},{10,... | collective-permute-start | bytes 860168 | tf_op jit(solution)/shard_map/ppermute | solution.py:27
  164.7 2.0 collective-permute-start.27
  168.2 5.0 %collective-permute-done.21.refs_1_ = bf16[40,3584]{1,0:T(8,128)(2,1)S(1)} collective-permute-done((bf16[40,3584]{1,0:T(8,128)(2,1)S(1)}, bf16[40,3584]{1,0:T(8,128)(2,1)S(1)}, u32[]{:S(2)}, u32[]{:S(2)}) %collective-permute-start.21) | collective-permute-done | bytes 286752 | tf_op jit(solution)/shard_map/ppermute | solution.py:27
  174.1 2.8 %collective-permute-done.25.crossed_ref = bf16[80,3712]{1,0:T(8,128)(2,1)S(1)} collective-permute-done((bf16[80,3712]{1,0:T(8,128)(2,1)S(1)}, bf16[80,3712]{1,0:T(8,128)(2,1)S(1)}, u32[]{:S(2)}, u32[]{:S(2)}) %collective-permute-start.25) | collective-permute-done | bytes 593952 | tf_op jit(solution)/shard_map/ppermute | solution.py:27
  178.9 1.6 collective-permute-start.31
  180.5 2.2 %collective-permute-done.31 = f32[1,3584]{1,0:T(1,128)S(1)} collective-permute-done((f32[1,3584]{1,0:T(1,128)S(1)}, f32[1,3584]{1,0:T(1,128)S(1)}, u32[]{:S(2)}, u32[]{:S(2)}) %collective-permute-start.31) | collective-permute-done | bytes 14368 | tf_op jit(solution)/shard_map/ppermute | solution.py:27
  182.7 3.4 %collective-permute-start.34 = (f32[1,3584]{1,0:T(1,128)S(1)}, f32[1,3584]{1,0:T(1,128)S(1)}, u32[]{:S(2)}, u32[]{:S(2)}) collective-permute-start(f32[1,3584]{1,0:T(1,128)S(1)} %add.37), channel_id=1, source_target_pairs={{0,12},{1,13},{2,14},{3,15},{4,8},{5,9},{6,10},{7,11},{8,4},{9,5},... | collective-permute-start | bytes 43016 | tf_op jit(solution)/shard_map/ppermute | solution.py:27
  186.3 2.1 collective-permute-done.27.refs_2_
  188.4 3.4 %collective-permute-start.24 = (bf16[64,3584]{1,0:T(8,128)(2,1)S(1)}, bf16[64,3584]{1,0:T(8,128)(2,1)S(1)}, u32[]{:S(2)}, u32[]{:S(2)}) collective-permute-start(bf16[64,3584]{1,0:T(8,128)(2,1)S(1)} %mixed.1), channel_id=1, source_target_pairs={{0,16},{1,17},{2,18},{3,19},{4,20},{5,21},{6,22},{7,23},{8,24},{9,... | collective-permute-start | bytes 1376264 | tf_op jit(solution)/shard_map/ppermute | solution.py:33
  192.1 4.2 %input_grad.1 = (bf16[64,3584]{1,0:T(8,128)(2,1)S(1)}, f32[2,64]{1,0:T(2,128)}) custom-call(s32[1]{0:T(128)} %bitcast.plane_ref, s32[2,64]{1,0:T(2,128)S(1)} %bitcast.52, bf16[2,64]{1,0:T(2,128)(2,1)S(1)} %bitcast.55, bf16[64,3584]{1,0:T(8,128)(2,1)S(1)} %bitcast.46, bf16[64,3584]{1,0:T(8,128)(2,1)S(1)} %bitcast.48, f32[1,3584]{1,0:T(1,128)S(1)} %copy-done.6, ...), custom_call_target="tpu_custom_call" | custom-call | flops 99999997952 | bytes 1048576 | tf_op jit(solution)/shard_map/input_grad/pallas_call | solution.py:273
  198.9 9.7 %collective-permute-done.29 = bf16[64,3584]{1,0:T(8,128)(2,1)S(1)} collective-permute-done((bf16[64,3584]{1,0:T(8,128)(2,1)S(1)}, bf16[64,3584]{1,0:T(8,128)(2,1)S(1)}, u32[]{:S(2)}, u32[]{:S(2)}) %collective-permute-start.29) | collective-permute-done | bytes 458784 | tf_op jit(solution)/shard_map/ppermute | solution.py:33
  (130 shorter events, 40.1 us)
Async XLA Ops:
  6.8 27.5 %collective-permute-start = (bf16[120,3584]{1,0:T(8,128)(2,1)S(1)}, bf16[120,3584]{1,0:T(8,128)(2,1)S(1)}, u32[]{:S(2)}, u32[]{:S(2)}) collective-permute-start(bf16[120,3584]{1,0:T(8,128)(2,1)S(1)} %near_blocks.1), channel_id=1, source_target_pairs={{0,2},{1,3},{2,0},{3,1},{4,6},{5,7},{6,4},{7,5},{8,10},{9,11},{10,... | collective-permute-start | bytes 2580488 | tf_op jit(solution)/shard_map/ppermute | solution.py:27
  9.8 13.5 %collective-permute-start.1 = (bf16[40,3584]{1,0:T(8,128)(2,1)S(1)}, bf16[40,3584]{1,0:T(8,128)(2,1)S(1)}, u32[]{:S(2)}, u32[]{:S(2)}) collective-permute-start(bf16[40,3584]{1,0:T(8,128)(2,1)S(1)} %get-tuple-element.99), channel_id=1, source_target_pairs={{0,4},{1,5},{2,6},{3,7},{4,0},{5,1},{6,2},{7,3},{8,12},{9,13},{10,... | collective-permute-start | bytes 860168 | tf_op jit(solution)/shard_map/ppermute | solution.py:27
  11.3 23.0 %collective-permute-start.2 = (bf16[40,3584]{1,0:T(8,128)(2,1)S(1)}, bf16[40,3584]{1,0:T(8,128)(2,1)S(1)}, u32[]{:S(2)}, u32[]{:S(2)}) collective-permute-start(bf16[40,3584]{1,0:T(8,128)(2,1)S(1)} %get-tuple-element.100), channel_id=1, source_target_pairs={{0,8},{1,9},{2,10},{3,11},{4,12},{5,13},{6,14},{7,15},{8,0},{9,1},... | collective-permute-start | bytes 860168 | tf_op jit(solution)/shard_map/ppermute | solution.py:27
  13.9 20.4 %collective-permute-start.3 = (bf16[40,3584]{1,0:T(8,128)(2,1)S(1)}, bf16[40,3584]{1,0:T(8,128)(2,1)S(1)}, u32[]{:S(2)}, u32[]{:S(2)}) collective-permute-start(bf16[40,3584]{1,0:T(8,128)(2,1)S(1)} %get-tuple-element.101), channel_id=1, source_target_pairs={{0,12},{1,13},{2,14},{3,15},{4,8},{5,9},{6,10},{7,11},{8,4},{9,5},... | collective-permute-start | bytes 860168 | tf_op jit(solution)/shard_map/ppermute | solution.py:27
  34.5 28.5 %collective-permute-start.7 = (bf16[120,3584]{1,0:T(8,128)(2,1)S(1)}, bf16[120,3584]{1,0:T(8,128)(2,1)S(1)}, u32[]{:S(2)}, u32[]{:S(2)}) collective-permute-start(bf16[120,3584]{1,0:T(8,128)(2,1)S(1)} %far_fwd.1.refs_4_), channel_id=1, source_target_pairs={{0,2},{1,3},{2,0},{3,1},{4,6},{5,7},{6,4},{7,5},{8,10},{9,11},{10,... | collective-permute-start | bytes 2580488 | tf_op jit(solution)/shard_map/ppermute | solution.py:27
  35.1 14.4 %collective-permute-start.4 = (bf16[40,3584]{1,0:T(8,128)(2,1)S(1)}, bf16[40,3584]{1,0:T(8,128)(2,1)S(1)}, u32[]{:S(2)}, u32[]{:S(2)}) collective-permute-start(bf16[40,3584]{1,0:T(8,128)(2,1)S(1)} %get-tuple-element.106), channel_id=1, source_target_pairs={{0,4},{1,5},{2,6},{3,7},{4,0},{5,1},{6,2},{7,3},{8,12},{9,13},{10,... | collective-permute-start | bytes 860168 | tf_op jit(solution)/shard_map/ppermute | solution.py:27
  40.1 22.9 %collective-permute-start.5 = (bf16[40,3584]{1,0:T(8,128)(2,1)S(1)}, bf16[40,3584]{1,0:T(8,128)(2,1)S(1)}, u32[]{:S(2)}, u32[]{:S(2)}) collective-permute-start(bf16[40,3584]{1,0:T(8,128)(2,1)S(1)} %get-tuple-element.107), channel_id=1, source_target_pairs={{0,8},{1,9},{2,10},{3,11},{4,12},{5,13},{6,14},{7,15},{8,0},{9,1},... | collective-permute-start | bytes 860168 | tf_op jit(solution)/shard_map/ppermute | solution.py:27
  41.1 21.9 %collective-permute-start.6 = (bf16[40,3584]{1,0:T(8,128)(2,1)S(1)}, bf16[40,3584]{1,0:T(8,128)(2,1)S(1)}, u32[]{:S(2)}, u32[]{:S(2)}) collective-permute-start(bf16[40,3584]{1,0:T(8,128)(2,1)S(1)} %get-tuple-element.108), channel_id=1, source_target_pairs={{0,12},{1,13},{2,14},{3,15},{4,8},{5,9},{6,10},{7,11},{8,4},{9,5},... | collective-permute-start | bytes 860168 | tf_op jit(solution)/shard_map/ppermute | solution.py:27
  63.6 11.2 %collective-permute-start.8 = (bf16[40,3584]{1,0:T(8,128)(2,1)S(1)}, bf16[40,3584]{1,0:T(8,128)(2,1)S(1)}, u32[]{:S(2)}, u32[]{:S(2)}) collective-permute-start(bf16[40,3584]{1,0:T(8,128)(2,1)S(1)} %get-tuple-element.113), channel_id=1, source_target_pairs={{0,4},{1,5},{2,6},{3,7},{4,0},{5,1},{6,2},{7,3},{8,12},{9,13},{10,... | collective-permute-start | bytes 860168 | tf_op jit(solution)/shard_map/ppermute | solution.py:27
  67.3 21.5 %collective-permute-start.9 = (bf16[40,3584]{1,0:T(8,128)(2,1)S(1)}, bf16[40,3584]{1,0:T(8,128)(2,1)S(1)}, u32[]{:S(2)}, u32[]{:S(2)}) collective-permute-start(bf16[40,3584]{1,0:T(8,128)(2,1)S(1)} %get-tuple-element.114), channel_id=1, source_target_pairs={{0,8},{1,9},{2,10},{3,11},{4,12},{5,13},{6,14},{7,15},{8,0},{9,1},... | collective-permute-start | bytes 860168 | tf_op jit(solution)/shard_map/ppermute | solution.py:27
  68.4 20.4 %collective-permute-start.10 = (bf16[40,3584]{1,0:T(8,128)(2,1)S(1)}, bf16[40,3584]{1,0:T(8,128)(2,1)S(1)}, u32[]{:S(2)}, u32[]{:S(2)}) collective-permute-start(bf16[40,3584]{1,0:T(8,128)(2,1)S(1)} %get-tuple-element.115), channel_id=1, source_target_pairs={{0,12},{1,13},{2,14},{3,15},{4,8},{5,9},{6,10},{7,11},{8,4},{9,5},... | collective-permute-start | bytes 860168 | tf_op jit(solution)/shard_map/ppermute | solution.py:27
  69.8 19.0 %collective-permute-start.11 = (bf16[120,3584]{1,0:T(8,128)(2,1)S(1)}, bf16[120,3584]{1,0:T(8,128)(2,1)S(1)}, u32[]{:S(2)}, u32[]{:S(2)}) collective-permute-start(bf16[120,3584]{1,0:T(8,128)(2,1)S(1)} %get-tuple-element.116.refs_4_), channel_id=1, source_target_pairs={{0,2},{1,3},{2,0},{3,1},{4,6},{5,7},{6,4},{7,5},{8,10},{9,11},{10,... | collective-permute-start | bytes 2580488 | tf_op jit(solution)/shard_map/ppermute | solution.py:27
  71.3 17.5 %collective-permute-start.12 = (bf16[320,3584]{1,0:T(8,128)(2,1)S(1)}, bf16[320,3584]{1,0:T(8,128)(2,1)S(1)}, u32[]{:S(2)}, u32[]{:S(2)}) collective-permute-start(bf16[320,3584]{1,0:T(8,128)(2,1)S(1)} %get-tuple-element.112.rows_ref), channel_id=1, source_target_pairs={{0,1},{1,0},{2,3},{3,2},{4,5},{5,4},{6,7},{7,6},{8,9},{9,8},{10,11... | collective-permute-start | bytes 6881288 | tf_op jit(solution)/shard_map/ppermute | solution.py:27
  91.6 4.7 %collective-permute-start.14 = (bf16[320,3584]{1,0:T(8,128)(2,1)S(1)}, bf16[320,3584]{1,0:T(8,128)(2,1)S(1)}, u32[]{:S(2)}, u32[]{:S(2)}) collective-permute-start(bf16[320,3584]{1,0:T(8,128)(2,1)S(1)} %get-tuple-element.125.rows_ref.own_ref), channel_id=1, source_target_pairs={{0,1},{1,0},{2,3},{3,2},{4,5},{5,4},{6,7},{7,6},{8,9},{9,8},{10,11... | collective-permute-start | bytes 6881288 | tf_op jit(solution)/shard_map/ppermute | solution.py:27
  94.7 20.6 %collective-permute-start.13 = (bf16[120,3584]{1,0:T(8,128)(2,1)S(1)}, bf16[120,3584]{1,0:T(8,128)(2,1)S(1)}, u32[]{:S(2)}, u32[]{:S(2)}) collective-permute-start(bf16[120,3584]{1,0:T(8,128)(2,1)S(1)} %get-tuple-element.124.refs_1_), channel_id=1, source_target_pairs={{0,2},{1,3},{2,0},{3,1},{4,6},{5,7},{6,4},{7,5},{8,10},{9,11},{10,... | collective-permute-start | bytes 2580488 | tf_op jit(solution)/shard_map/ppermute | solution.py:27
  96.3 19.0 %collective-permute-start.15 = (bf16[320,3584]{1,0:T(8,128)(2,1)S(1)}, bf16[320,3584]{1,0:T(8,128)(2,1)S(1)}, u32[]{:S(2)}, u32[]{:S(2)}) collective-permute-start(bf16[320,3584]{1,0:T(8,128)(2,1)S(1)} %forward_other.1), channel_id=1, source_target_pairs={{0,1},{1,0},{2,3},{3,2},{4,5},{5,4},{6,7},{7,6},{8,9},{9,8},{10,11... | collective-permute-start | bytes 6881288 | tf_op jit(solution)/shard_map/ppermute | solution.py:27
  118.0 16.2 %collective-permute-start.20 = (bf16[80,3584]{1,0:T(8,128)(2,1)}, bf16[80,3584]{1,0:T(8,128)(2,1)}, u32[]{:S(2)}, u32[]{:S(2)}) collective-permute-start(bf16[80,3584]{1,0:T(8,128)(2,1)} %get-tuple-element.175), channel_id=1, source_target_pairs={{0,2},{1,3},{2,0},{3,1},{4,6},{5,7},{6,4},{7,5},{8,10},{9,11},{10,... | collective-permute-start | bytes 1720328 | tf_op jit(solution)/shard_map/ppermute | solution.py:27
  119.5 32.5 %collective-permute-start.19 = (bf16[80,3584]{1,0:T(8,128)(2,1)}, bf16[80,3584]{1,0:T(8,128)(2,1)}, u32[]{:S(2)}, u32[]{:S(2)}) collective-permute-start(bf16[80,3584]{1,0:T(8,128)(2,1)} %get-tuple-element.176), channel_id=1, source_target_pairs={{0,2},{1,3},{2,0},{3,1},{4,6},{5,7},{6,4},{7,5},{8,10},{9,11},{10,... | collective-permute-start | bytes 1720328 | tf_op jit(solution)/shard_map/ppermute | solution.py:27
  123.5 18.0 %collective-permute-start.17 = (bf16[320,3712]{1,0:T(8,128)(2,1)S(1)}, bf16[320,3712]{1,0:T(8,128)(2,1)S(1)}, u32[]{:S(2)}, u32[]{:S(2)}) collective-permute-start(bf16[320,3712]{1,0:T(8,128)(2,1)S(1)} %get-tuple-element.139), channel_id=1, source_target_pairs={{0,1},{1,0},{2,3},{3,2},{4,5},{5,4},{6,7},{7,6},{8,9},{9,8},{10,11... | collective-permute-start | bytes 7127048 | tf_op jit(solution)/shard_map/ppermute | solution.py:27
  135.5 31.2 %collective-permute-start.22 = (bf16[40,3584]{1,0:T(8,128)(2,1)S(1)}, bf16[40,3584]{1,0:T(8,128)(2,1)S(1)}, u32[]{:S(2)}, u32[]{:S(2)}) collective-permute-start(bf16[40,3584]{1,0:T(8,128)(2,1)S(1)} %get-tuple-element.150), channel_id=1, source_target_pairs={{0,8},{1,9},{2,10},{3,11},{4,12},{5,13},{6,14},{7,15},{8,0},{9,1},... | collective-permute-start | bytes 860168 | tf_op jit(solution)/shard_map/ppermute | solution.py:27
  141.0 27.1 %collective-permute-start.23 = (bf16[40,3584]{1,0:T(8,128)(2,1)S(1)}, bf16[40,3584]{1,0:T(8,128)(2,1)S(1)}, u32[]{:S(2)}, u32[]{:S(2)}) collective-permute-start(bf16[40,3584]{1,0:T(8,128)(2,1)S(1)} %get-tuple-element.151), channel_id=1, source_target_pairs={{0,12},{1,13},{2,14},{3,15},{4,8},{5,9},{6,10},{7,11},{8,4},{9,5},... | collective-permute-start | bytes 860168 | tf_op jit(solution)/shard_map/ppermute | solution.py:27
  141.8 16.2 %collective-permute-start.18 = (bf16[80,3712]{1,0:T(8,128)(2,1)S(1)}, bf16[80,3712]{1,0:T(8,128)(2,1)S(1)}, u32[]{:S(2)}, u32[]{:S(2)}) collective-permute-start(bf16[80,3712]{1,0:T(8,128)(2,1)S(1)} %get-tuple-element.174), channel_id=1, source_target_pairs={{0,2},{1,3},{2,0},{3,1},{4,6},{5,7},{6,4},{7,5},{8,10},{9,11},{10,... | collective-permute-start | bytes 1781768 | tf_op jit(solution)/shard_map/ppermute | solution.py:27
  159.2 14.0 %collective-permute-start.21 = (bf16[40,3584]{1,0:T(8,128)(2,1)S(1)}, bf16[40,3584]{1,0:T(8,128)(2,1)S(1)}, u32[]{:S(2)}, u32[]{:S(2)}) collective-permute-start(bf16[40,3584]{1,0:T(8,128)(2,1)S(1)} %get-tuple-element.149), channel_id=1, source_target_pairs={{0,4},{1,5},{2,6},{3,7},{4,0},{5,1},{6,2},{7,3},{8,12},{9,13},{10,... | collective-permute-start | bytes 860168 | tf_op jit(solution)/shard_map/ppermute | solution.py:27
  162.9 14.0 %collective-permute-start.25 = (bf16[80,3712]{1,0:T(8,128)(2,1)S(1)}, bf16[80,3712]{1,0:T(8,128)(2,1)S(1)}, u32[]{:S(2)}, u32[]{:S(2)}) collective-permute-start(bf16[80,3712]{1,0:T(8,128)(2,1)S(1)} %get-tuple-element.173), channel_id=1, source_target_pairs={{0,2},{1,3},{2,0},{3,1},{4,6},{5,7},{6,4},{7,5},{8,10},{9,11},{10,... | collective-permute-start | bytes 1781768 | tf_op jit(solution)/shard_map/ppermute | solution.py:27
  164.7 23.7 %collective-permute-start.27 = (bf16[40,3712]{1,0:T(8,128)(2,1)S(1)}, bf16[40,3712]{1,0:T(8,128)(2,1)S(1)}, u32[]{:S(2)}, u32[]{:S(2)}) collective-permute-start(bf16[40,3712]{1,0:T(8,128)(2,1)S(1)} %get-tuple-element.162), channel_id=1, source_target_pairs={{0,8},{1,9},{2,10},{3,11},{4,12},{5,13},{6,14},{7,15},{8,0},{9,1},... | collective-permute-start | bytes 890888 | tf_op jit(solution)/shard_map/ppermute | solution.py:27
  166.7 21.7 %collective-permute-start.28 = (bf16[40,3712]{1,0:T(8,128)(2,1)S(1)}, bf16[40,3712]{1,0:T(8,128)(2,1)S(1)}, u32[]{:S(2)}, u32[]{:S(2)}) collective-permute-start(bf16[40,3712]{1,0:T(8,128)(2,1)S(1)} %get-tuple-element.163), channel_id=1, source_target_pairs={{0,12},{1,13},{2,14},{3,15},{4,8},{5,9},{6,10},{7,11},{8,4},{9,5},... | collective-permute-start | bytes 890888 | tf_op jit(solution)/shard_map/ppermute | solution.py:27
  177.2 14.9 %collective-permute-start.26 = (bf16[40,3712]{1,0:T(8,128)(2,1)S(1)}, bf16[40,3712]{1,0:T(8,128)(2,1)S(1)}, u32[]{:S(2)}, u32[]{:S(2)}) collective-permute-start(bf16[40,3712]{1,0:T(8,128)(2,1)S(1)} %get-tuple-element.161), channel_id=1, source_target_pairs={{0,4},{1,5},{2,6},{3,7},{4,0},{5,1},{6,2},{7,3},{8,12},{9,13},{10,... | collective-permute-start | bytes 890888 | tf_op jit(solution)/shard_map/ppermute | solution.py:27
  182.7 14.9 %collective-permute-start.34 = (f32[1,3584]{1,0:T(1,128)S(1)}, f32[1,3584]{1,0:T(1,128)S(1)}, u32[]{:S(2)}, u32[]{:S(2)}) collective-permute-start(f32[1,3584]{1,0:T(1,128)S(1)} %add.37), channel_id=1, source_target_pairs={{0,12},{1,13},{2,14},{3,15},{4,8},{5,9},{6,10},{7,11},{8,4},{9,5},... | collective-permute-start | bytes 43016 | tf_op jit(solution)/shard_map/ppermute | solution.py:27
  186.1 11.5 %collective-permute-start.33 = (f32[1,3584]{1,0:T(1,128)S(1)}, f32[1,3584]{1,0:T(1,128)S(1)}, u32[]{:S(2)}, u32[]{:S(2)}) collective-permute-start(f32[1,3584]{1,0:T(1,128)S(1)} %add.37), channel_id=1, source_target_pairs={{0,8},{1,9},{2,10},{3,11},{4,12},{5,13},{6,14},{7,15},{8,0},{9,1},... | collective-permute-start | bytes 43016 | tf_op jit(solution)/shard_map/ppermute | solution.py:27
  188.4 9.2 %collective-permute-start.32 = (f32[1,3584]{1,0:T(1,128)S(1)}, f32[1,3584]{1,0:T(1,128)S(1)}, u32[]{:S(2)}, u32[]{:S(2)}) collective-permute-start(f32[1,3584]{1,0:T(1,128)S(1)} %add.37), channel_id=1, source_target_pairs={{0,4},{1,5},{2,6},{3,7},{4,0},{5,1},{6,2},{7,3},{8,12},{9,13},{10,... | collective-permute-start | bytes 43016 | tf_op jit(solution)/shard_map/ppermute | solution.py:27
  188.4 10.5 %collective-permute-start.24 = (bf16[64,3584]{1,0:T(8,128)(2,1)S(1)}, bf16[64,3584]{1,0:T(8,128)(2,1)S(1)}, u32[]{:S(2)}, u32[]{:S(2)}) collective-permute-start(bf16[64,3584]{1,0:T(8,128)(2,1)S(1)} %mixed.1), channel_id=1, source_target_pairs={{0,16},{1,17},{2,18},{3,19},{4,20},{5,21},{6,22},{7,23},{8,24},{9,... | collective-permute-start | bytes 1376264 | tf_op jit(solution)/shard_map/ppermute | solution.py:33
  196.3 12.3 %collective-permute-start.29 = (bf16[64,3584]{1,0:T(8,128)(2,1)S(1)}, bf16[64,3584]{1,0:T(8,128)(2,1)S(1)}, u32[]{:S(2)}, u32[]{:S(2)}) collective-permute-start(bf16[64,3584]{1,0:T(8,128)(2,1)S(1)} %get-tuple-element.164), channel_id=1, source_target_pairs={{16,0},{17,1},{18,2},{19,3},{20,4},{21,5},{22,6},{23,7},{24,8},{25... | collective-permute-start | bytes 1376264 | tf_op jit(solution)/shard_map/ppermute | solution.py:33
  (35 other events, 367.4 us)

commit v4 on v3

--- a/solution.py
+++ b/solution.py
@@ -72,7 +72,7 @@
         part = values_ref[:, pl.ds(pl.multiple_of(i * chunk, chunk), chunk)].astype(F32)
         return total + jnp.sum(part * part, axis=1, keepdims=True)
 
-    total = lax.fori_loop(0, width // chunk, add, jnp.zeros((tokens, 1), F32))
+    total = lax.fori_loop(0, width // chunk, add, jnp.zeros((tokens, 1), F32), unroll=True)
     return lax.rsqrt(total * (1.0 / width) + EPSILON)
 
 
@@ -252,7 +252,7 @@
         normed = values_ref[:, cols].astype(F32) * inverse
         return carry + jnp.sum(grads * normed, axis=1, keepdims=True)
 
-    mean = lax.fori_loop(0, width // chunk, first, jnp.zeros((tokens, 1), F32)) * (1.0 / width)
+    mean = lax.fori_loop(0, width // chunk, first, jnp.zeros((tokens, 1), F32), unroll=True) * (1.0 / width)
 
     def second(i, carry):
         cols = pl.ds(pl.multiple_of(i * chunk, chunk), chunk)
@@ -262,7 +262,7 @@
         ).astype(BF16)
         return carry
 
-    lax.fori_loop(0, width // chunk, second, 0)
+    lax.fori_loop(0, width // chunk, second, 0, unroll=True)
 
 
 SMEM_SPEC = pl.BlockSpec(memory_space=pltpu.SMEM)

time: 213 us -> 209 us (0.981)
  Pallas kernels: 34.6 us -> 30.1 us
    pallas_call x14, Pallas kernels: 23.8 us -> 19.5 us  [call(): pl.pallas_call(body, out_shape=[jax.ShapeDtypeStruct(shape, dtype) for sh...]
  transfers between devices with their start and end apart: 35 -> 35, of which waited for: 18 -> 17; matrix products, arithmetic and copies ran while one was open for 1% -> 1% of each run, Pallas kernels for 13% -> 12%
where the time goes in v4:
time: 209 us; the launch traced here: 206 us
  waiting for transfers between devices  111 us (53%)
  starting transfers between devices  53.8 us (26%)
  Pallas kernels  30.1 us (14%)
  local copies, waits for them, and re-layouts  7.76 us (4%)
  other arithmetic  2.28 us (1%)
    ppermute x33, waiting for transfers between devices, swap(): lax.ppermute(value, 'expert', [(source, source ^ mask) for source in rang...  101 us
    ppermute x33, starting transfers between devices, swap(): lax.ppermute(value, 'expert', [(source, source ^ mask) for source in rang...  49 us
    pallas_call x14, Pallas kernels, call(): pl.pallas_call(body, out_shape=[jax.ShapeDtypeStruct(shape, dtype) for sh...  19.5 us
    ppermute x2, waiting for transfers between devices, along_pipe(): lax.ppermute(value, 'pipe', [(source, source + steps) for source in range...  10.1 us
    pallas_call x1, Pallas kernels, weight_grads(): pl.pallas_call(weight_kernel, grid=(width // chunk,), out_shape=[jax.Shap...  8.61 us
    unnamed x66, local copies, waits for them, and re-layouts  7.76 us
    ppermute x2, starting transfers between devices, along_pipe(): lax.ppermute(value, 'pipe', [(source, source + steps) for source in range...  4.71 us
  transfers between devices with their start and end apart: 35, of which 17 were waited for; matrix products, arithmetic and copies ran while one was open for 1% of the time, Pallas kernels for 12%

profile of v4, /device:TPU:0, one launch (start us, length us, event | category | flops | bytes accessed | tf_op | source)
XLA Modules:
  0.0 205.7 jit_solution(12236297253744132084)
XLA Ops:
  6.0 3.0 %collective-permute-start = (bf16[120,3584]{1,0:T(8,128)(2,1)S(1)}, bf16[120,3584]{1,0:T(8,128)(2,1)S(1)}, u32[]{:S(2)}, u32[]{:S(2)}) collective-permute-start(bf16[120,3584]{1,0:T(8,128)(2,1)S(1)} %near_blocks.1), channel_id=1, source_target_pairs={{0,2},{1,3},{2,0},{3,1},{4,6},{5,7},{6,4},{7,5},{8,10},{9,11},{10,... | collective-permute-start | bytes 2580488 | tf_op jit(solution)/shard_map/ppermute | solution.py:27
  9.0 1.6 collective-permute-start.1
  10.5 2.6 %collective-permute-start.2 = (bf16[40,3584]{1,0:T(8,128)(2,1)S(1)}, bf16[40,3584]{1,0:T(8,128)(2,1)S(1)}, u32[]{:S(2)}, u32[]{:S(2)}) collective-permute-start(bf16[40,3584]{1,0:T(8,128)(2,1)S(1)} %get-tuple-element.100), channel_id=1, source_target_pairs={{0,8},{1,9},{2,10},{3,11},{4,12},{5,13},{6,14},{7,15},{8,0},{9,1},... | collective-permute-start | bytes 860168 | tf_op jit(solution)/shard_map/ppermute | solution.py:27
  13.4 9.1 %collective-permute-done.1.refs_0_ = bf16[40,3584]{1,0:T(8,128)(2,1)S(1)} collective-permute-done((bf16[40,3584]{1,0:T(8,128)(2,1)S(1)}, bf16[40,3584]{1,0:T(8,128)(2,1)S(1)}, u32[]{:S(2)}, u32[]{:S(2)}) %collective-permute-start.1) | collective-permute-done | bytes 286752 | tf_op jit(solution)/shard_map/ppermute | solution.py:27
  22.5 11.0 %collective-permute-done.2.refs_1_ = bf16[40,3584]{1,0:T(8,128)(2,1)S(1)} collective-permute-done((bf16[40,3584]{1,0:T(8,128)(2,1)S(1)}, bf16[40,3584]{1,0:T(8,128)(2,1)S(1)}, u32[]{:S(2)}, u32[]{:S(2)}) %collective-permute-start.2) | collective-permute-done | bytes 286752 | tf_op jit(solution)/shard_map/ppermute | solution.py:27
  34.3 5.0 %collective-permute-start.4 = (bf16[40,3584]{1,0:T(8,128)(2,1)S(1)}, bf16[40,3584]{1,0:T(8,128)(2,1)S(1)}, u32[]{:S(2)}, u32[]{:S(2)}) collective-permute-start(bf16[40,3584]{1,0:T(8,128)(2,1)S(1)} %get-tuple-element.106), channel_id=1, source_target_pairs={{0,4},{1,5},{2,6},{3,7},{4,0},{5,1},{6,2},{7,3},{8,12},{9,13},{10,... | collective-permute-start | bytes 860168 | tf_op jit(solution)/shard_map/ppermute | solution.py:27
  41.8 6.9 %collective-permute-done.4.refs_0_ = bf16[40,3584]{1,0:T(8,128)(2,1)S(1)} collective-permute-done((bf16[40,3584]{1,0:T(8,128)(2,1)S(1)}, bf16[40,3584]{1,0:T(8,128)(2,1)S(1)}, u32[]{:S(2)}, u32[]{:S(2)}) %collective-permute-start.4) | collective-permute-done | bytes 286752 | tf_op jit(solution)/shard_map/ppermute | solution.py:27
  48.7 13.5 %collective-permute-done.5.refs_1_ = bf16[40,3584]{1,0:T(8,128)(2,1)S(1)} collective-permute-done((bf16[40,3584]{1,0:T(8,128)(2,1)S(1)}, bf16[40,3584]{1,0:T(8,128)(2,1)S(1)}, u32[]{:S(2)}, u32[]{:S(2)}) %collective-permute-start.5) | collective-permute-done | bytes 286752 | tf_op jit(solution)/shard_map/ppermute | solution.py:27
  62.8 3.7 %collective-permute-start.8 = (bf16[40,3584]{1,0:T(8,128)(2,1)S(1)}, bf16[40,3584]{1,0:T(8,128)(2,1)S(1)}, u32[]{:S(2)}, u32[]{:S(2)}) collective-permute-start(bf16[40,3584]{1,0:T(8,128)(2,1)S(1)} %get-tuple-element.113), channel_id=1, source_target_pairs={{0,4},{1,5},{2,6},{3,7},{4,0},{5,1},{6,2},{7,3},{8,12},{9,13},{10,... | collective-permute-start | bytes 860168 | tf_op jit(solution)/shard_map/ppermute | solution.py:27
  70.5 2.0 forward_own.1.own_ref
  74.0 14.0 %collective-permute-done.9.refs_1_ = bf16[40,3584]{1,0:T(8,128)(2,1)S(1)} collective-permute-done((bf16[40,3584]{1,0:T(8,128)(2,1)S(1)}, bf16[40,3584]{1,0:T(8,128)(2,1)S(1)}, u32[]{:S(2)}, u32[]{:S(2)}) %collective-permute-start.9) | collective-permute-done | bytes 286752 | tf_op jit(solution)/shard_map/ppermute | solution.py:27
  91.9 2.0 forward_other.1
  93.9 1.6 collective-permute-start.13
  96.9 17.6 %collective-permute-done.13.refs_3_ = bf16[120,3584]{1,0:T(8,128)(2,1)S(1)} collective-permute-done((bf16[120,3584]{1,0:T(8,128)(2,1)S(1)}, bf16[120,3584]{1,0:T(8,128)(2,1)S(1)}, u32[]{:S(2)}, u32[]{:S(2)}) %collective-permute-start.13) | collective-permute-done | bytes 860192 | tf_op jit(solution)/shard_map/ppermute | solution.py:27
  119.5 3.1 %backward_other.1 = (bf16[320,3712]{1,0:T(8,128)(2,1)S(1)}, bf16[320,256]{1,0:T(8,128)(2,1)S(1)}, bf16[320,256]{1,0:T(8,128)(2,1)S(1)}, f32[1,3584]{1,0:T(1,128)S(1)}) custom-call(bf16[320,3584]{1,0:T(8,128)(2,1)S(1)} %collective-permute-done.14.rows_ref.other_ref, bf16[320,3584]{1,0:T(8,128)(2,1)S(1)} %collective-permute-done.16.cot_ref.cot_other, ...), custom_call_target="tpu_custom_call" | custom-call | flops 99999997952 | bytes 1048576 | tf_op jit(solution)/shard_map/backward_other/pallas_call | solution.py:273
  122.8 3.1 %backward_own.1 = (bf16[320,3712]{1,0:T(8,128)(2,1)S(1)}, bf16[320,256]{1,0:T(8,128)(2,1)S(1)}, bf16[320,256]{1,0:T(8,128)(2,1)S(1)}, f32[1,3584]{1,0:T(1,128)S(1)}) custom-call(bf16[320,3584]{1,0:T(8,128)(2,1)S(1)} %copy-done.8, bf16[320,3584]{1,0:T(8,128)(2,1)S(1)} %own_cot.1.cot_ref.cot_own, bf16[320,256]{1,0:T(8,128)(2,1)S(1)} %get-tuple-element.127.act_ref.act_own, ...), custom_call_target="tpu_custom_call" | custom-call | flops 99999997952 | bytes 1048576 | tf_op jit(solution)/shard_map/backward_own/pallas_call | solution.py:273
  125.9 7.6 %collective-permute-done.20.crossed_ref = bf16[80,3584]{1,0:T(8,128)(2,1)} collective-permute-done((bf16[80,3584]{1,0:T(8,128)(2,1)}, bf16[80,3584]{1,0:T(8,128)(2,1)}, u32[]{:S(2)}, u32[]{:S(2)}) %collective-permute-start.20) | collective-permute-done | bytes 573472 | tf_op jit(solution)/shard_map/ppermute | solution.py:27
  134.7 5.5 %collective-permute-start.22 = (bf16[40,3584]{1,0:T(8,128)(2,1)S(1)}, bf16[40,3584]{1,0:T(8,128)(2,1)S(1)}, u32[]{:S(2)}, u32[]{:S(2)}) collective-permute-start(bf16[40,3584]{1,0:T(8,128)(2,1)S(1)} %get-tuple-element.150), channel_id=1, source_target_pairs={{0,8},{1,9},{2,10},{3,11},{4,12},{5,13},{6,14},{7,15},{8,0},{9,1},... | collective-permute-start | bytes 860168 | tf_op jit(solution)/shard_map/ppermute | solution.py:27
  141.0 1.6 collective-permute-start.18
  142.6 8.6 %weight_grads.1 = (bf16[3584,256]{1,0:T(8,128)(2,1)}, bf16[3584,256]{1,0:T(8,128)(2,1)}, bf16[256,3584]{1,0:T(8,128)(2,1)}) custom-call(bf16[320,3584]{1,0:T(8,128)(2,1)S(1)} %copy-done.8, bf16[320,3584]{1,0:T(8,128)(2,1)S(1)} %collective-permute-done.14.rows_ref.other_ref, bf16[320,3584]{1,0:T(8,128)(2,1)S(1)} %own_cot.1.cot_ref.cot_own, ...), custom_call_target="tpu_custom_call" | custom-call | flops 99999997952 | bytes 1048576 | tf_op jit(solution)/shard_map/weight_grads/pallas_call | solution.py:290
  151.2 5.8 %collective-permute-done.18.crossed_ref = bf16[80,3712]{1,0:T(8,128)(2,1)S(1)} collective-permute-done((bf16[80,3712]{1,0:T(8,128)(2,1)S(1)}, bf16[80,3712]{1,0:T(8,128)(2,1)S(1)}, u32[]{:S(2)}, u32[]{:S(2)}) %collective-permute-start.18) | collective-permute-done | bytes 593952 | tf_op jit(solution)/shard_map/ppermute | solution.py:27
  158.3 3.7 %collective-permute-start.21 = (bf16[40,3584]{1,0:T(8,128)(2,1)S(1)}, bf16[40,3584]{1,0:T(8,128)(2,1)S(1)}, u32[]{:S(2)}, u32[]{:S(2)}) collective-permute-start(bf16[40,3584]{1,0:T(8,128)(2,1)S(1)} %get-tuple-element.149), channel_id=1, source_target_pairs={{0,4},{1,5},{2,6},{3,7},{4,0},{5,1},{6,2},{7,3},{8,12},{9,13},{10,... | collective-permute-start | bytes 860168 | tf_op jit(solution)/shard_map/ppermute | solution.py:27
  163.7 2.1 %collective-permute-start.27 = (bf16[40,3712]{1,0:T(8,128)(2,1)S(1)}, bf16[40,3712]{1,0:T(8,128)(2,1)S(1)}, u32[]{:S(2)}, u32[]{:S(2)}) collective-permute-start(bf16[40,3712]{1,0:T(8,128)(2,1)S(1)} %get-tuple-element.162), channel_id=1, source_target_pairs={{0,8},{1,9},{2,10},{3,11},{4,12},{5,13},{6,14},{7,15},{8,0},{9,1},... | collective-permute-start | bytes 890888 | tf_op jit(solution)/shard_map/ppermute | solution.py:27
  167.2 4.6 %collective-permute-done.21.refs_1_ = bf16[40,3584]{1,0:T(8,128)(2,1)S(1)} collective-permute-done((bf16[40,3584]{1,0:T(8,128)(2,1)S(1)}, bf16[40,3584]{1,0:T(8,128)(2,1)S(1)}, u32[]{:S(2)}, u32[]{:S(2)}) %collective-permute-start.21) | collective-permute-done | bytes 286752 | tf_op jit(solution)/shard_map/ppermute | solution.py:27
  172.7 3.1 %collective-permute-done.25.crossed_ref = bf16[80,3712]{1,0:T(8,128)(2,1)S(1)} collective-permute-done((bf16[80,3712]{1,0:T(8,128)(2,1)S(1)}, bf16[80,3712]{1,0:T(8,128)(2,1)S(1)}, u32[]{:S(2)}, u32[]{:S(2)}) %collective-permute-start.25) | collective-permute-done | bytes 593952 | tf_op jit(solution)/shard_map/ppermute | solution.py:27
  177.7 1.6 collective-permute-start.31
  179.3 2.2 %collective-permute-done.31 = f32[1,3584]{1,0:T(1,128)S(1)} collective-permute-done((f32[1,3584]{1,0:T(1,128)S(1)}, f32[1,3584]{1,0:T(1,128)S(1)}, u32[]{:S(2)}, u32[]{:S(2)}) %collective-permute-start.31) | collective-permute-done | bytes 14368 | tf_op jit(solution)/shard_map/ppermute | solution.py:27
  181.5 3.4 %collective-permute-start.34 = (f32[1,3584]{1,0:T(1,128)S(1)}, f32[1,3584]{1,0:T(1,128)S(1)}, u32[]{:S(2)}, u32[]{:S(2)}) collective-permute-start(f32[1,3584]{1,0:T(1,128)S(1)} %add.37), channel_id=1, source_target_pairs={{0,12},{1,13},{2,14},{3,15},{4,8},{5,9},{6,10},{7,11},{8,4},{9,5},... | collective-permute-start | bytes 43016 | tf_op jit(solution)/shard_map/ppermute | solution.py:27
  185.2 2.2 %collective-permute-done.27.refs_2_ = bf16[40,3712]{1,0:T(8,128)(2,1)S(1)} collective-permute-done((bf16[40,3712]{1,0:T(8,128)(2,1)S(1)}, bf16[40,3712]{1,0:T(8,128)(2,1)S(1)}, u32[]{:S(2)}, u32[]{:S(2)}) %collective-permute-start.27) | collective-permute-done | bytes 296992 | tf_op jit(solution)/shard_map/ppermute | solution.py:27
  187.4 3.4 %collective-permute-start.24 = (bf16[64,3584]{1,0:T(8,128)(2,1)S(1)}, bf16[64,3584]{1,0:T(8,128)(2,1)S(1)}, u32[]{:S(2)}, u32[]{:S(2)}) collective-permute-start(bf16[64,3584]{1,0:T(8,128)(2,1)S(1)} %mixed.1), channel_id=1, source_target_pairs={{0,16},{1,17},{2,18},{3,19},{4,20},{5,21},{6,22},{7,23},{8,24},{9,... | collective-permute-start | bytes 1376264 | tf_op jit(solution)/shard_map/ppermute | solution.py:33
  194.1 3.7 %collective-permute-done.24 = bf16[64,3584]{1,0:T(8,128)(2,1)S(1)} collective-permute-done((bf16[64,3584]{1,0:T(8,128)(2,1)S(1)}, bf16[64,3584]{1,0:T(8,128)(2,1)S(1)}, u32[]{:S(2)}, u32[]{:S(2)}) %collective-permute-start.24) | collective-permute-done | bytes 458784 | tf_op jit(solution)/shard_map/ppermute | solution.py:33
  197.7 6.4 %collective-permute-done.29 = bf16[64,3584]{1,0:T(8,128)(2,1)S(1)} collective-permute-done((bf16[64,3584]{1,0:T(8,128)(2,1)S(1)}, bf16[64,3584]{1,0:T(8,128)(2,1)S(1)}, u32[]{:S(2)}, u32[]{:S(2)}) %collective-permute-start.29) | collective-permute-done | bytes 458784 | tf_op jit(solution)/shard_map/ppermute | solution.py:33
  (130 shorter events, 39.4 us)
Async XLA Ops:
  6.0 27.5 %collective-permute-start = (bf16[120,3584]{1,0:T(8,128)(2,1)S(1)}, bf16[120,3584]{1,0:T(8,128)(2,1)S(1)}, u32[]{:S(2)}, u32[]{:S(2)}) collective-permute-start(bf16[120,3584]{1,0:T(8,128)(2,1)S(1)} %near_blocks.1), channel_id=1, source_target_pairs={{0,2},{1,3},{2,0},{3,1},{4,6},{5,7},{6,4},{7,5},{8,10},{9,11},{10,... | collective-permute-start | bytes 2580488 | tf_op jit(solution)/shard_map/ppermute | solution.py:27
  9.0 13.5 %collective-permute-start.1 = (bf16[40,3584]{1,0:T(8,128)(2,1)S(1)}, bf16[40,3584]{1,0:T(8,128)(2,1)S(1)}, u32[]{:S(2)}, u32[]{:S(2)}) collective-permute-start(bf16[40,3584]{1,0:T(8,128)(2,1)S(1)} %get-tuple-element.99), channel_id=1, source_target_pairs={{0,4},{1,5},{2,6},{3,7},{4,0},{5,1},{6,2},{7,3},{8,12},{9,13},{10,... | collective-permute-start | bytes 860168 | tf_op jit(solution)/shard_map/ppermute | solution.py:27
  10.5 23.0 %collective-permute-start.2 = (bf16[40,3584]{1,0:T(8,128)(2,1)S(1)}, bf16[40,3584]{1,0:T(8,128)(2,1)S(1)}, u32[]{:S(2)}, u32[]{:S(2)}) collective-permute-start(bf16[40,3584]{1,0:T(8,128)(2,1)S(1)} %get-tuple-element.100), channel_id=1, source_target_pairs={{0,8},{1,9},{2,10},{3,11},{4,12},{5,13},{6,14},{7,15},{8,0},{9,1},... | collective-permute-start | bytes 860168 | tf_op jit(solution)/shard_map/ppermute | solution.py:27
  13.1 20.4 %collective-permute-start.3 = (bf16[40,3584]{1,0:T(8,128)(2,1)S(1)}, bf16[40,3584]{1,0:T(8,128)(2,1)S(1)}, u32[]{:S(2)}, u32[]{:S(2)}) collective-permute-start(bf16[40,3584]{1,0:T(8,128)(2,1)S(1)} %get-tuple-element.101), channel_id=1, source_target_pairs={{0,12},{1,13},{2,14},{3,15},{4,8},{5,9},{6,10},{7,11},{8,4},{9,5},... | collective-permute-start | bytes 860168 | tf_op jit(solution)/shard_map/ppermute | solution.py:27
  33.7 28.5 %collective-permute-start.7 = (bf16[120,3584]{1,0:T(8,128)(2,1)S(1)}, bf16[120,3584]{1,0:T(8,128)(2,1)S(1)}, u32[]{:S(2)}, u32[]{:S(2)}) collective-permute-start(bf16[120,3584]{1,0:T(8,128)(2,1)S(1)} %far_fwd.1.refs_4_), channel_id=1, source_target_pairs={{0,2},{1,3},{2,0},{3,1},{4,6},{5,7},{6,4},{7,5},{8,10},{9,11},{10,... | collective-permute-start | bytes 2580488 | tf_op jit(solution)/shard_map/ppermute | solution.py:27
  34.3 14.4 %collective-permute-start.4 = (bf16[40,3584]{1,0:T(8,128)(2,1)S(1)}, bf16[40,3584]{1,0:T(8,128)(2,1)S(1)}, u32[]{:S(2)}, u32[]{:S(2)}) collective-permute-start(bf16[40,3584]{1,0:T(8,128)(2,1)S(1)} %get-tuple-element.106), channel_id=1, source_target_pairs={{0,4},{1,5},{2,6},{3,7},{4,0},{5,1},{6,2},{7,3},{8,12},{9,13},{10,... | collective-permute-start | bytes 860168 | tf_op jit(solution)/shard_map/ppermute | solution.py:27
  39.3 22.9 %collective-permute-start.5 = (bf16[40,3584]{1,0:T(8,128)(2,1)S(1)}, bf16[40,3584]{1,0:T(8,128)(2,1)S(1)}, u32[]{:S(2)}, u32[]{:S(2)}) collective-permute-start(bf16[40,3584]{1,0:T(8,128)(2,1)S(1)} %get-tuple-element.107), channel_id=1, source_target_pairs={{0,8},{1,9},{2,10},{3,11},{4,12},{5,13},{6,14},{7,15},{8,0},{9,1},... | collective-permute-start | bytes 860168 | tf_op jit(solution)/shard_map/ppermute | solution.py:27
  40.3 21.9 %collective-permute-start.6 = (bf16[40,3584]{1,0:T(8,128)(2,1)S(1)}, bf16[40,3584]{1,0:T(8,128)(2,1)S(1)}, u32[]{:S(2)}, u32[]{:S(2)}) collective-permute-start(bf16[40,3584]{1,0:T(8,128)(2,1)S(1)} %get-tuple-element.108), channel_id=1, source_target_pairs={{0,12},{1,13},{2,14},{3,15},{4,8},{5,9},{6,10},{7,11},{8,4},{9,5},... | collective-permute-start | bytes 860168 | tf_op jit(solution)/shard_map/ppermute | solution.py:27
  62.8 11.2 %collective-permute-start.8 = (bf16[40,3584]{1,0:T(8,128)(2,1)S(1)}, bf16[40,3584]{1,0:T(8,128)(2,1)S(1)}, u32[]{:S(2)}, u32[]{:S(2)}) collective-permute-start(bf16[40,3584]{1,0:T(8,128)(2,1)S(1)} %get-tuple-element.113), channel_id=1, source_target_pairs={{0,4},{1,5},{2,6},{3,7},{4,0},{5,1},{6,2},{7,3},{8,12},{9,13},{10,... | collective-permute-start | bytes 860168 | tf_op jit(solution)/shard_map/ppermute | solution.py:27
  66.5 21.5 %collective-permute-start.9 = (bf16[40,3584]{1,0:T(8,128)(2,1)S(1)}, bf16[40,3584]{1,0:T(8,128)(2,1)S(1)}, u32[]{:S(2)}, u32[]{:S(2)}) collective-permute-start(bf16[40,3584]{1,0:T(8,128)(2,1)S(1)} %get-tuple-element.114), channel_id=1, source_target_pairs={{0,8},{1,9},{2,10},{3,11},{4,12},{5,13},{6,14},{7,15},{8,0},{9,1},... | collective-permute-start | bytes 860168 | tf_op jit(solution)/shard_map/ppermute | solution.py:27
  67.6 20.4 %collective-permute-start.10 = (bf16[40,3584]{1,0:T(8,128)(2,1)S(1)}, bf16[40,3584]{1,0:T(8,128)(2,1)S(1)}, u32[]{:S(2)}, u32[]{:S(2)}) collective-permute-start(bf16[40,3584]{1,0:T(8,128)(2,1)S(1)} %get-tuple-element.115), channel_id=1, source_target_pairs={{0,12},{1,13},{2,14},{3,15},{4,8},{5,9},{6,10},{7,11},{8,4},{9,5},... | collective-permute-start | bytes 860168 | tf_op jit(solution)/shard_map/ppermute | solution.py:27
  69.0 19.0 %collective-permute-start.11 = (bf16[120,3584]{1,0:T(8,128)(2,1)S(1)}, bf16[120,3584]{1,0:T(8,128)(2,1)S(1)}, u32[]{:S(2)}, u32[]{:S(2)}) collective-permute-start(bf16[120,3584]{1,0:T(8,128)(2,1)S(1)} %get-tuple-element.116.refs_4_), channel_id=1, source_target_pairs={{0,2},{1,3},{2,0},{3,1},{4,6},{5,7},{6,4},{7,5},{8,10},{9,11},{10,... | collective-permute-start | bytes 2580488 | tf_op jit(solution)/shard_map/ppermute | solution.py:27
  70.5 17.5 %collective-permute-start.12 = (bf16[320,3584]{1,0:T(8,128)(2,1)S(1)}, bf16[320,3584]{1,0:T(8,128)(2,1)S(1)}, u32[]{:S(2)}, u32[]{:S(2)}) collective-permute-start(bf16[320,3584]{1,0:T(8,128)(2,1)S(1)} %get-tuple-element.112.rows_ref), channel_id=1, source_target_pairs={{0,1},{1,0},{2,3},{3,2},{4,5},{5,4},{6,7},{7,6},{8,9},{9,8},{10,11... | collective-permute-start | bytes 6881288 | tf_op jit(solution)/shard_map/ppermute | solution.py:27
  90.8 4.7 %collective-permute-start.14 = (bf16[320,3584]{1,0:T(8,128)(2,1)S(1)}, bf16[320,3584]{1,0:T(8,128)(2,1)S(1)}, u32[]{:S(2)}, u32[]{:S(2)}) collective-permute-start(bf16[320,3584]{1,0:T(8,128)(2,1)S(1)} %get-tuple-element.125.rows_ref.own_ref), channel_id=1, source_target_pairs={{0,1},{1,0},{2,3},{3,2},{4,5},{5,4},{6,7},{7,6},{8,9},{9,8},{10,11... | collective-permute-start | bytes 6881288 | tf_op jit(solution)/shard_map/ppermute | solution.py:27
  93.9 20.6 %collective-permute-start.13 = (bf16[120,3584]{1,0:T(8,128)(2,1)S(1)}, bf16[120,3584]{1,0:T(8,128)(2,1)S(1)}, u32[]{:S(2)}, u32[]{:S(2)}) collective-permute-start(bf16[120,3584]{1,0:T(8,128)(2,1)S(1)} %get-tuple-element.124.refs_1_), channel_id=1, source_target_pairs={{0,2},{1,3},{2,0},{3,1},{4,6},{5,7},{6,4},{7,5},{8,10},{9,11},{10,... | collective-permute-start | bytes 2580488 | tf_op jit(solution)/shard_map/ppermute | solution.py:27
  95.5 19.0 %collective-permute-start.15 = (bf16[320,3584]{1,0:T(8,128)(2,1)S(1)}, bf16[320,3584]{1,0:T(8,128)(2,1)S(1)}, u32[]{:S(2)}, u32[]{:S(2)}) collective-permute-start(bf16[320,3584]{1,0:T(8,128)(2,1)S(1)} %forward_other.1), channel_id=1, source_target_pairs={{0,1},{1,0},{2,3},{3,2},{4,5},{5,4},{6,7},{7,6},{8,9},{9,8},{10,11... | collective-permute-start | bytes 6881288 | tf_op jit(solution)/shard_map/ppermute | solution.py:27
  117.2 16.2 %collective-permute-start.20 = (bf16[80,3584]{1,0:T(8,128)(2,1)}, bf16[80,3584]{1,0:T(8,128)(2,1)}, u32[]{:S(2)}, u32[]{:S(2)}) collective-permute-start(bf16[80,3584]{1,0:T(8,128)(2,1)} %get-tuple-element.175), channel_id=1, source_target_pairs={{0,2},{1,3},{2,0},{3,1},{4,6},{5,7},{6,4},{7,5},{8,10},{9,11},{10,... | collective-permute-start | bytes 1720328 | tf_op jit(solution)/shard_map/ppermute | solution.py:27
  118.7 32.5 %collective-permute-start.19 = (bf16[80,3584]{1,0:T(8,128)(2,1)}, bf16[80,3584]{1,0:T(8,128)(2,1)}, u32[]{:S(2)}, u32[]{:S(2)}) collective-permute-start(bf16[80,3584]{1,0:T(8,128)(2,1)} %get-tuple-element.176), channel_id=1, source_target_pairs={{0,2},{1,3},{2,0},{3,1},{4,6},{5,7},{6,4},{7,5},{8,10},{9,11},{10,... | collective-permute-start | bytes 1720328 | tf_op jit(solution)/shard_map/ppermute | solution.py:27
  122.6 18.2 %collective-permute-start.17 = (bf16[320,3712]{1,0:T(8,128)(2,1)S(1)}, bf16[320,3712]{1,0:T(8,128)(2,1)S(1)}, u32[]{:S(2)}, u32[]{:S(2)}) collective-permute-start(bf16[320,3712]{1,0:T(8,128)(2,1)S(1)} %get-tuple-element.139), channel_id=1, source_target_pairs={{0,1},{1,0},{2,3},{3,2},{4,5},{5,4},{6,7},{7,6},{8,9},{9,8},{10,11... | collective-permute-start | bytes 7127048 | tf_op jit(solution)/shard_map/ppermute | solution.py:27
  134.7 31.0 %collective-permute-start.22 = (bf16[40,3584]{1,0:T(8,128)(2,1)S(1)}, bf16[40,3584]{1,0:T(8,128)(2,1)S(1)}, u32[]{:S(2)}, u32[]{:S(2)}) collective-permute-start(bf16[40,3584]{1,0:T(8,128)(2,1)S(1)} %get-tuple-element.150), channel_id=1, source_target_pairs={{0,8},{1,9},{2,10},{3,11},{4,12},{5,13},{6,14},{7,15},{8,0},{9,1},... | collective-permute-start | bytes 860168 | tf_op jit(solution)/shard_map/ppermute | solution.py:27
  140.3 26.9 %collective-permute-start.23 = (bf16[40,3584]{1,0:T(8,128)(2,1)S(1)}, bf16[40,3584]{1,0:T(8,128)(2,1)S(1)}, u32[]{:S(2)}, u32[]{:S(2)}) collective-permute-start(bf16[40,3584]{1,0:T(8,128)(2,1)S(1)} %get-tuple-element.151), channel_id=1, source_target_pairs={{0,12},{1,13},{2,14},{3,15},{4,8},{5,9},{6,10},{7,11},{8,4},{9,5},... | collective-permute-start | bytes 860168 | tf_op jit(solution)/shard_map/ppermute | solution.py:27
  141.0 15.9 %collective-permute-start.18 = (bf16[80,3712]{1,0:T(8,128)(2,1)S(1)}, bf16[80,3712]{1,0:T(8,128)(2,1)S(1)}, u32[]{:S(2)}, u32[]{:S(2)}) collective-permute-start(bf16[80,3712]{1,0:T(8,128)(2,1)S(1)} %get-tuple-element.174), channel_id=1, source_target_pairs={{0,2},{1,3},{2,0},{3,1},{4,6},{5,7},{6,4},{7,5},{8,10},{9,11},{10,... | collective-permute-start | bytes 1781768 | tf_op jit(solution)/shard_map/ppermute | solution.py:27
  158.3 13.6 %collective-permute-start.21 = (bf16[40,3584]{1,0:T(8,128)(2,1)S(1)}, bf16[40,3584]{1,0:T(8,128)(2,1)S(1)}, u32[]{:S(2)}, u32[]{:S(2)}) collective-permute-start(bf16[40,3584]{1,0:T(8,128)(2,1)S(1)} %get-tuple-element.149), channel_id=1, source_target_pairs={{0,4},{1,5},{2,6},{3,7},{4,0},{5,1},{6,2},{7,3},{8,12},{9,13},{10,... | collective-permute-start | bytes 860168 | tf_op jit(solution)/shard_map/ppermute | solution.py:27
  162.0 13.8 %collective-permute-start.25 = (bf16[80,3712]{1,0:T(8,128)(2,1)S(1)}, bf16[80,3712]{1,0:T(8,128)(2,1)S(1)}, u32[]{:S(2)}, u32[]{:S(2)}) collective-permute-start(bf16[80,3712]{1,0:T(8,128)(2,1)S(1)} %get-tuple-element.173), channel_id=1, source_target_pairs={{0,2},{1,3},{2,0},{3,1},{4,6},{5,7},{6,4},{7,5},{8,10},{9,11},{10,... | collective-permute-start | bytes 1781768 | tf_op jit(solution)/shard_map/ppermute | solution.py:27
  163.7 23.7 %collective-permute-start.27 = (bf16[40,3712]{1,0:T(8,128)(2,1)S(1)}, bf16[40,3712]{1,0:T(8,128)(2,1)S(1)}, u32[]{:S(2)}, u32[]{:S(2)}) collective-permute-start(bf16[40,3712]{1,0:T(8,128)(2,1)S(1)} %get-tuple-element.162), channel_id=1, source_target_pairs={{0,8},{1,9},{2,10},{3,11},{4,12},{5,13},{6,14},{7,15},{8,0},{9,1},... | collective-permute-start | bytes 890888 | tf_op jit(solution)/shard_map/ppermute | solution.py:27
  165.7 21.7 %collective-permute-start.28 = (bf16[40,3712]{1,0:T(8,128)(2,1)S(1)}, bf16[40,3712]{1,0:T(8,128)(2,1)S(1)}, u32[]{:S(2)}, u32[]{:S(2)}) collective-permute-start(bf16[40,3712]{1,0:T(8,128)(2,1)S(1)} %get-tuple-element.163), channel_id=1, source_target_pairs={{0,12},{1,13},{2,14},{3,15},{4,8},{5,9},{6,10},{7,11},{8,4},{9,5},... | collective-permute-start | bytes 890888 | tf_op jit(solution)/shard_map/ppermute | solution.py:27
  176.0 14.9 %collective-permute-start.26 = (bf16[40,3712]{1,0:T(8,128)(2,1)S(1)}, bf16[40,3712]{1,0:T(8,128)(2,1)S(1)}, u32[]{:S(2)}, u32[]{:S(2)}) collective-permute-start(bf16[40,3712]{1,0:T(8,128)(2,1)S(1)} %get-tuple-element.161), channel_id=1, source_target_pairs={{0,4},{1,5},{2,6},{3,7},{4,0},{5,1},{6,2},{7,3},{8,12},{9,13},{10,... | collective-permute-start | bytes 890888 | tf_op jit(solution)/shard_map/ppermute | solution.py:27
  181.5 11.9 %collective-permute-start.34 = (f32[1,3584]{1,0:T(1,128)S(1)}, f32[1,3584]{1,0:T(1,128)S(1)}, u32[]{:S(2)}, u32[]{:S(2)}) collective-permute-start(f32[1,3584]{1,0:T(1,128)S(1)} %add.37), channel_id=1, source_target_pairs={{0,12},{1,13},{2,14},{3,15},{4,8},{5,9},{6,10},{7,11},{8,4},{9,5},... | collective-permute-start | bytes 43016 | tf_op jit(solution)/shard_map/ppermute | solution.py:27
  184.9 8.5 %collective-permute-start.33 = (f32[1,3584]{1,0:T(1,128)S(1)}, f32[1,3584]{1,0:T(1,128)S(1)}, u32[]{:S(2)}, u32[]{:S(2)}) collective-permute-start(f32[1,3584]{1,0:T(1,128)S(1)} %add.37), channel_id=1, source_target_pairs={{0,8},{1,9},{2,10},{3,11},{4,12},{5,13},{6,14},{7,15},{8,0},{9,1},... | collective-permute-start | bytes 43016 | tf_op jit(solution)/shard_map/ppermute | solution.py:27
  187.4 6.0 %collective-permute-start.32 = (f32[1,3584]{1,0:T(1,128)S(1)}, f32[1,3584]{1,0:T(1,128)S(1)}, u32[]{:S(2)}, u32[]{:S(2)}) collective-permute-start(f32[1,3584]{1,0:T(1,128)S(1)} %add.37), channel_id=1, source_target_pairs={{0,4},{1,5},{2,6},{3,7},{4,0},{5,1},{6,2},{7,3},{8,12},{9,13},{10,... | collective-permute-start | bytes 43016 | tf_op jit(solution)/shard_map/ppermute | solution.py:27
  187.4 10.3 %collective-permute-start.24 = (bf16[64,3584]{1,0:T(8,128)(2,1)S(1)}, bf16[64,3584]{1,0:T(8,128)(2,1)S(1)}, u32[]{:S(2)}, u32[]{:S(2)}) collective-permute-start(bf16[64,3584]{1,0:T(8,128)(2,1)S(1)} %mixed.1), channel_id=1, source_target_pairs={{0,16},{1,17},{2,18},{3,19},{4,20},{5,21},{6,22},{7,23},{8,24},{9,... | collective-permute-start | bytes 1376264 | tf_op jit(solution)/shard_map/ppermute | solution.py:33
  192.1 12.1 %collective-permute-start.29 = (bf16[64,3584]{1,0:T(8,128)(2,1)S(1)}, bf16[64,3584]{1,0:T(8,128)(2,1)S(1)}, u32[]{:S(2)}, u32[]{:S(2)}) collective-permute-start(bf16[64,3584]{1,0:T(8,128)(2,1)S(1)} %get-tuple-element.164), channel_id=1, source_target_pairs={{16,0},{17,1},{18,2},{19,3},{20,4},{21,5},{22,6},{23,7},{24,8},{25... | collective-permute-start | bytes 1376264 | tf_op jit(solution)/shard_map/ppermute | solution.py:33
  (35 other events, 366.2 us)
